TPU v7x, 32 devices: a whole 2x2x4 slice. The times are simulated.
32 devices in a mesh: groups: 2 (over x), gx: 16 (over z, y, core).
Axes of the slice: x: 2, y: 2, z: 4, core: 2. Of those that a mesh axis runs over, the one named last changes fastest.
Arguments:
- first_volume: bfloat16 [512, 32, 128], P(('groups', 'gx')), parts along dimension 0, may hold values from -6 to 6
- second_volume: bfloat16 [512, 32, 128], P(('groups', 'gx')), parts along dimension 0, may hold values from -6 to 6
- shift_x: int32 [32, 8], P(('groups', 'gx')), parts along dimension 0, may hold values from -48 to 48
- shift_y: int32 [32, 8], P(('groups', 'gx')), parts along dimension 0, may hold values from -16 to 16
Outputs:
- corrected: float32 [32, 16, 16, 128], P(('groups', 'gx')), parts along dimension 0
There are 2 independent parts, one for each index of `groups`. A program takes and returns all parts, laid end to end along the dimension named above; each array names one. Nothing has to cross between parts.
All inputs are finite; a program needn't handle non-finite values.
Results may differ from a plain program's by a relative error of at most 0.0003.
Values may be sent and summed in bfloat16 or wider, within the bound.
No kernel may reach another device: no remote copies, remote signals or barrier semaphores. Data moves between devices by JAX's collectives and lax.ppermute only.
A program may use at most 64 MiB of HBM per device.

v0:
```python
import math

import jax
import jax.numpy as jnp
import numpy as np
from jax import lax
from jax.experimental import pallas as pl
from jax.experimental.pallas import tpu as pltpu
from jax.sharding import PartitionSpec as P

WIN = 32
STEP = 16
ZS = 32
SR = 16
WY = 8
NY = WY * STEP
LANES = 128
HALF = WIN // 2
BF16 = jnp.bfloat16
F32 = jnp.float32
VMEM_LIMIT = 48 * 2**20

Z_ORDER = np.array([*range(16), 16, *range(31, 16, -1)])


def split_table(table):
    high = np.asarray(table, np.float32).astype(BF16)
    low = (np.asarray(table, np.float64) - high.astype(np.float64)).astype(BF16)
    return high, low


def phase(numbers):
    return 2.0 * math.pi * (np.asarray(numbers) % WIN) / WIN


def y_columns():
    angles = phase(np.outer(np.arange(WIN), np.arange(HALF)))
    real, imag = np.cos(angles), -np.sin(angles)
    imag[:, 0] = 1.0 - 2.0 * (np.arange(WIN) % 2)
    return real, imag


def first_y_table():
    real, imag = y_columns()
    table = np.zeros((NY + STEP, 2, WY, HALF))
    for j in range(WY):
        table[j * STEP : j * STEP + WIN, 0, j] = real
        table[j * STEP : j * STEP + WIN, 1, j] = imag
    high, low = split_table(table[:NY].reshape(NY, 2 * LANES))
    return np.concatenate([high, low], 0)


def second_y_table():
    real, imag = y_columns()
    table = np.zeros((WY, WIN, 2, WY, HALF))
    for j in range(WY):
        table[j, :, 0, j] = real
        table[j, :, 1, j] = imag
    return split_table(table.reshape(2 * LANES, 2 * LANES))


def three_terms(table, axis):
    high, low = split_table(table)
    return np.concatenate([high, high, low], axis)


def z_table():
    angles = phase(np.outer(Z_ORDER, np.arange(ZS)))
    four = np.eye(4)
    cosine, sine = np.kron(four, np.cos(angles)), np.kron(four, np.sin(angles))
    return three_terms(np.block([[cosine, sine], [-sine, cosine]]), 1)


def z_inverse_table():
    angles = phase(np.outer(np.arange(SR) - SR // 2, Z_ORDER))
    four = np.eye(4)
    cosine, sine = np.kron(four, np.cos(angles)), np.kron(four, np.sin(angles))
    return three_terms(np.block([[cosine, -sine], [sine, cosine]]), 1)


def y_inverse_table():
    shifts = np.arange(SR) - SR // 2
    angles = phase(np.outer(np.arange(HALF), shifts))
    real, imag = 2.0 * np.cos(angles), -2.0 * np.sin(angles)
    real[0] = 1.0
    imag[0] = 1.0 - 2.0 * (shifts % 2)
    eight = np.eye(WY)
    table = np.concatenate([np.kron(eight, real), np.kron(eight, imag)], 0)
    return three_terms(table / (WIN * WIN), 0)


def dot(a, b):
    return jnp.dot(a, b, preferred_element_type=F32)


def split(value, axis):
    high = value.astype(BF16)
    low = (value - high.astype(F32)).astype(BF16)
    return jnp.concatenate([high, low, high], axis)


def positions(shape):
    rows = lax.broadcasted_iota(jnp.int32, shape, len(shape) - 2)
    lanes = lax.broadcasted_iota(jnp.int32, shape, len(shape) - 1)
    return rows, lanes % HALF == 0


def z_stage(part_0, part_1, table_ref, real_ref, imag_ref, start):
    columns = [
        jnp.concatenate([part[:, :LANES], part[:, LANES:]], 0) for part in (part_0, part_1)
    ]
    slots = dot(table_ref[...], split(jnp.concatenate(columns, 1), 0))
    rows, zero_lane = positions((4, 8, LANES))
    mixed = [zero_lane & (rows != 0), zero_lane]
    weight = jnp.where(zero_lane & (rows == 0), 1.0, 2.0)
    no_mean = jnp.where(zero_lane & (rows == 0), 0.0, 2.0)
    energy = jnp.zeros((8, LANES), F32)
    for h in range(2):
        lanes = slice(h * LANES, (h + 1) * LANES)
        real = slots[: 4 * ZS, lanes].reshape(4, ZS, LANES)
        imag = slots[4 * ZS :, lanes].reshape(4, ZS, LANES)
        where_x = pl.ds(start + 4 * h, 4)
        for group in range(2):
            up = slice(group * 8, group * 8 + 8)
            down = slice(group * 8 + 16, group * 8 + 24)
            ur, ui, dr, di = real[:, up], imag[:, up], real[:, down], imag[:, down]
            mask = mixed[group]
            new = (
                jnp.where(mask, 0.5 * (ur + dr), ur),
                jnp.where(mask, 0.5 * (ui - di), ui),
                jnp.where(mask, 0.5 * (ui + di), dr),
                jnp.where(mask, 0.5 * (dr - ur), di),
            )
            real_ref[where_x, up] = new[0]
            imag_ref[where_x, up] = new[1]
            real_ref[where_x, down] = new[2]
            imag_ref[where_x, down] = new[3]
            if group == 0:
                parts = no_mean * new[0] * new[0] + weight * (
                    new[1] * new[1] + new[2] * new[2] + new[3] * new[3]
                )
            else:
                parts = 2.0 * sum(v * v for v in new)
            energy = energy + jnp.sum(parts, 0)
    return energy


def finish_stage(energy, real_ref):
    rows, zero_lane = positions((8, LANES))
    is_mean = zero_lane & (rows == 0)
    block = real_ref[:, 0:8]
    means = jnp.where(is_mean, jnp.sum(block, 0) * (1.0 / WIN), 0.0)
    centred = block - means[None]
    real_ref[:, 0:8] = centred
    total = energy + jnp.sum(jnp.where(is_mean[None], centred * centred, 0.0), 0)
    total = jnp.broadcast_to(jnp.sum(total, 0, keepdims=True), (8, LANES))
    group_row = lax.broadcasted_iota(jnp.int32, (LANES, LANES), 0) // HALF
    group_col = lax.broadcasted_iota(jnp.int32, (LANES, LANES), 1) // HALF
    same = (group_row == group_col).astype(F32)
    summed = jnp.dot(total, same, precision=lax.Precision.HIGHEST, preferred_element_type=F32)
    return summed * (1.0 / (ZS * WIN * WIN * ZS * WIN))


def first_kernel(tile_ref, next_ref, y_ref, z_ref, real_ref, imag_ref, var_ref):
    energy = jnp.zeros((8, LANES), F32)
    table = y_ref[...]
    for source, base in ((tile_ref, 0), (next_ref, STEP)):
        for start in range(0, STEP, 8):
            rows = source[start : start + 8].reshape(8 * ZS, NY)
            values = dot(jnp.concatenate([rows, rows], 1), table)
            energy = energy + z_stage(
                values[: 4 * ZS], values[4 * ZS :], z_ref, real_ref, imag_ref, base + start
            )
    var_ref[...] = finish_stage(energy, real_ref)


def second_kernel(
    starts_ref,
    own_ref,
    mate_ref,
    near_ref,
    far_ref,
    mate_near_ref,
    mate_far_ref,
    first_real_ref,
    first_imag_ref,
    first_var_ref,
    y_high_ref,
    y_low_ref,
    z_ref,
    z_inverse_ref,
    y_inverse_ref,
    out_ref,
    region_ref,
    real_ref,
    imag_ref,
    cross_real_ref,
    cross_imag_ref,
    sems,
):
    odd = starts_ref[2, 0]
    two = 2 * STEP
    copies = [
        pltpu.make_async_copy(source, region_ref.at[pl.ds(place, source.shape[0])], sems.at[n])
        for n, (source, place) in enumerate(
            (
                (own_ref, 2 * two + STEP * odd),
                (mate_ref, 2 * two + STEP * (1 - odd)),
                (near_ref, two + 2 * two * (1 - odd)),
                (far_ref, 4 * two * (1 - odd)),
                (mate_near_ref, two + 2 * two * odd),
                (mate_far_ref, 4 * two * odd),
            )
        )
    ]
    for copy in copies:
        copy.start()
    for copy in copies:
        copy.wait()

    lane = lax.broadcasted_iota(jnp.int32, (1, LANES), 1)

    def eight_x(step, energy):
        start = step * 8
        packs = []
        for half in range(2):
            total = None
            for n in range(4):
                j = half * 4 + n
                start_y = starts_ref[1, j]
                block = region_ref[pl.ds(starts_ref[0, j] + start, 8)].reshape(8 * ZS, NY)
                turned = pltpu.roll(block.astype(F32), (n * WIN - start_y) & (LANES - 1), 1)
                y = lane - n * WIN + start_y
                inside = (lane // WIN == n) & (y >= 0) & (y < NY)
                if total is None:
                    total = jnp.where(inside, turned, 0.0)
                else:
                    total = jnp.where(inside, turned, total)
            packs.append(total.astype(BF16))
        windows = jnp.concatenate(packs, 1)
        values = dot(windows, y_high_ref[...]) + dot(windows, y_low_ref[...])
        return energy + z_stage(
            values[: 4 * ZS], values[4 * ZS :], z_ref, real_ref, imag_ref, start
        )

    energy = lax.fori_loop(0, WIN // 8, eight_x, jnp.zeros((8, LANES), F32))
    second_var = finish_stage(energy, real_ref)

    rows, zero_lane = positions((8, LANES))
    special = zero_lane & (rows == 0)

    def eight_slots(block, carry):
        where_z = pl.ds(pl.multiple_of(block * 8, 8), 8)
        alone = special & (block % 2 == 0)
        for base in range(0, SR, 8):
            rr = [None] * 8
            ii = [None] * 8
            ri = [None] * 8
            for x in range(WIN):
                fr = first_real_ref[x, where_z]
                fi = first_imag_ref[x, where_z]
                for s in range(8):
                    at = (x + base + s - SR // 2) % WIN
                    gr = real_ref[at, where_z]
                    gi = imag_ref[at, where_z]
                    if x == 0:
                        rr[s], ii[s], ri[s] = fr * gr, fi * gi, fr * gi - fi * gr
                    else:
                        rr[s] = rr[s] + fr * gr
                        ii[s] = ii[s] + fi * gi
                        ri[s] = ri[s] + fr * gi - fi * gr
            for s in range(8):
                cross_real_ref[base + s, where_z] = jnp.where(alone, rr[s], rr[s] + ii[s])
                cross_imag_ref[base + s, where_z] = jnp.where(alone, ii[s], ri[s])
        return carry

    lax.fori_loop(0, ZS // 8, eight_slots, 0)

    rows, zero_lane = positions((4, 8, LANES))
    mixed = [zero_lane & (rows != 0), zero_lane]
    scale = 1.0 / (
        WIN**1.5 * (jnp.sqrt(first_var_ref[...] + 1e-6) * jnp.sqrt(second_var + 1e-6))
    )
    for start in range(0, SR, 8):
        columns = []
        for quarter in range(start, start + 8, 4):
            where_x = slice(quarter, quarter + 4)
            real = [None] * 4
            imag = [None] * 4
            for group in range(2):
                up = slice(group * 8, group * 8 + 8)
                down = slice(group * 8 + 16, group * 8 + 24)
                ur, ui = cross_real_ref[where_x, up], cross_imag_ref[where_x, up]
                dr, di = cross_real_ref[where_x, down], cross_imag_ref[where_x, down]
                mask = mixed[group]
                real[group] = jnp.where(mask, ur - di, ur)
                imag[group] = jnp.where(mask, ui + dr, ui)
                real[group + 2] = jnp.where(mask, ur + di, dr)
                imag[group + 2] = jnp.where(mask, dr - ui, di)
            columns.append(
                jnp.concatenate(
                    [jnp.concatenate(v, 1).reshape(4 * ZS, LANES) for v in (real, imag)], 0
                )
            )
        slots = dot(z_inverse_ref[...], split(jnp.concatenate(columns, 1), 0))
        for h in range(2):
            lanes = slice(h * LANES, (h + 1) * LANES)
            pair = jnp.concatenate([slots[: 4 * SR, lanes], slots[4 * SR :, lanes]], 1)
            values = dot(split(pair, 1), y_inverse_ref[...])
            where_out = slice((start + 4 * h) * SR, (start + 4 * h + 4) * SR)
            out_ref[where_out] = values * scale[0:1]


def product_kernel(edge_ref, own_ref, mate_ref, other_ref, out_ref):
    own = own_ref[...]
    lane = lax.broadcasted_iota(jnp.int32, own.shape, 1)
    below = jnp.where(lane < SR, 1.0, pltpu.roll(own, SR, 1))
    above = jnp.where(lane >= LANES - SR, 1.0, pltpu.roll(own, LANES - SR, 1))
    other = jnp.where(edge_ref[0] == 1, 1.0, other_ref[...])
    out_ref[...] = own * mate_ref[...] * other * below * above


def params():
    return pltpu.CompilerParams(vmem_limit_bytes=VMEM_LIMIT)


VMEM = pl.BlockSpec(memory_space=pltpu.VMEM)
SMEM = pl.BlockSpec(memory_space=pltpu.SMEM)
ANY = pl.BlockSpec(memory_space=pl.ANY)


def local(first_volume, second_volume, shift_x, shift_y):
    size = lax.axis_size("gx")
    chips = size // 2
    position = lax.axis_index("gx")
    odd = position % 2

    def send(value, pairs):
        return lax.ppermute(value, "gx", pairs)

    mates = [(i, i ^ 1) for i in range(size)]
    near = [(2 * q + 2, 2 * q) for q in range(chips - 1)]
    near += [(2 * q - 1, 2 * q + 1) for q in range(1, chips)]
    far = [(2 * q + 4, 2 * q) for q in range(chips - 2)]
    far += [(2 * q - 3, 2 * q + 1) for q in range(2, chips)]
    after = [(2 * q + 2, 2 * q + 1) for q in range(chips - 1)]
    across = after + [(b, a) for a, b in after]

    mate_tile = send(second_volume, mates)
    low = jnp.where(odd == 0, second_volume, mate_tile)
    high = jnp.where(odd == 0, mate_tile, second_volume)
    pair = jnp.concatenate([low, high], 0)
    far_pair = send(pair, far)
    near_pair = send(pair, near)
    next_tile = send(first_volume, [(i + 1, i) for i in range(size - 1)])
    mate_far = send(far_pair, mates)
    mate_near = send(near_pair, mates)

    spectrum = jax.ShapeDtypeStruct((WIN, ZS, LANES), F32)
    first_real, first_imag, first_var = pl.pallas_call(
        first_kernel,
        out_shape=(spectrum, spectrum, jax.ShapeDtypeStruct((8, LANES), F32)),
        in_specs=[VMEM] * 4,
        out_specs=(VMEM, VMEM, VMEM),
        compiler_params=params(),
        name="first_spectra",
    )(first_volume, next_tile, first_y_table(), z_table())

    starts_x = shift_x[0] + STEP * (4 + odd)
    starts_y = shift_y[0] + jnp.arange(WY, dtype=jnp.int32) * STEP
    starts = jnp.stack([starts_x, starts_y, jnp.full((WY,), odd, jnp.int32)], 0)
    y_high, y_low = second_y_table()
    maps = pl.pallas_call(
        second_kernel,
        out_shape=jax.ShapeDtypeStruct((SR * SR, LANES), F32),
        in_specs=[SMEM] + [ANY] * 6 + [VMEM] * 8,
        out_specs=VMEM,
        scratch_shapes=[
            pltpu.VMEM((10 * STEP, ZS, NY), BF16),
            pltpu.VMEM((WIN, ZS, LANES), F32),
            pltpu.VMEM((WIN, ZS, LANES), F32),
            pltpu.VMEM((SR, ZS, LANES), F32),
            pltpu.VMEM((SR, ZS, LANES), F32),
            pltpu.SemaphoreType.DMA((6,)),
        ],
        compiler_params=params(),
        name="second_maps",
    )(
        starts,
        second_volume,
        mate_tile,
        near_pair,
        far_pair,
        mate_near,
        mate_far,
        first_real,
        first_imag,
        first_var,
        y_high,
        y_low,
        z_table(),
        z_inverse_table(),
        y_inverse_table(),
    )

    other_maps = send(maps, across)
    mate_maps = send(maps, mates)
    edge = ((position == 0) | (position == size - 1)).astype(jnp.int32).reshape(1)
    product = pl.pallas_call(
        product_kernel,
        out_shape=jax.ShapeDtypeStruct((SR * SR, LANES), F32),
        in_specs=[SMEM, VMEM, VMEM, VMEM],
        out_specs=VMEM,
        compiler_params=params(),
        name="product",
    )(edge, maps, mate_maps, other_maps)
    return product.reshape(1, SR, SR, LANES)


def solution(mesh):
    return jax.shard_map(
        local,
        mesh=mesh,
        in_specs=(
            P(("groups", "gx"), None, None),
            P(("groups", "gx"), None, None),
            P(("groups", "gx"), None),
            P(("groups", "gx"), None),
        ),
        out_specs=P(("groups", "gx"), None, None, None),
        check_vma=False,
    )
```

profile of v0, /device:TPU:9, one launch (start us, length us, event | category | flops | bytes accessed | tf_op | source)
XLA Modules:
  0.0 36.3 jit_solution(18200484283127344058)
XLA Ops:
  0.0 0.7 %collective-permute-start = (bf16[16,32,128]{2,1,0:T(8,128)(2,1)}, bf16[16,32,128]{2,1,0:T(8,128)(2,1)S(1)}, u32[]{:S(2)}, u32[]{:S(2)}) collective-permute-start(bf16[16,32,128]{2,1,0:T(8,128)(2,1)} %own_ref.1), channel_id=1, source_target_pairs={{0,1},{1,0},{2,3},{3,2},{4,5},{5,4},{6,7},{7,6},{8,9},{9,8},{10,11... | collective-permute-start | bytes 393224 | tf_op jit(solution)/shard_map/ppermute | solution.py:339
  0.7 1.2 %collective-permute-done.mate_ref = bf16[16,32,128]{2,1,0:T(8,128)(2,1)S(1)} collective-permute-done((bf16[16,32,128]{2,1,0:T(8,128)(2,1)}, bf16[16,32,128]{2,1,0:T(8,128)(2,1)S(1)}, u32[]{:S(2)}, u32[]{:S(2)}) %collective-permute-start) | collective-permute-done | bytes 131104 | tf_op jit(solution)/shard_map/ppermute | solution.py:339
  1.9 1.0 %broadcast_select_fusion.1 = (bf16[16,32,128]{2,1,0:T(8,128)(2,1)S(1)}, bf16[16,32,128]{2,1,0:T(8,128)(2,1)S(1)}) fusion(bf16[16,32,128]{2,1,0:T(8,128)(2,1)} %own_ref.1, bf16[16,32,128]{2,1,0:T(8,128)(2,1)S(1)} %collective-permute-done.mate_ref, pred[]{:T(512)S(6)} %eq.14), kind=kLoop, calls=%fused_computation.2 | loop fusion | flops 131072 | bytes 524289 | tf_op jit(solution)/shard_map/jit(_where)/select_n | solution.py:350
  2.8 0.0 copy-start
  2.9 0.0 copy-start.4
  2.9 3.3 %collective-permute-start.2 = (bf16[32,32,128]{2,1,0:T(8,128)(2,1)S(1)}, bf16[32,32,128]{2,1,0:T(8,128)(2,1)S(1)}, u32[]{:S(2)}, u32[]{:S(2)}) collective-permute-start(bf16[32,32,128]{2,1,0:T(8,128)(2,1)S(1)} %pad_maximum_fusion), channel_id=1, source_target_pairs={{4,0},{6,2},{8,4},{10,6},{12,8},{14,10},{1,5},{3,7},{5,9},{7,11},{... | collective-permute-start | bytes 786440 | tf_op jit(solution)/shard_map/ppermute | solution.py:339
  6.2 3.1 %collective-permute-start.1 = (bf16[32,32,128]{2,1,0:T(8,128)(2,1)S(1)}, bf16[32,32,128]{2,1,0:T(8,128)(2,1)S(1)}, u32[]{:S(2)}, u32[]{:S(2)}) collective-permute-start(bf16[32,32,128]{2,1,0:T(8,128)(2,1)S(1)} %pad_maximum_fusion), channel_id=1, source_target_pairs={{2,0},{4,2},{6,4},{8,6},{10,8},{12,10},{14,12},{1,3},{3,5},{5,7},{... | collective-permute-start | bytes 786440 | tf_op jit(solution)/shard_map/ppermute | solution.py:339
  9.4 0.0 copy-done.4
  9.4 1.9 %collective-permute-start.5 = (bf16[16,32,128]{2,1,0:T(8,128)(2,1)S(1)}, bf16[16,32,128]{2,1,0:T(8,128)(2,1)S(1)}, u32[]{:S(2)}, u32[]{:S(2)}) collective-permute-start(bf16[16,32,128]{2,1,0:T(8,128)(2,1)S(1)} %copy-done.4), channel_id=1, source_target_pairs={{1,0},{2,1},{3,2},{4,3},{5,4},{6,5},{7,6},{8,7},{9,8},{10,9},{11,1... | collective-permute-start | bytes 393224 | tf_op jit(solution)/shard_map/ppermute | solution.py:339
  11.3 0.0 copy-start.8
  11.3 0.0 copy-start.9
  11.4 0.0 collective-permute-done.2.far_ref
  11.4 1.6 %collective-permute-start.4 = (bf16[32,32,128]{2,1,0:T(8,128)(2,1)S(1)}, bf16[32,32,128]{2,1,0:T(8,128)(2,1)S(1)}, u32[]{:S(2)}, u32[]{:S(2)}) collective-permute-start(bf16[32,32,128]{2,1,0:T(8,128)(2,1)S(1)} %collective-permute-done.2.far_ref), channel_id=1, source_target_pairs={{0,1},{1,0},{2,3},{3,2},{4,5},{5,4},{6,7},{7,6},{8,9},{9,8},{10,11... | collective-permute-start | bytes 786440 | tf_op jit(solution)/shard_map/ppermute | solution.py:339
  12.9 4.0 %collective-permute-done.1.near_ref = bf16[32,32,128]{2,1,0:T(8,128)(2,1)S(1)} collective-permute-done((bf16[32,32,128]{2,1,0:T(8,128)(2,1)S(1)}, bf16[32,32,128]{2,1,0:T(8,128)(2,1)S(1)}, u32[]{:S(2)}, u32[]{:S(2)}) %collective-permute-start.1) | collective-permute-done | bytes 262176 | tf_op jit(solution)/shard_map/ppermute | solution.py:339
  16.9 0.0 collective-permute-start.3
  16.9 0.0 copy-done.9
  16.9 0.1 pad.4.clone
  17.0 0.1 add_add_fusion.starts_ref
  17.1 0.0 copy-start.7
  17.1 0.0 collective-permute-done.5.next_ref
  17.1 1.6 %first_spectra.1 = (f32[32,32,128]{2,1,0:T(8,128)S(1)}, f32[32,32,128]{2,1,0:T(8,128)S(1)}, f32[8,128]{1,0:T(8,128)S(1)}) custom-call(bf16[16,32,128]{2,1,0:T(8,128)(2,1)S(1)} %copy-done.4, bf16[16,32,128]{2,1,0:T(8,128)(2,1)S(1)} %collective-permute-done.5.next_ref, bf16[256,256]{1,0:T(8,128)(2,1)S(1)} %copy-done.5, bf16[256,768]{1,0:T(8,128)(2,1)S(1)} %copy-done), custom_call_target="tpu_custom_call" | custom-call | tf_op jit(solution)/shard_map/first_spectra/pallas_call | solution.py:360
  18.7 0.0 collective-permute-done.4.mate_far_ref
  18.7 0.0 collective-permute-done.3.mate_near_ref
  18.7 0.0 copy-done.1
  18.7 0.0 copy-done.2
  18.7 0.0 copy-done.3
  18.8 8.5 %second_maps.1.own_ref = f32[256,128]{1,0:T(8,128)S(1)} custom-call(s32[3,8]{1,0:T(4,128)S(1)} %add_add_fusion.starts_ref, bf16[16,32,128]{2,1,0:T(8,128)(2,1)S(1)} %copy-done.1, bf16[16,32,128]{2,1,0:T(8,128)(2,1)S(1)} %collective-permute-done.mate_ref, bf16[32,32,128]{2,1,0:T(8,128)(2,1)S(1)} %collective-permute-done.1.near_ref, ...), custom_call_target="tpu_custom_call" | custom-call | tf_op jit(solution)/shard_map/second_maps/pallas_call | solution.py:373
  27.2 4.2 %collective-permute-start.7 = (f32[256,128]{1,0:T(8,128)S(1)}, f32[256,128]{1,0:T(8,128)S(1)}, u32[]{:S(2)}, u32[]{:S(2)}) collective-permute-start(f32[256,128]{1,0:T(8,128)S(1)} %second_maps.1.own_ref), channel_id=1, source_target_pairs={{2,1},{4,3},{6,5},{8,7},{10,9},{12,11},{14,13},{1,2},{3,4},{5,6},{... | collective-permute-start | bytes 393224 | tf_op jit(solution)/shard_map/ppermute | solution.py:339
  31.5 0.1 collective-permute-start.6
  31.5 4.0 %collective-permute-done.7.other_ref = f32[256,128]{1,0:T(8,128)S(1)} collective-permute-done((f32[256,128]{1,0:T(8,128)S(1)}, f32[256,128]{1,0:T(8,128)S(1)}, u32[]{:S(2)}, u32[]{:S(2)}) %collective-permute-start.7) | collective-permute-done | bytes 131104 | tf_op jit(solution)/shard_map/ppermute | solution.py:339
  35.5 0.0 collective-permute-done.6.mate_ref
  35.5 0.8 %product.1 = f32[256,128]{1,0:T(8,128)} custom-call(s32[1]{0:T(128)} %bitcast.edge_ref, f32[256,128]{1,0:T(8,128)S(1)} %second_maps.1.own_ref, f32[256,128]{1,0:T(8,128)S(1)} %collective-permute-done.6.mate_ref, f32[256,128]{1,0:T(8,128)S(1)} %collective-permute-done.7.other_ref), custom_call_target="tpu_custom_call" | custom-call | tf_op jit(solution)/shard_map/product/pallas_call | solution.py:409
  (12 shorter events, 0.1 us)
Async XLA Ops:
  0.0 1.9 %collective-permute-start = (bf16[16,32,128]{2,1,0:T(8,128)(2,1)}, bf16[16,32,128]{2,1,0:T(8,128)(2,1)S(1)}, u32[]{:S(2)}, u32[]{:S(2)}) collective-permute-start(bf16[16,32,128]{2,1,0:T(8,128)(2,1)} %own_ref.1), channel_id=1, source_target_pairs={{0,1},{1,0},{2,3},{3,2},{4,5},{5,4},{6,7},{7,6},{8,9},{9,8},{10,11... | collective-permute-start | bytes 393224 | tf_op jit(solution)/shard_map/ppermute | solution.py:339
  1.9 15.2 %copy-start.5 = (bf16[256,256]{1,0:T(8,128)(2,1)S(1)}, bf16[256,256]{1,0:T(8,128)(2,1)}, u32[]{:S(2)}) copy-start(bf16[256,256]{1,0:T(8,128)(2,1)} %constant.37.clone.y_ref) | copy-start | bytes 393220
  2.8 14.3 %copy-start = (bf16[256,768]{1,0:T(8,128)(2,1)S(1)}, bf16[256,768]{1,0:T(8,128)(2,1)}, u32[]{:S(2)}) copy-start(bf16[256,768]{1,0:T(8,128)(2,1)} %constant.38.clone.z_ref) | copy-start | bytes 1179652
  2.9 6.5 %copy-start.4 = (bf16[16,32,128]{2,1,0:T(8,128)(2,1)S(1)}, bf16[16,32,128]{2,1,0:T(8,128)(2,1)}, u32[]{:S(2)}) copy-start(bf16[16,32,128]{2,1,0:T(8,128)(2,1)} %tile_ref.1) | copy-start | bytes 393220
  2.9 8.5 %collective-permute-start.2 = (bf16[32,32,128]{2,1,0:T(8,128)(2,1)S(1)}, bf16[32,32,128]{2,1,0:T(8,128)(2,1)S(1)}, u32[]{:S(2)}, u32[]{:S(2)}) collective-permute-start(bf16[32,32,128]{2,1,0:T(8,128)(2,1)S(1)} %pad_maximum_fusion), channel_id=1, source_target_pairs={{4,0},{6,2},{8,4},{10,6},{12,8},{14,10},{1,5},{3,7},{5,9},{7,11},{... | collective-permute-start | bytes 786440 | tf_op jit(solution)/shard_map/ppermute | solution.py:339
  6.2 10.7 %collective-permute-start.1 = (bf16[32,32,128]{2,1,0:T(8,128)(2,1)S(1)}, bf16[32,32,128]{2,1,0:T(8,128)(2,1)S(1)}, u32[]{:S(2)}, u32[]{:S(2)}) collective-permute-start(bf16[32,32,128]{2,1,0:T(8,128)(2,1)S(1)} %pad_maximum_fusion), channel_id=1, source_target_pairs={{2,0},{4,2},{6,4},{8,6},{10,8},{12,10},{14,12},{1,3},{3,5},{5,7},{... | collective-permute-start | bytes 786440 | tf_op jit(solution)/shard_map/ppermute | solution.py:339
  9.4 7.7 %collective-permute-start.5 = (bf16[16,32,128]{2,1,0:T(8,128)(2,1)S(1)}, bf16[16,32,128]{2,1,0:T(8,128)(2,1)S(1)}, u32[]{:S(2)}, u32[]{:S(2)}) collective-permute-start(bf16[16,32,128]{2,1,0:T(8,128)(2,1)S(1)} %copy-done.4), channel_id=1, source_target_pairs={{1,0},{2,1},{3,2},{4,3},{5,4},{6,5},{7,6},{8,7},{9,8},{10,9},{11,1... | collective-permute-start | bytes 393224 | tf_op jit(solution)/shard_map/ppermute | solution.py:339
  11.3 5.6 %copy-start.8 = (s32[1,8]{1,0:T(1,128)S(1)}, s32[1,8]{1,0:T(1,128)}, u32[]{:S(2)}) copy-start(s32[1,8]{1,0:T(1,128)} %param.14) | copy-start | bytes 100
  11.3 5.6 %copy-start.9 = (s32[1,8]{1,0:T(1,128)S(1)}, s32[1,8]{1,0:T(1,128)}, u32[]{:S(2)}) copy-start(s32[1,8]{1,0:T(1,128)} %param.13) | copy-start | bytes 100
  11.4 7.3 %collective-permute-start.4 = (bf16[32,32,128]{2,1,0:T(8,128)(2,1)S(1)}, bf16[32,32,128]{2,1,0:T(8,128)(2,1)S(1)}, u32[]{:S(2)}, u32[]{:S(2)}) collective-permute-start(bf16[32,32,128]{2,1,0:T(8,128)(2,1)S(1)} %collective-permute-done.2.far_ref), channel_id=1, source_target_pairs={{0,1},{1,0},{2,3},{3,2},{4,5},{5,4},{6,7},{7,6},{8,9},{9,8},{10,11... | collective-permute-start | bytes 786440 | tf_op jit(solution)/shard_map/ppermute | solution.py:339
  16.9 1.8 %collective-permute-start.3 = (bf16[32,32,128]{2,1,0:T(8,128)(2,1)S(1)}, bf16[32,32,128]{2,1,0:T(8,128)(2,1)S(1)}, u32[]{:S(2)}, u32[]{:S(2)}) collective-permute-start(bf16[32,32,128]{2,1,0:T(8,128)(2,1)S(1)} %collective-permute-done.1.near_ref), channel_id=1, source_target_pairs={{0,1},{1,0},{2,3},{3,2},{4,5},{5,4},{6,7},{7,6},{8,9},{9,8},{10,11... | collective-permute-start | bytes 786440 | tf_op jit(solution)/shard_map/ppermute | solution.py:339
  17.1 1.6 %copy-start.1 = (bf16[16,32,128]{2,1,0:T(8,128)(2,1)S(1)}, bf16[16,32,128]{2,1,0:T(8,128)(2,1)}, u32[]{:S(2)}) copy-start(bf16[16,32,128]{2,1,0:T(8,128)(2,1)} %own_ref.1) | copy-start | bytes 393220
  17.1 1.6 %copy-start.2 = (bf16[768,128]{1,0:T(8,128)(2,1)S(1)}, bf16[768,128]{1,0:T(8,128)(2,1)}, u32[]{:S(2)}) copy-start(bf16[768,128]{1,0:T(8,128)(2,1)} %constant.42.clone.y_inverse_ref) | copy-start | bytes 589828
  17.1 1.7 %copy-start.3 = (bf16[128,768]{1,0:T(8,128)(2,1)S(1)}, bf16[128,768]{1,0:T(8,128)(2,1)}, u32[]{:S(2)}) copy-start(bf16[128,768]{1,0:T(8,128)(2,1)} %constant.41.clone.z_inverse_ref) | copy-start | bytes 589828
  17.1 1.7 %copy-start.6 = (bf16[256,256]{1,0:T(8,128)(2,1)S(1)}, bf16[256,256]{1,0:T(8,128)(2,1)}, u32[]{:S(2)}) copy-start(bf16[256,256]{1,0:T(8,128)(2,1)} %constant.40.clone.y_low_ref) | copy-start | bytes 393220
  17.1 1.7 %copy-start.7 = (bf16[256,256]{1,0:T(8,128)(2,1)S(1)}, bf16[256,256]{1,0:T(8,128)(2,1)}, u32[]{:S(2)}) copy-start(bf16[256,256]{1,0:T(8,128)(2,1)} %constant.39.clone.y_high_ref) | copy-start | bytes 393220
  27.2 8.3 %collective-permute-start.7 = (f32[256,128]{1,0:T(8,128)S(1)}, f32[256,128]{1,0:T(8,128)S(1)}, u32[]{:S(2)}, u32[]{:S(2)}) collective-permute-start(f32[256,128]{1,0:T(8,128)S(1)} %second_maps.1.own_ref), channel_id=1, source_target_pairs={{2,1},{4,3},{6,5},{8,7},{10,9},{12,11},{14,13},{1,2},{3,4},{5,6},{... | collective-permute-start | bytes 393224 | tf_op jit(solution)/shard_map/ppermute | solution.py:339
  31.5 4.0 %collective-permute-start.6 = (f32[256,128]{1,0:T(8,128)S(1)}, f32[256,128]{1,0:T(8,128)S(1)}, u32[]{:S(2)}, u32[]{:S(2)}) collective-permute-start(f32[256,128]{1,0:T(8,128)S(1)} %second_maps.1.own_ref), channel_id=1, source_target_pairs={{0,1},{1,0},{2,3},{3,2},{4,5},{5,4},{6,7},{7,6},{8,9},{9,8},{10,11... | collective-permute-start | bytes 393224 | tf_op jit(solution)/shard_map/ppermute | solution.py:339
where the time goes:
time: 36.5 us; the launch traced here: 36.3 us
  starting transfers between devices  14.9 us (41%)
  Pallas kernels  10.8 us (30%)
  waiting for transfers between devices  9.13 us (25%)
  other arithmetic  1.07 us (3%)
    ppermute x8, starting transfers between devices, send(): return lax.ppermute(value, 'gx', pairs)  14.9 us
    ppermute x8, waiting for transfers between devices, send(): return lax.ppermute(value, 'gx', pairs)  9.13 us
    pallas_call x1, Pallas kernels, local(): pl.pallas_call(second_kernel, out_shape=jax.ShapeDtypeStruct((SR * SR, LA...  8.47 us
    pallas_call x1, Pallas kernels, local(): pl.pallas_call(first_kernel, out_shape=(spectrum, spectrum, jax.ShapeDtyp...  1.57 us
    select_n x1, other arithmetic, local(): low = jnp.where(odd == 0, second_volume, mate_tile)  0.96 us
    pallas_call x1, Pallas kernels, local(): pl.pallas_call(product_kernel, out_shape=jax.ShapeDtypeStruct((SR * SR, L...  0.79 us
  transfers between devices with their start and end apart: 8, of which 3 were waited for; matrix products, arithmetic and copies ran while one was open for 0% of the time, Pallas kernels for 4%

commit v1 on v0

--- a/solution.py
+++ b/solution.py
@@ -145,33 +145,33 @@
     return energy
 
 
-def finish_stage(energy, real_ref):
+def finish_stage(energy, block):
     rows, zero_lane = positions((8, LANES))
     is_mean = zero_lane & (rows == 0)
-    block = real_ref[:, 0:8]
     means = jnp.where(is_mean, jnp.sum(block, 0) * (1.0 / WIN), 0.0)
     centred = block - means[None]
-    real_ref[:, 0:8] = centred
     total = energy + jnp.sum(jnp.where(is_mean[None], centred * centred, 0.0), 0)
     total = jnp.broadcast_to(jnp.sum(total, 0, keepdims=True), (8, LANES))
     group_row = lax.broadcasted_iota(jnp.int32, (LANES, LANES), 0) // HALF
     group_col = lax.broadcasted_iota(jnp.int32, (LANES, LANES), 1) // HALF
     same = (group_row == group_col).astype(F32)
     summed = jnp.dot(total, same, precision=lax.Precision.HIGHEST, preferred_element_type=F32)
-    return summed * (1.0 / (ZS * WIN * WIN * ZS * WIN))
-
-
-def first_kernel(tile_ref, next_ref, y_ref, z_ref, real_ref, imag_ref, var_ref):
+    return centred, summed * (1.0 / (ZS * WIN * WIN * ZS * WIN))
+
+
+def first_kernel(use_ref, tile_ref, other_ref, y_ref, z_ref, real_ref, imag_ref, energy_ref):
     energy = jnp.zeros((8, LANES), F32)
     table = y_ref[...]
-    for source, base in ((tile_ref, 0), (next_ref, STEP)):
-        for start in range(0, STEP, 8):
-            rows = source[start : start + 8].reshape(8 * ZS, NY)
-            values = dot(jnp.concatenate([rows, rows], 1), table)
-            energy = energy + z_stage(
-                values[: 4 * ZS], values[4 * ZS :], z_ref, real_ref, imag_ref, base + start
-            )
-    var_ref[...] = finish_stage(energy, real_ref)
+    use = use_ref[0].astype(BF16)
+    use_other = use_ref[1].astype(BF16)
+    for start in range(0, STEP, 8):
+        rows = tile_ref[start : start + 8] * use + other_ref[start : start + 8] * use_other
+        rows = rows.reshape(8 * ZS, NY)
+        values = dot(jnp.concatenate([rows, rows], 1), table)
+        energy = energy + z_stage(
+            values[: 4 * ZS], values[4 * ZS :], z_ref, real_ref, imag_ref, start
+        )
+    energy_ref[...] = energy
 
 
 def second_kernel(
@@ -182,9 +182,12 @@
     far_ref,
     mate_near_ref,
     mate_far_ref,
-    first_real_ref,
-    first_imag_ref,
-    first_var_ref,
+    low_real_ref,
+    low_imag_ref,
+    low_energy_ref,
+    high_real_ref,
+    high_imag_ref,
+    high_energy_ref,
     y_high_ref,
     y_low_ref,
     z_ref,
@@ -199,6 +202,8 @@
     sems,
 ):
     odd = starts_ref[2, 0]
+    tiles_below = starts_ref[2, 1]
+    tiles = starts_ref[2, 2]
     two = 2 * STEP
     copies = [
         pltpu.make_async_copy(source, region_ref.at[pl.ds(place, source.shape[0])], sems.at[n])
@@ -217,6 +222,11 @@
         copy.start()
     for copy in copies:
         copy.wait()
+    for tile in range(10):
+
+        @pl.when((tiles_below + tile < 0) | (tiles_below + tile >= tiles))
+        def _(tile=tile):
+            region_ref[tile * STEP : (tile + 1) * STEP] = jnp.zeros((STEP, ZS, NY), BF16)
 
     lane = lax.broadcasted_iota(jnp.int32, (1, LANES), 1)
 
@@ -244,7 +254,9 @@
         )
 
     energy = lax.fori_loop(0, WIN // 8, eight_x, jnp.zeros((8, LANES), F32))
-    second_var = finish_stage(energy, real_ref)
+    real_ref[:, 0:8], second_var = finish_stage(energy, real_ref[:, 0:8])
+    first_means = jnp.concatenate([low_real_ref[:, 0:8], high_real_ref[:, 0:8]], 0)
+    _, first_var = finish_stage(low_energy_ref[...] + high_energy_ref[...], first_means)
 
     rows, zero_lane = positions((8, LANES))
     special = zero_lane & (rows == 0)
@@ -257,8 +269,10 @@
             ii = [None] * 8
             ri = [None] * 8
             for x in range(WIN):
-                fr = first_real_ref[x, where_z]
-                fi = first_imag_ref[x, where_z]
+                fr_ref = low_real_ref if x < STEP else high_real_ref
+                fi_ref = low_imag_ref if x < STEP else high_imag_ref
+                fr = fr_ref[x % STEP, where_z]
+                fi = fi_ref[x % STEP, where_z]
                 for s in range(8):
                     at = (x + base + s - SR // 2) % WIN
                     gr = real_ref[at, where_z]
@@ -279,7 +293,7 @@
     rows, zero_lane = positions((4, 8, LANES))
     mixed = [zero_lane & (rows != 0), zero_lane]
     scale = 1.0 / (
-        WIN**1.5 * (jnp.sqrt(first_var_ref[...] + 1e-6) * jnp.sqrt(second_var + 1e-6))
+        WIN**1.5 * (jnp.sqrt(first_var + 1e-6) * jnp.sqrt(second_var + 1e-6))
     )
     for start in range(0, SR, 8):
         columns = []
@@ -338,42 +352,55 @@
     def send(value, pairs):
         return lax.ppermute(value, "gx", pairs)
 
+    last = size - 1
     mates = [(i, i ^ 1) for i in range(size)]
-    near = [(2 * q + 2, 2 * q) for q in range(chips - 1)]
-    near += [(2 * q - 1, 2 * q + 1) for q in range(1, chips)]
-    far = [(2 * q + 4, 2 * q) for q in range(chips - 2)]
-    far += [(2 * q - 3, 2 * q + 1) for q in range(2, chips)]
-    after = [(2 * q + 2, 2 * q + 1) for q in range(chips - 1)]
-    across = after + [(b, a) for a, b in after]
+    near = [(2 * q + 2, 2 * q) for q in range(chips - 1)] + [(last, last - 1)]
+    near += [(2 * q - 1, 2 * q + 1) for q in range(1, chips)] + [(0, 1)]
+    far = [(2 * q + 4, 2 * q) for q in range(chips - 2)] + [(last, last - 1), (last - 2, last - 3)]
+    far += [(2 * q - 3, 2 * q + 1) for q in range(2, chips)] + [(0, 1), (2, 3)]
+    across = [(i, i + 1 if i % 2 else i - 1) for i in range(1, last)] + [(0, 0), (last, last)]
 
     mate_tile = send(second_volume, mates)
     low = jnp.where(odd == 0, second_volume, mate_tile)
     high = jnp.where(odd == 0, mate_tile, second_volume)
     pair = jnp.concatenate([low, high], 0)
+    low_tile, pair = lax.optimization_barrier((first_volume, pair))
+    near_pair = send(pair, near)
     far_pair = send(pair, far)
-    near_pair = send(pair, near)
-    next_tile = send(first_volume, [(i + 1, i) for i in range(size - 1)])
+    near_first = send(first_volume, near)
+    mate_first = send(first_volume, mates)
+    mate_near_first = send(near_first, mates)
+
+    def first_spectra(use, tile, other_tile):
+        spectrum = jax.ShapeDtypeStruct((STEP, ZS, LANES), F32)
+        return pl.pallas_call(
+            first_kernel,
+            out_shape=(spectrum, spectrum, jax.ShapeDtypeStruct((8, LANES), F32)),
+            in_specs=[SMEM] + [VMEM] * 4,
+            out_specs=(VMEM, VMEM, VMEM),
+            compiler_params=params(),
+            cost_estimate=pl.CostEstimate(
+                flops=2 * 10**9, transcendentals=0, bytes_accessed=2 * 10**6
+            ),
+            name="first_spectra",
+        )(use, tile, other_tile, first_y_table(), z_table())
+
+    low_part = first_spectra(jnp.array([1, 0], jnp.int32), low_tile, low_tile)
+    far_pair, *low_part = lax.optimization_barrier((far_pair, *low_part))
     mate_far = send(far_pair, mates)
     mate_near = send(near_pair, mates)
-
-    spectrum = jax.ShapeDtypeStruct((WIN, ZS, LANES), F32)
-    first_real, first_imag, first_var = pl.pallas_call(
-        first_kernel,
-        out_shape=(spectrum, spectrum, jax.ShapeDtypeStruct((8, LANES), F32)),
-        in_specs=[VMEM] * 4,
-        out_specs=(VMEM, VMEM, VMEM),
-        compiler_params=params(),
-        name="first_spectra",
-    )(first_volume, next_tile, first_y_table(), z_table())
+    high_use = jnp.stack([(odd == 0) & (position < last), (odd == 1) & (position < last)])
+    high_part = first_spectra(high_use.astype(jnp.int32), mate_first, mate_near_first)
 
     starts_x = shift_x[0] + STEP * (4 + odd)
     starts_y = shift_y[0] + jnp.arange(WY, dtype=jnp.int32) * STEP
-    starts = jnp.stack([starts_x, starts_y, jnp.full((WY,), odd, jnp.int32)], 0)
+    settings = jnp.stack([odd, position - odd - 4, size])
+    starts = jnp.stack([starts_x, starts_y, jnp.pad(settings, (0, WY - 3))], 0)
     y_high, y_low = second_y_table()
     maps = pl.pallas_call(
         second_kernel,
         out_shape=jax.ShapeDtypeStruct((SR * SR, LANES), F32),
-        in_specs=[SMEM] + [ANY] * 6 + [VMEM] * 8,
+        in_specs=[SMEM] + [ANY] * 6 + [VMEM] * 11,
         out_specs=VMEM,
         scratch_shapes=[
             pltpu.VMEM((10 * STEP, ZS, NY), BF16),
@@ -393,9 +420,8 @@
         far_pair,
         mate_near,
         mate_far,
-        first_real,
-        first_imag,
-        first_var,
+        *low_part,
+        *high_part,
         y_high,
         y_low,
         z_table(),

time: 36.5 us -> 33 us (0.904)
  starting transfers between devices: 14.9 us -> 9.7 us
  Pallas kernels: 10.8 us -> 11.6 us
  local copies, waits for them, and re-layouts: 0.13 us -> 0.91 us
    ppermute x8 -> x10, starting transfers between devices: 14.9 us -> 9.7 us  [send(): return lax.ppermute(value, 'gx', pairs)]
    unnamed x20 -> x22, local copies, waits for them, and re-layouts: 0.06 us -> 0.9 us
    pallas_call x1 -> x2, Pallas kernels: 1.57 us -> 2.35 us  [first_spectra(): pl.pallas_call(first_kernel, out_shape=(spectrum, spectrum, jax.ShapeDtyp...]
    ppermute x8 -> x10, waiting for transfers between devices: 9.13 us -> 8.91 us  [send(): return lax.ppermute(value, 'gx', pairs)]
  transfers between devices with their start and end apart: 8 -> 10, of which waited for: 3 -> 4; matrix products, arithmetic and copies ran while one was open for 0% -> 4% of each run, Pallas kernels for 4% -> 7%
where the time goes in v1:
time: 33 us; the launch traced here: 32.4 us
  Pallas kernels  11.6 us (35%)
  starting transfers between devices  9.7 us (29%)
  waiting for transfers between devices  8.91 us (27%)
  other arithmetic  1.15 us (3%)
  local copies, waits for them, and re-layouts  0.91 us (3%)
    ppermute x10, starting transfers between devices, send(): return lax.ppermute(value, 'gx', pairs)  9.7 us
    ppermute x10, waiting for transfers between devices, send(): return lax.ppermute(value, 'gx', pairs)  8.91 us
    pallas_call x1, Pallas kernels, local(): pl.pallas_call(second_kernel, out_shape=jax.ShapeDtypeStruct((SR * SR, LA...  8.44 us
    pallas_call x2, Pallas kernels, first_spectra(): pl.pallas_call(first_kernel, out_shape=(spectrum, spectrum, jax.ShapeDtyp...  2.35 us
    select_n x1, other arithmetic, local(): low = jnp.where(odd == 0, second_volume, mate_tile)  0.96 us
    unnamed x22, local copies, waits for them, and re-layouts  0.9 us
    pallas_call x1, Pallas kernels, local(): pl.pallas_call(product_kernel, out_shape=jax.ShapeDtypeStruct((SR * SR, L...  0.79 us
  transfers between devices with their start and end apart: 10, of which 4 were waited for; matrix products, arithmetic and copies ran while one was open for 4% of the time, Pallas kernels for 7%

profile of v1, /device:TPU:9, one launch (start us, length us, event | category | flops | bytes accessed | tf_op | source)
XLA Modules:
  0.0 32.4 jit_solution(5457214787461074952)
XLA Ops:
  0.0 1.2 %collective-permute-start.6 = (bf16[16,32,128]{2,1,0:T(8,128)(2,1)}, bf16[16,32,128]{2,1,0:T(8,128)(2,1)S(1)}, u32[]{:S(2)}, u32[]{:S(2)}) collective-permute-start(bf16[16,32,128]{2,1,0:T(8,128)(2,1)} %other_ref), channel_id=1, source_target_pairs={{2,0},{4,2},{6,4},{8,6},{10,8},{12,10},{14,12},{15,14},{1,3},{3,5}... | collective-permute-start | bytes 393224 | tf_op jit(solution)/shard_map/ppermute | solution.py:353
  1.2 0.8 %collective-permute-start.5 = (bf16[16,32,128]{2,1,0:T(8,128)(2,1)}, bf16[16,32,128]{2,1,0:T(8,128)(2,1)S(1)}, u32[]{:S(2)}, u32[]{:S(2)}) collective-permute-start(bf16[16,32,128]{2,1,0:T(8,128)(2,1)} %other_ref), channel_id=1, source_target_pairs={{0,1},{1,0},{2,3},{3,2},{4,5},{5,4},{6,7},{7,6},{8,9},{9,8},{10,11... | collective-permute-start | bytes 393224 | tf_op jit(solution)/shard_map/ppermute | solution.py:353
  2.1 0.0 collective-permute-start
  2.1 0.7 %copy-done.9 = s32[1,8]{1,0:T(1,128)S(1)} copy-done((s32[1,8]{1,0:T(1,128)S(1)}, s32[1,8]{1,0:T(1,128)}, u32[]{:S(2)}) %copy-start.9) | copy-done | bytes 56
  2.7 0.0 copy-done.10
  2.8 0.1 pad_add_fusion.1
  2.8 0.8 %collective-permute-done.mate_ref = bf16[16,32,128]{2,1,0:T(8,128)(2,1)S(1)} collective-permute-done((bf16[16,32,128]{2,1,0:T(8,128)(2,1)}, bf16[16,32,128]{2,1,0:T(8,128)(2,1)S(1)}, u32[]{:S(2)}, u32[]{:S(2)}) %collective-permute-start) | collective-permute-done | bytes 131104 | tf_op jit(solution)/shard_map/ppermute | solution.py:353
  3.6 1.0 %broadcast_select_fusion.1 = (bf16[16,32,128]{2,1,0:T(8,128)(2,1)S(1)}, bf16[16,32,128]{2,1,0:T(8,128)(2,1)S(1)}) fusion(bf16[16,32,128]{2,1,0:T(8,128)(2,1)} %own_ref.1, bf16[16,32,128]{2,1,0:T(8,128)(2,1)S(1)} %collective-permute-done.mate_ref, pred[]{:T(512)S(6)} %eq.18), kind=kLoop, calls=%fused_computation.2 | loop fusion | flops 131072 | bytes 524289 | tf_op jit(solution)/shard_map/jit(_where)/select_n | solution.py:364
  4.6 0.0 copy-start.1
  4.6 0.0 copy-start.6
  4.7 1.3 %collective-permute-start.2 = (bf16[32,32,128]{2,1,0:T(8,128)(2,1)S(1)}, bf16[32,32,128]{2,1,0:T(8,128)(2,1)S(1)}, u32[]{:S(2)}, u32[]{:S(2)}) collective-permute-start(bf16[32,32,128]{2,1,0:T(8,128)(2,1)S(1)} %pad_maximum_fusion), channel_id=1, source_target_pairs={{4,0},{6,2},{8,4},{10,6},{12,8},{14,10},{15,14},{13,12},{1,5},{3,7... | collective-permute-start | bytes 786440 | tf_op jit(solution)/shard_map/ppermute | solution.py:353
  6.0 0.6 %collective-permute-start.1 = (bf16[32,32,128]{2,1,0:T(8,128)(2,1)S(1)}, bf16[32,32,128]{2,1,0:T(8,128)(2,1)S(1)}, u32[]{:S(2)}, u32[]{:S(2)}) collective-permute-start(bf16[32,32,128]{2,1,0:T(8,128)(2,1)S(1)} %pad_maximum_fusion), channel_id=1, source_target_pairs={{2,0},{4,2},{6,4},{8,6},{10,8},{12,10},{14,12},{15,14},{1,3},{3,5}... | collective-permute-start | bytes 786440 | tf_op jit(solution)/shard_map/ppermute | solution.py:353
  6.6 0.0 collective-permute-done.6
  6.6 0.4 %collective-permute-start.7 = (bf16[16,32,128]{2,1,0:T(8,128)(2,1)S(1)}, bf16[16,32,128]{2,1,0:T(8,128)(2,1)S(1)}, u32[]{:S(2)}, u32[]{:S(2)}) collective-permute-start(bf16[16,32,128]{2,1,0:T(8,128)(2,1)S(1)} %collective-permute-done.6), channel_id=1, source_target_pairs={{0,1},{1,0},{2,3},{3,2},{4,5},{5,4},{6,7},{7,6},{8,9},{9,8},{10,11... | collective-permute-start | bytes 393224 | tf_op jit(solution)/shard_map/ppermute | solution.py:353
  7.0 0.2 copy-done.8
  7.2 1.2 %first_spectra.2 = (f32[16,32,128]{2,1,0:T(8,128)S(1)}, f32[16,32,128]{2,1,0:T(8,128)S(1)}, f32[8,128]{1,0:T(8,128)S(1)}) custom-call(s32[2]{0:T(128)S(1)} %copy-done.8, bf16[16,32,128]{2,1,0:T(8,128)(2,1)S(1)} %copy-done.6, bf16[16,32,128]{2,1,0:T(8,128)(2,1)S(1)} %copy-done.6, bf16[256,256]{1,0:T(8,128)(2,1)S(1)} %copy-done.7, bf16[256,768]{1,0:T(8,128)(2,1)S(1)} %copy-done.1), custom_call_target="tpu_custom_call" | custom-call | flops 2000000000 | bytes 2000000 | tf_op jit(solution)/shard_map/first_spectra/pallas_call | solution.py:376
  8.4 1.8 %collective-permute-done.2.far_ref = bf16[32,32,128]{2,1,0:T(8,128)(2,1)S(1)} collective-permute-done((bf16[32,32,128]{2,1,0:T(8,128)(2,1)S(1)}, bf16[32,32,128]{2,1,0:T(8,128)(2,1)S(1)}, u32[]{:S(2)}, u32[]{:S(2)}) %collective-permute-start.2) | collective-permute-done | bytes 262176 | tf_op jit(solution)/shard_map/ppermute | solution.py:353
  10.2 1.0 %collective-permute-start.4 = (bf16[32,32,128]{2,1,0:T(8,128)(2,1)S(1)}, bf16[32,32,128]{2,1,0:T(8,128)(2,1)S(1)}, u32[]{:S(2)}, u32[]{:S(2)}) collective-permute-start(bf16[32,32,128]{2,1,0:T(8,128)(2,1)S(1)} %collective-permute-done.2.far_ref), channel_id=1, source_target_pairs={{0,1},{1,0},{2,3},{3,2},{4,5},{5,4},{6,7},{7,6},{8,9},{9,8},{10,11... | collective-permute-start | bytes 786440 | tf_op jit(solution)/shard_map/ppermute | solution.py:353
  11.2 1.9 %collective-permute-done.1.near_ref = bf16[32,32,128]{2,1,0:T(8,128)(2,1)S(1)} collective-permute-done((bf16[32,32,128]{2,1,0:T(8,128)(2,1)S(1)}, bf16[32,32,128]{2,1,0:T(8,128)(2,1)S(1)}, u32[]{:S(2)}, u32[]{:S(2)}) %collective-permute-start.1) | collective-permute-done | bytes 262176 | tf_op jit(solution)/shard_map/ppermute | solution.py:353
  13.1 1.0 %collective-permute-start.3 = (bf16[32,32,128]{2,1,0:T(8,128)(2,1)S(1)}, bf16[32,32,128]{2,1,0:T(8,128)(2,1)S(1)}, u32[]{:S(2)}, u32[]{:S(2)}) collective-permute-start(bf16[32,32,128]{2,1,0:T(8,128)(2,1)S(1)} %collective-permute-done.1.near_ref), channel_id=1, source_target_pairs={{0,1},{1,0},{2,3},{3,2},{4,5},{5,4},{6,7},{7,6},{8,9},{9,8},{10,11... | collective-permute-start | bytes 786440 | tf_op jit(solution)/shard_map/ppermute | solution.py:353
  14.1 0.1 add_convert_fusion.use_ref
  14.2 0.0 copy-start.5
  14.2 0.0 collective-permute-done.5.tile_ref
  14.2 0.0 collective-permute-done.7.other_ref
  14.2 1.2 %first_spectra.3 = (f32[16,32,128]{2,1,0:T(8,128)S(1)}, f32[16,32,128]{2,1,0:T(8,128)S(1)}, f32[8,128]{1,0:T(8,128)S(1)}) custom-call(s32[2]{0:T(128)S(1)} %add_convert_fusion.use_ref, bf16[16,32,128]{2,1,0:T(8,128)(2,1)S(1)} %collective-permute-done.5.tile_ref, bf16[16,32,128]{2,1,0:T(8,128)(2,1)S(1)} %collective-permute-done.7.other_ref, ...), custom_call_target="tpu_custom_call" | custom-call | flops 2000000000 | bytes 2000000 | tf_op jit(solution)/shard_map/first_spectra/pallas_call | solution.py:376
  15.4 0.0 collective-permute-done.3.mate_near_ref
  15.4 0.0 collective-permute-done.4.mate_far_ref
  15.5 8.4 %second_maps.1.own_ref = f32[256,128]{1,0:T(8,128)S(1)} custom-call(s32[3,8]{1,0:T(4,128)S(1)} %pad_add_fusion.starts_ref, bf16[16,32,128]{2,1,0:T(8,128)(2,1)S(1)} %copy-done, bf16[16,32,128]{2,1,0:T(8,128)(2,1)S(1)} %collective-permute-done.mate_ref, bf16[32,32,128]{2,1,0:T(8,128)(2,1)S(1)} %collective-permute-done.1.near_ref, ...), custom_call_target="tpu_custom_call" | custom-call | tf_op jit(solution)/shard_map/second_maps/pallas_call | solution.py:400
  23.9 3.2 %collective-permute-start.9 = (f32[256,128]{1,0:T(8,128)S(1)}, f32[256,128]{1,0:T(8,128)S(1)}, u32[]{:S(2)}, u32[]{:S(2)}) collective-permute-start(f32[256,128]{1,0:T(8,128)S(1)} %second_maps.1.own_ref), channel_id=1, source_target_pairs={{1,2},{2,1},{3,4},{4,3},{5,6},{6,5},{7,8},{8,7},{9,10},{10,9},{11,... | collective-permute-start | bytes 393224 | tf_op jit(solution)/shard_map/ppermute | solution.py:353
  27.1 0.1 collective-permute-start.8
  27.2 4.4 %collective-permute-done.9.other_ref = f32[256,128]{1,0:T(8,128)S(1)} collective-permute-done((f32[256,128]{1,0:T(8,128)S(1)}, f32[256,128]{1,0:T(8,128)S(1)}, u32[]{:S(2)}, u32[]{:S(2)}) %collective-permute-start.9) | collective-permute-done | bytes 131104 | tf_op jit(solution)/shard_map/ppermute | solution.py:353
  31.6 0.8 %product.1 = f32[256,128]{1,0:T(8,128)} custom-call(s32[1]{0:T(128)} %bitcast.edge_ref, f32[256,128]{1,0:T(8,128)S(1)} %second_maps.1.own_ref, f32[256,128]{1,0:T(8,128)S(1)} %collective-permute-done.8.mate_ref, f32[256,128]{1,0:T(8,128)S(1)} %collective-permute-done.9.other_ref), custom_call_target="tpu_custom_call" | custom-call | tf_op jit(solution)/shard_map/product/pallas_call | solution.py:435
  (21 shorter events, 0.1 us)
Async XLA Ops:
  0.0 6.6 %collective-permute-start.6 = (bf16[16,32,128]{2,1,0:T(8,128)(2,1)}, bf16[16,32,128]{2,1,0:T(8,128)(2,1)S(1)}, u32[]{:S(2)}, u32[]{:S(2)}) collective-permute-start(bf16[16,32,128]{2,1,0:T(8,128)(2,1)} %other_ref), channel_id=1, source_target_pairs={{2,0},{4,2},{6,4},{8,6},{10,8},{12,10},{14,12},{15,14},{1,3},{3,5}... | collective-permute-start | bytes 393224 | tf_op jit(solution)/shard_map/ppermute | solution.py:353
  1.2 13.0 %collective-permute-start.5 = (bf16[16,32,128]{2,1,0:T(8,128)(2,1)}, bf16[16,32,128]{2,1,0:T(8,128)(2,1)S(1)}, u32[]{:S(2)}, u32[]{:S(2)}) collective-permute-start(bf16[16,32,128]{2,1,0:T(8,128)(2,1)} %other_ref), channel_id=1, source_target_pairs={{0,1},{1,0},{2,3},{3,2},{4,5},{5,4},{6,7},{7,6},{8,9},{9,8},{10,11... | collective-permute-start | bytes 393224 | tf_op jit(solution)/shard_map/ppermute | solution.py:353
  2.1 1.6 %collective-permute-start = (bf16[16,32,128]{2,1,0:T(8,128)(2,1)}, bf16[16,32,128]{2,1,0:T(8,128)(2,1)S(1)}, u32[]{:S(2)}, u32[]{:S(2)}) collective-permute-start(bf16[16,32,128]{2,1,0:T(8,128)(2,1)} %own_ref.1), channel_id=1, source_target_pairs={{0,1},{1,0},{2,3},{3,2},{4,5},{5,4},{6,7},{7,6},{8,9},{9,8},{10,11... | collective-permute-start | bytes 393224 | tf_op jit(solution)/shard_map/ppermute | solution.py:353
  2.1 0.7 %copy-start.9 = (s32[1,8]{1,0:T(1,128)S(1)}, s32[1,8]{1,0:T(1,128)}, u32[]{:S(2)}) copy-start(s32[1,8]{1,0:T(1,128)} %param.17) | copy-start | bytes 100
  2.1 0.7 %copy-start.10 = (s32[1,8]{1,0:T(1,128)S(1)}, s32[1,8]{1,0:T(1,128)}, u32[]{:S(2)}) copy-start(s32[1,8]{1,0:T(1,128)} %param.16) | copy-start | bytes 100
  3.6 3.4 %copy-start.7 = (bf16[256,256]{1,0:T(8,128)(2,1)S(1)}, bf16[256,256]{1,0:T(8,128)(2,1)}, u32[]{:S(2)}) copy-start(bf16[256,256]{1,0:T(8,128)(2,1)} %constant.45.clone.y_ref) | copy-start | bytes 393220
  4.6 2.4 %copy-start.1 = (bf16[256,768]{1,0:T(8,128)(2,1)S(1)}, bf16[256,768]{1,0:T(8,128)(2,1)}, u32[]{:S(2)}) copy-start(bf16[256,768]{1,0:T(8,128)(2,1)} %constant.46.clone.z_ref) | copy-start | bytes 1179652
  4.6 2.4 %copy-start.6 = (bf16[16,32,128]{2,1,0:T(8,128)(2,1)S(1)}, bf16[16,32,128]{2,1,0:T(8,128)(2,1)}, u32[]{:S(2)}) copy-start(bf16[16,32,128]{2,1,0:T(8,128)(2,1)} %other_ref) | copy-start | bytes 393220
  4.7 5.5 %collective-permute-start.2 = (bf16[32,32,128]{2,1,0:T(8,128)(2,1)S(1)}, bf16[32,32,128]{2,1,0:T(8,128)(2,1)S(1)}, u32[]{:S(2)}, u32[]{:S(2)}) collective-permute-start(bf16[32,32,128]{2,1,0:T(8,128)(2,1)S(1)} %pad_maximum_fusion), channel_id=1, source_target_pairs={{4,0},{6,2},{8,4},{10,6},{12,8},{14,10},{15,14},{13,12},{1,5},{3,7... | collective-permute-start | bytes 786440 | tf_op jit(solution)/shard_map/ppermute | solution.py:353
  6.0 7.1 %collective-permute-start.1 = (bf16[32,32,128]{2,1,0:T(8,128)(2,1)S(1)}, bf16[32,32,128]{2,1,0:T(8,128)(2,1)S(1)}, u32[]{:S(2)}, u32[]{:S(2)}) collective-permute-start(bf16[32,32,128]{2,1,0:T(8,128)(2,1)S(1)} %pad_maximum_fusion), channel_id=1, source_target_pairs={{2,0},{4,2},{6,4},{8,6},{10,8},{12,10},{14,12},{15,14},{1,3},{3,5}... | collective-permute-start | bytes 786440 | tf_op jit(solution)/shard_map/ppermute | solution.py:353
  6.6 0.7 %copy-start.8 = (s32[2]{0:T(128)S(1)}, s32[2]{0:T(128)}, u32[]{:S(2)}) copy-start(s32[2]{0:T(128)} %constant.44.clone.use_ref) | copy-start | bytes 28
  6.6 7.6 %collective-permute-start.7 = (bf16[16,32,128]{2,1,0:T(8,128)(2,1)S(1)}, bf16[16,32,128]{2,1,0:T(8,128)(2,1)S(1)}, u32[]{:S(2)}, u32[]{:S(2)}) collective-permute-start(bf16[16,32,128]{2,1,0:T(8,128)(2,1)S(1)} %collective-permute-done.6), channel_id=1, source_target_pairs={{0,1},{1,0},{2,3},{3,2},{4,5},{5,4},{6,7},{7,6},{8,9},{9,8},{10,11... | collective-permute-start | bytes 393224 | tf_op jit(solution)/shard_map/ppermute | solution.py:353
  10.2 5.2 %collective-permute-start.4 = (bf16[32,32,128]{2,1,0:T(8,128)(2,1)S(1)}, bf16[32,32,128]{2,1,0:T(8,128)(2,1)S(1)}, u32[]{:S(2)}, u32[]{:S(2)}) collective-permute-start(bf16[32,32,128]{2,1,0:T(8,128)(2,1)S(1)} %collective-permute-done.2.far_ref), channel_id=1, source_target_pairs={{0,1},{1,0},{2,3},{3,2},{4,5},{5,4},{6,7},{7,6},{8,9},{9,8},{10,11... | collective-permute-start | bytes 786440 | tf_op jit(solution)/shard_map/ppermute | solution.py:353
  13.1 2.3 %collective-permute-start.3 = (bf16[32,32,128]{2,1,0:T(8,128)(2,1)S(1)}, bf16[32,32,128]{2,1,0:T(8,128)(2,1)S(1)}, u32[]{:S(2)}, u32[]{:S(2)}) collective-permute-start(bf16[32,32,128]{2,1,0:T(8,128)(2,1)S(1)} %collective-permute-done.1.near_ref), channel_id=1, source_target_pairs={{0,1},{1,0},{2,3},{3,2},{4,5},{5,4},{6,7},{7,6},{8,9},{9,8},{10,11... | collective-permute-start | bytes 786440 | tf_op jit(solution)/shard_map/ppermute | solution.py:353
  14.2 1.2 %copy-start = (bf16[16,32,128]{2,1,0:T(8,128)(2,1)S(1)}, bf16[16,32,128]{2,1,0:T(8,128)(2,1)}, u32[]{:S(2)}) copy-start(bf16[16,32,128]{2,1,0:T(8,128)(2,1)} %own_ref.1) | copy-start | bytes 393220
  14.2 1.3 %copy-start.2 = (bf16[768,128]{1,0:T(8,128)(2,1)S(1)}, bf16[768,128]{1,0:T(8,128)(2,1)}, u32[]{:S(2)}) copy-start(bf16[768,128]{1,0:T(8,128)(2,1)} %constant.50.clone.y_inverse_ref) | copy-start | bytes 589828
  14.2 1.3 %copy-start.3 = (bf16[128,768]{1,0:T(8,128)(2,1)S(1)}, bf16[128,768]{1,0:T(8,128)(2,1)}, u32[]{:S(2)}) copy-start(bf16[128,768]{1,0:T(8,128)(2,1)} %constant.49.clone.z_inverse_ref) | copy-start | bytes 589828
  14.2 1.3 %copy-start.4 = (bf16[256,256]{1,0:T(8,128)(2,1)S(1)}, bf16[256,256]{1,0:T(8,128)(2,1)}, u32[]{:S(2)}) copy-start(bf16[256,256]{1,0:T(8,128)(2,1)} %constant.48.clone.y_low_ref) | copy-start | bytes 393220
  14.2 1.3 %copy-start.5 = (bf16[256,256]{1,0:T(8,128)(2,1)S(1)}, bf16[256,256]{1,0:T(8,128)(2,1)}, u32[]{:S(2)}) copy-start(bf16[256,256]{1,0:T(8,128)(2,1)} %constant.47.clone.y_high_ref) | copy-start | bytes 393220
  23.9 7.7 %collective-permute-start.9 = (f32[256,128]{1,0:T(8,128)S(1)}, f32[256,128]{1,0:T(8,128)S(1)}, u32[]{:S(2)}, u32[]{:S(2)}) collective-permute-start(f32[256,128]{1,0:T(8,128)S(1)} %second_maps.1.own_ref), channel_id=1, source_target_pairs={{1,2},{2,1},{3,4},{4,3},{5,6},{6,5},{7,8},{8,7},{9,10},{10,9},{11,... | collective-permute-start | bytes 393224 | tf_op jit(solution)/shard_map/ppermute | solution.py:353
  27.1 4.5 %collective-permute-start.8 = (f32[256,128]{1,0:T(8,128)S(1)}, f32[256,128]{1,0:T(8,128)S(1)}, u32[]{:S(2)}, u32[]{:S(2)}) collective-permute-start(f32[256,128]{1,0:T(8,128)S(1)} %second_maps.1.own_ref), channel_id=1, source_target_pairs={{0,1},{1,0},{2,3},{3,2},{4,5},{5,4},{6,7},{7,6},{8,9},{9,8},{10,11... | collective-permute-start | bytes 393224 | tf_op jit(solution)/shard_map/ppermute | solution.py:353

commit v2 on v1

--- a/solution.py
+++ b/solution.py
@@ -159,14 +159,11 @@
     return centred, summed * (1.0 / (ZS * WIN * WIN * ZS * WIN))
 
 
-def first_kernel(use_ref, tile_ref, other_ref, y_ref, z_ref, real_ref, imag_ref, energy_ref):
+def first_stage(tile, y_ref, z_ref, real_ref, imag_ref, energy_ref):
     energy = jnp.zeros((8, LANES), F32)
     table = y_ref[...]
-    use = use_ref[0].astype(BF16)
-    use_other = use_ref[1].astype(BF16)
     for start in range(0, STEP, 8):
-        rows = tile_ref[start : start + 8] * use + other_ref[start : start + 8] * use_other
-        rows = rows.reshape(8 * ZS, NY)
+        rows = tile[start : start + 8].reshape(8 * ZS, NY)
         values = dot(jnp.concatenate([rows, rows], 1), table)
         energy = energy + z_stage(
             values[: 4 * ZS], values[4 * ZS :], z_ref, real_ref, imag_ref, start
@@ -174,14 +171,49 @@
     energy_ref[...] = energy
 
 
+def low_kernel(tile_hbm, y_hbm, z_hbm, shift_x_hbm, shift_y_hbm, *refs):
+    *outs, shift_x_ref, shift_y_ref, tile_ref, y_ref, z_ref, sems = refs
+    copies = [
+        pltpu.make_async_copy(source, target, sems.at[n])
+        for n, (source, target) in enumerate(
+            (
+                (z_hbm, z_ref),
+                (y_hbm, y_ref),
+                (tile_hbm, tile_ref),
+                (shift_x_hbm, shift_x_ref),
+                (shift_y_hbm, shift_y_ref),
+            )
+        )
+    ]
+    for copy in copies:
+        copy.start()
+    for copy in copies:
+        copy.wait()
+    first_stage(tile_ref[...], y_ref, z_ref, *outs)
+
+
+def high_kernel(even_ref, odd_ref, *refs):
+    position = lax.axis_index("gx")
+    inside = position < lax.axis_size("gx") - 1
+    odd = position % 2
+    use_even = jnp.where(inside & (odd == 0), 1.0, 0.0).astype(BF16)
+    use_odd = jnp.where(inside & (odd == 1), 1.0, 0.0).astype(BF16)
+    first_stage(even_ref[...] * use_even + odd_ref[...] * use_odd, *refs)
+
+
 def second_kernel(
-    starts_ref,
+    shift_x_ref,
+    shift_y_ref,
     own_ref,
     mate_ref,
-    near_ref,
-    far_ref,
-    mate_near_ref,
-    mate_far_ref,
+    near_own_ref,
+    near_mate_ref,
+    far_own_ref,
+    far_mate_ref,
+    mate_near_own_ref,
+    mate_near_mate_ref,
+    mate_far_own_ref,
+    mate_far_mate_ref,
     low_real_ref,
     low_imag_ref,
     low_energy_ref,
@@ -199,29 +231,29 @@
     imag_ref,
     cross_real_ref,
     cross_imag_ref,
-    sems,
 ):
-    odd = starts_ref[2, 0]
-    tiles_below = starts_ref[2, 1]
-    tiles = starts_ref[2, 2]
-    two = 2 * STEP
-    copies = [
-        pltpu.make_async_copy(source, region_ref.at[pl.ds(place, source.shape[0])], sems.at[n])
-        for n, (source, place) in enumerate(
-            (
-                (own_ref, 2 * two + STEP * odd),
-                (mate_ref, 2 * two + STEP * (1 - odd)),
-                (near_ref, two + 2 * two * (1 - odd)),
-                (far_ref, 4 * two * (1 - odd)),
-                (mate_near_ref, two + 2 * two * odd),
-                (mate_far_ref, 4 * two * odd),
-            )
-        )
-    ]
-    for copy in copies:
-        copy.start()
-    for copy in copies:
-        copy.wait()
+    position = lax.axis_index("gx")
+    tiles = lax.axis_size("gx")
+    odd = position % 2
+    even = 1 - odd
+    tiles_below = position - odd - 4
+    shifts_x, shifts_y = shift_x_ref[...], shift_y_ref[...]
+    starts_x = [shifts_x[0, j] + STEP * (4 + odd) for j in range(WY)]
+    starts_y = [shifts_y[0, j] + STEP * j for j in range(WY)]
+    tiles_at = (
+        (own_ref, 4 + odd),
+        (mate_ref, 4 + even),
+        (near_own_ref, 3 + 3 * even),
+        (near_mate_ref, 2 + 5 * even),
+        (far_own_ref, 1 + 7 * even),
+        (far_mate_ref, 9 * even),
+        (mate_near_own_ref, 3 + 3 * odd),
+        (mate_near_mate_ref, 2 + 5 * odd),
+        (mate_far_own_ref, 1 + 7 * odd),
+        (mate_far_mate_ref, 9 * odd),
+    )
+    for tile_ref, at in tiles_at:
+        region_ref[pl.ds(at * STEP, STEP)] = tile_ref[...]
     for tile in range(10):
 
         @pl.when((tiles_below + tile < 0) | (tiles_below + tile >= tiles))
@@ -237,8 +269,8 @@
             total = None
             for n in range(4):
                 j = half * 4 + n
-                start_y = starts_ref[1, j]
-                block = region_ref[pl.ds(starts_ref[0, j] + start, 8)].reshape(8 * ZS, NY)
+                start_y = starts_y[j]
+                block = region_ref[pl.ds(starts_x[j] + start, 8)].reshape(8 * ZS, NY)
                 turned = pltpu.roll(block.astype(F32), (n * WIN - start_y) & (LANES - 1), 1)
                 y = lane - n * WIN + start_y
                 inside = (lane // WIN == n) & (y >= 0) & (y < NY)
@@ -325,12 +357,14 @@
             out_ref[where_out] = values * scale[0:1]
 
 
-def product_kernel(edge_ref, own_ref, mate_ref, other_ref, out_ref):
+def product_kernel(own_ref, mate_ref, other_ref, out_ref):
+    position = lax.axis_index("gx")
+    edge = (position == 0) | (position == lax.axis_size("gx") - 1)
     own = own_ref[...]
     lane = lax.broadcasted_iota(jnp.int32, own.shape, 1)
     below = jnp.where(lane < SR, 1.0, pltpu.roll(own, SR, 1))
     above = jnp.where(lane >= LANES - SR, 1.0, pltpu.roll(own, LANES - SR, 1))
-    other = jnp.where(edge_ref[0] == 1, 1.0, other_ref[...])
+    other = jnp.where(edge, 1.0, other_ref[...])
     out_ref[...] = own * mate_ref[...] * other * below * above
 
 
@@ -339,15 +373,12 @@
 
 
 VMEM = pl.BlockSpec(memory_space=pltpu.VMEM)
-SMEM = pl.BlockSpec(memory_space=pltpu.SMEM)
-ANY = pl.BlockSpec(memory_space=pl.ANY)
+HBM = pl.BlockSpec(memory_space=pltpu.HBM)
 
 
 def local(first_volume, second_volume, shift_x, shift_y):
     size = lax.axis_size("gx")
     chips = size // 2
-    position = lax.axis_index("gx")
-    odd = position % 2
 
     def send(value, pairs):
         return lax.ppermute(value, "gx", pairs)
@@ -360,47 +391,52 @@
     far += [(2 * q - 3, 2 * q + 1) for q in range(2, chips)] + [(0, 1), (2, 3)]
     across = [(i, i + 1 if i % 2 else i - 1) for i in range(1, last)] + [(0, 0), (last, last)]
 
+    near_first = send(first_volume, near)
+    near_own = send(second_volume, near)
     mate_tile = send(second_volume, mates)
-    low = jnp.where(odd == 0, second_volume, mate_tile)
-    high = jnp.where(odd == 0, mate_tile, second_volume)
-    pair = jnp.concatenate([low, high], 0)
-    low_tile, pair = lax.optimization_barrier((first_volume, pair))
-    near_pair = send(pair, near)
-    far_pair = send(pair, far)
-    near_first = send(first_volume, near)
+    low_tile, mate_tile = lax.optimization_barrier((first_volume, mate_tile))
+    near_mate = send(mate_tile, near)
+    far_own = send(second_volume, far)
+    far_mate = send(mate_tile, far)
     mate_first = send(first_volume, mates)
-    mate_near_first = send(near_first, mates)
-
-    def first_spectra(use, tile, other_tile):
-        spectrum = jax.ShapeDtypeStruct((STEP, ZS, LANES), F32)
+
+    tables = (first_y_table(), z_table())
+    spectrum = jax.ShapeDtypeStruct((STEP, ZS, LANES), F32)
+
+    def first_spectra(kernel, specs, scratch, more_out, *operands):
+        outs = (spectrum, spectrum, jax.ShapeDtypeStruct((8, LANES), F32), *more_out)
         return pl.pallas_call(
-            first_kernel,
-            out_shape=(spectrum, spectrum, jax.ShapeDtypeStruct((8, LANES), F32)),
-            in_specs=[SMEM] + [VMEM] * 4,
-            out_specs=(VMEM, VMEM, VMEM),
+            kernel,
+            out_shape=outs,
+            in_specs=specs,
+            out_specs=(VMEM,) * len(outs),
+            scratch_shapes=scratch,
             compiler_params=params(),
             cost_estimate=pl.CostEstimate(
                 flops=2 * 10**9, transcendentals=0, bytes_accessed=2 * 10**6
             ),
             name="first_spectra",
-        )(use, tile, other_tile, first_y_table(), z_table())
-
-    low_part = first_spectra(jnp.array([1, 0], jnp.int32), low_tile, low_tile)
-    far_pair, *low_part = lax.optimization_barrier((far_pair, *low_part))
-    mate_far = send(far_pair, mates)
-    mate_near = send(near_pair, mates)
-    high_use = jnp.stack([(odd == 0) & (position < last), (odd == 1) & (position < last)])
-    high_part = first_spectra(high_use.astype(jnp.int32), mate_first, mate_near_first)
-
-    starts_x = shift_x[0] + STEP * (4 + odd)
-    starts_y = shift_y[0] + jnp.arange(WY, dtype=jnp.int32) * STEP
-    settings = jnp.stack([odd, position - odd - 4, size])
-    starts = jnp.stack([starts_x, starts_y, jnp.pad(settings, (0, WY - 3))], 0)
+        )(*operands)
+
+    scratch = [pltpu.VMEM(v.shape, BF16) for v in (first_volume, *tables)]
+    scratch.append(pltpu.SemaphoreType.DMA((5,)))
+    in_hbm = [
+        pltpu.with_memory_space_constraint(jnp.asarray(v), pltpu.HBM)
+        for v in (low_tile, *tables, shift_x, shift_y)
+    ]
+    shifts = [jax.ShapeDtypeStruct(v.shape, v.dtype) for v in (shift_x, shift_y)]
+    *low_part, shift_x, shift_y = first_spectra(low_kernel, [HBM] * 5, scratch, shifts, *in_hbm)
+    near_first, *low_part = lax.optimization_barrier((near_first, *low_part))
+    mate_near_first = send(near_first, mates)
+    side = (near_own, near_mate, far_own, far_mate)
+    mate_side = [send(tile, mates) for tile in side]
+    high_part = first_spectra(high_kernel, [VMEM] * 4, [], [], mate_first, mate_near_first, *tables)
+
     y_high, y_low = second_y_table()
     maps = pl.pallas_call(
         second_kernel,
         out_shape=jax.ShapeDtypeStruct((SR * SR, LANES), F32),
-        in_specs=[SMEM] + [ANY] * 6 + [VMEM] * 11,
+        in_specs=[VMEM] * 23,
         out_specs=VMEM,
         scratch_shapes=[
             pltpu.VMEM((10 * STEP, ZS, NY), BF16),
@@ -408,18 +444,16 @@
             pltpu.VMEM((WIN, ZS, LANES), F32),
             pltpu.VMEM((SR, ZS, LANES), F32),
             pltpu.VMEM((SR, ZS, LANES), F32),
-            pltpu.SemaphoreType.DMA((6,)),
         ],
         compiler_params=params(),
         name="second_maps",
     )(
-        starts,
+        shift_x,
+        shift_y,
         second_volume,
         mate_tile,
-        near_pair,
-        far_pair,
-        mate_near,
-        mate_far,
+        *side,
+        *mate_side,
         *low_part,
         *high_part,
         y_high,
@@ -431,15 +465,14 @@
 
     other_maps = send(maps, across)
     mate_maps = send(maps, mates)
-    edge = ((position == 0) | (position == size - 1)).astype(jnp.int32).reshape(1)
     product = pl.pallas_call(
         product_kernel,
         out_shape=jax.ShapeDtypeStruct((SR * SR, LANES), F32),
-        in_specs=[SMEM, VMEM, VMEM, VMEM],
+        in_specs=[VMEM] * 3,
         out_specs=VMEM,
         compiler_params=params(),
         name="product",
-    )(edge, maps, mate_maps, other_maps)
+    )(maps, mate_maps, other_maps)
     return product.reshape(1, SR, SR, LANES)
 
 

time: 33 us -> 31.2 us (0.945); the launches traced: 32.4 us -> 31.1 us
  starting transfers between devices: 9.7 us -> 14.2 us
  waiting for transfers between devices: 8.91 us -> 6.1 us
  other arithmetic: 1.15 us -> 0 us
  Pallas kernels: 11.6 us -> 10.6 us
  local copies, waits for them, and re-layouts: 0.91 us -> 0.04 us
    ppermute x10 -> x14, starting transfers between devices: 9.7 us -> 14.2 us  [send(): return lax.ppermute(value, 'gx', pairs)]
    ppermute x10 -> x14, waiting for transfers between devices: 8.91 us -> 6.1 us  [send(): return lax.ppermute(value, 'gx', pairs)]
    pallas_call x1, Pallas kernels: 8.44 us -> 7.43 us  [local(): pl.pallas_call(second_kernel, out_shape=jax.ShapeDtypeStruct((SR * SR, LA...]
    select_n x1 -> x0, other arithmetic: 0.96 us -> none  [local(): low = jnp.where(odd == 0, second_volume, mate_tile)]
    unnamed x22 -> x14, local copies, waits for them, and re-layouts: 0.9 us -> 0.04 us
  transfers between devices with their start and end apart: 10 -> 14, of which waited for: 4 -> 2; matrix products, arithmetic and copies ran while one was open for 4% -> 0% of each run, Pallas kernels for 7% -> 8%
where the time goes in v2:
time: 31.2 us; the launch traced here: 31.1 us
  starting transfers between devices  14.2 us (46%)
  Pallas kernels  10.6 us (34%)
  waiting for transfers between devices  6.1 us (20%)
    ppermute x14, starting transfers between devices, send(): return lax.ppermute(value, 'gx', pairs)  14.2 us
    pallas_call x1, Pallas kernels, local(): pl.pallas_call(second_kernel, out_shape=jax.ShapeDtypeStruct((SR * SR, LA...  7.43 us
    ppermute x14, waiting for transfers between devices, send(): return lax.ppermute(value, 'gx', pairs)  6.1 us
    pallas_call x2, Pallas kernels, first_spectra(): pl.pallas_call(kernel, out_shape=outs, in_specs=specs, out_specs=(VMEM,)...  2.38 us
    pallas_call x1, Pallas kernels, local(): pl.pallas_call(product_kernel, out_shape=jax.ShapeDtypeStruct((SR * SR, L...  0.79 us
  transfers between devices with their start and end apart: 14, of which 2 were waited for; matrix products, arithmetic and copies ran while one was open for 0% of the time, Pallas kernels for 8%

profile of v2, /device:TPU:9, one launch (start us, length us, event | category | flops | bytes accessed | tf_op | source)
XLA Modules:
  0.0 31.1 jit_solution(12265814218718094253)
XLA Ops:
  0.0 0.7 %collective-permute-start = (bf16[16,32,128]{2,1,0:T(8,128)(2,1)}, bf16[16,32,128]{2,1,0:T(8,128)(2,1)S(1)}, u32[]{:S(2)}, u32[]{:S(2)}) collective-permute-start(bf16[16,32,128]{2,1,0:T(8,128)(2,1)} %own_ref.1), channel_id=1, source_target_pairs={{0,1},{1,0},{2,3},{3,2},{4,5},{5,4},{6,7},{7,6},{8,9},{9,8},{10,11... | collective-permute-start | bytes 393224 | tf_op jit(solution)/shard_map/ppermute | solution.py:384
  0.7 1.2 %collective-permute-start.9 = (bf16[16,32,128]{2,1,0:T(8,128)(2,1)}, bf16[16,32,128]{2,1,0:T(8,128)(2,1)S(1)}, u32[]{:S(2)}, u32[]{:S(2)}) collective-permute-start(bf16[16,32,128]{2,1,0:T(8,128)(2,1)} %tile_hbm), channel_id=1, source_target_pairs={{2,0},{4,2},{6,4},{8,6},{10,8},{12,10},{14,12},{15,14},{1,3},{3,5}... | collective-permute-start | bytes 393224 | tf_op jit(solution)/shard_map/ppermute | solution.py:384
  1.9 0.2 collective-permute-start.10
  2.2 1.0 %collective-permute-start.1 = (bf16[16,32,128]{2,1,0:T(8,128)(2,1)}, bf16[16,32,128]{2,1,0:T(8,128)(2,1)S(1)}, u32[]{:S(2)}, u32[]{:S(2)}) collective-permute-start(bf16[16,32,128]{2,1,0:T(8,128)(2,1)} %own_ref.1), channel_id=1, source_target_pairs={{2,0},{4,2},{6,4},{8,6},{10,8},{12,10},{14,12},{15,14},{1,3},{3,5}... | collective-permute-start | bytes 393224 | tf_op jit(solution)/shard_map/ppermute | solution.py:384
  3.2 1.3 %collective-permute-start.3 = (bf16[16,32,128]{2,1,0:T(8,128)(2,1)}, bf16[16,32,128]{2,1,0:T(8,128)(2,1)S(1)}, u32[]{:S(2)}, u32[]{:S(2)}) collective-permute-start(bf16[16,32,128]{2,1,0:T(8,128)(2,1)} %own_ref.1), channel_id=1, source_target_pairs={{4,0},{6,2},{8,4},{10,6},{12,8},{14,10},{15,14},{13,12},{1,5},{3,7... | collective-permute-start | bytes 393224 | tf_op jit(solution)/shard_map/ppermute | solution.py:384
  4.5 0.0 collective-permute-done.mate_ref
  4.5 1.5 %collective-permute-start.2 = (bf16[16,32,128]{2,1,0:T(8,128)(2,1)S(1)}, bf16[16,32,128]{2,1,0:T(8,128)(2,1)S(1)}, u32[]{:S(2)}, u32[]{:S(2)}) collective-permute-start(bf16[16,32,128]{2,1,0:T(8,128)(2,1)S(1)} %collective-permute-done.mate_ref), channel_id=1, source_target_pairs={{2,0},{4,2},{6,4},{8,6},{10,8},{12,10},{14,12},{15,14},{1,3},{3,5}... | collective-permute-start | bytes 393224 | tf_op jit(solution)/shard_map/ppermute | solution.py:384
  5.9 1.8 %first_spectra.2 = (f32[16,32,128]{2,1,0:T(8,128)S(1)}, f32[16,32,128]{2,1,0:T(8,128)S(1)}, f32[8,128]{1,0:T(8,128)S(1)}, s32[1,8]{1,0:T(1,128)S(1)}, s32[1,8]{1,0:T(1,128)S(1)}) custom-call(bf16[16,32,128]{2,1,0:T(8,128)(2,1)} %tile_hbm, bf16[256,256]{1,0:T(8,128)(2,1)} %constant.12.clone.y_hbm.refs_0_, ...), custom_call_target="tpu_custom_call" | custom-call | flops 2000000000 | bytes 2000000 | tf_op jit(solution)/shard_map/first_spectra/pallas_call | solution.py:408
  7.7 0.0 collective-permute-done.9
  7.7 0.0 collective-permute-start.4
  7.7 0.0 copy-start.1
  7.7 0.0 copy-start.2
  7.8 0.0 copy-start.3
  7.8 0.0 copy-start.4
  7.8 0.0 copy-start.5
  7.8 0.0 collective-permute-done.10.even_ref
  7.8 1.0 %collective-permute-start.11 = (bf16[16,32,128]{2,1,0:T(8,128)(2,1)S(1)}, bf16[16,32,128]{2,1,0:T(8,128)(2,1)S(1)}, u32[]{:S(2)}, u32[]{:S(2)}) collective-permute-start(bf16[16,32,128]{2,1,0:T(8,128)(2,1)S(1)} %collective-permute-done.9), channel_id=1, source_target_pairs={{0,1},{1,0},{2,3},{3,2},{4,5},{5,4},{6,7},{7,6},{8,9},{9,8},{10,11... | collective-permute-start | bytes 393224 | tf_op jit(solution)/shard_map/ppermute | solution.py:384
  8.9 0.0 collective-permute-done.1.near_own_ref
  8.9 2.7 %collective-permute-start.5 = (bf16[16,32,128]{2,1,0:T(8,128)(2,1)S(1)}, bf16[16,32,128]{2,1,0:T(8,128)(2,1)S(1)}, u32[]{:S(2)}, u32[]{:S(2)}) collective-permute-start(bf16[16,32,128]{2,1,0:T(8,128)(2,1)S(1)} %collective-permute-done.1.near_own_ref), channel_id=1, source_target_pairs={{0,1},{1,0},{2,3},{3,2},{4,5},{5,4},{6,7},{7,6},{8,9},{9,8},{10,11... | collective-permute-start | bytes 393224 | tf_op jit(solution)/shard_map/ppermute | solution.py:384
  11.5 0.0 collective-permute-start.7
  11.6 1.4 %collective-permute-start.6 = (bf16[16,32,128]{2,1,0:T(8,128)(2,1)S(1)}, bf16[16,32,128]{2,1,0:T(8,128)(2,1)S(1)}, u32[]{:S(2)}, u32[]{:S(2)}) collective-permute-start(bf16[16,32,128]{2,1,0:T(8,128)(2,1)S(1)} %collective-permute-done.2.near_mate_ref), channel_id=1, source_target_pairs={{0,1},{1,0},{2,3},{3,2},{4,5},{5,4},{6,7},{7,6},{8,9},{9,8},{10,11... | collective-permute-start | bytes 393224 | tf_op jit(solution)/shard_map/ppermute | solution.py:384
  12.9 0.0 collective-permute-done.4.far_mate_ref
  13.0 0.8 %collective-permute-start.8 = (bf16[16,32,128]{2,1,0:T(8,128)(2,1)S(1)}, bf16[16,32,128]{2,1,0:T(8,128)(2,1)S(1)}, u32[]{:S(2)}, u32[]{:S(2)}) collective-permute-start(bf16[16,32,128]{2,1,0:T(8,128)(2,1)S(1)} %collective-permute-done.4.far_mate_ref), channel_id=1, source_target_pairs={{0,1},{1,0},{2,3},{3,2},{4,5},{5,4},{6,7},{7,6},{8,9},{9,8},{10,11... | collective-permute-start | bytes 393224 | tf_op jit(solution)/shard_map/ppermute | solution.py:384
  13.7 0.6 %first_spectra.3 = (f32[16,32,128]{2,1,0:T(8,128)S(1)}, f32[16,32,128]{2,1,0:T(8,128)S(1)}, f32[8,128]{1,0:T(8,128)S(1)}) custom-call(bf16[16,32,128]{2,1,0:T(8,128)(2,1)S(1)} %collective-permute-done.10.even_ref, bf16[16,32,128]{2,1,0:T(8,128)(2,1)S(1)} %collective-permute-done.11.odd_ref, bf16[256,256]{1,0:T(8,128)(2,1)S(1)} %copy-done.6, ...), custom_call_target="tpu_custom_call" | custom-call | flops 2000000000 | bytes 2000000 | tf_op jit(solution)/shard_map/first_spectra/pallas_call | solution.py:408
  14.3 0.0 collective-permute-done.5.mate_near_own_ref
  14.4 0.0 collective-permute-done.7.mate_far_own_ref
  14.4 0.3 %collective-permute-done.8.mate_far_mate_ref = bf16[16,32,128]{2,1,0:T(8,128)(2,1)S(1)} collective-permute-done((bf16[16,32,128]{2,1,0:T(8,128)(2,1)S(1)}, bf16[16,32,128]{2,1,0:T(8,128)(2,1)S(1)}, u32[]{:S(2)}, u32[]{:S(2)}) %collective-permute-start.8) | collective-permute-done | bytes 131104 | tf_op jit(solution)/shard_map/ppermute | solution.py:384
  14.7 7.4 %second_maps.1.own_ref = f32[256,128]{1,0:T(8,128)S(1)} custom-call(s32[1,8]{1,0:T(1,128)S(1)} %get-tuple-element.20.shift_x_ref, s32[1,8]{1,0:T(1,128)S(1)} %get-tuple-element.21.shift_y_ref, bf16[16,32,128]{2,1,0:T(8,128)(2,1)S(1)} %copy-done.3, bf16[16,32,128]{2,1,0:T(8,128)(2,1)S(1)} %collective-permute-done.mate_ref, ...), custom_call_target="tpu_custom_call" | custom-call | tf_op jit(solution)/shard_map/second_maps/pallas_call | solution.py:436
  22.2 0.4 %collective-permute-start.12 = (f32[256,128]{1,0:T(8,128)S(1)}, f32[256,128]{1,0:T(8,128)S(1)}, u32[]{:S(2)}, u32[]{:S(2)}) collective-permute-start(f32[256,128]{1,0:T(8,128)S(1)} %second_maps.1.own_ref), channel_id=1, source_target_pairs={{0,1},{1,0},{2,3},{3,2},{4,5},{5,4},{6,7},{7,6},{8,9},{9,8},{10,11... | collective-permute-start | bytes 393224 | tf_op jit(solution)/shard_map/ppermute | solution.py:384
  22.6 1.9 %collective-permute-start.13 = (f32[256,128]{1,0:T(8,128)S(1)}, f32[256,128]{1,0:T(8,128)S(1)}, u32[]{:S(2)}, u32[]{:S(2)}) collective-permute-start(f32[256,128]{1,0:T(8,128)S(1)} %second_maps.1.own_ref), channel_id=1, source_target_pairs={{1,2},{2,1},{3,4},{4,3},{5,6},{6,5},{7,8},{8,7},{9,10},{10,9},{11,... | collective-permute-start | bytes 393224 | tf_op jit(solution)/shard_map/ppermute | solution.py:384
  24.5 5.8 %collective-permute-done.13.other_ref = f32[256,128]{1,0:T(8,128)S(1)} collective-permute-done((f32[256,128]{1,0:T(8,128)S(1)}, f32[256,128]{1,0:T(8,128)S(1)}, u32[]{:S(2)}, u32[]{:S(2)}) %collective-permute-start.13) | collective-permute-done | bytes 131104 | tf_op jit(solution)/shard_map/ppermute | solution.py:384
  30.3 0.8 %product.1 = f32[256,128]{1,0:T(8,128)} custom-call(f32[256,128]{1,0:T(8,128)S(1)} %second_maps.1.own_ref, f32[256,128]{1,0:T(8,128)S(1)} %collective-permute-done.12.mate_ref, f32[256,128]{1,0:T(8,128)S(1)} %collective-permute-done.13.other_ref), custom_call_target="tpu_custom_call" | custom-call | tf_op jit(solution)/shard_map/product/pallas_call | solution.py:468
  (14 shorter events, 0.0 us)
Async XLA Ops:
  0.0 13.7 %copy-start = (bf16[256,768]{1,0:T(8,128)(2,1)S(1)}, bf16[256,768]{1,0:T(8,128)(2,1)}, u32[]{:S(2)}) copy-start(bf16[256,768]{1,0:T(8,128)(2,1)} %constant.13.clone.z_hbm.refs_1_.z_ref) | copy-start | bytes 1179652
  0.0 13.7 %copy-start.6 = (bf16[256,256]{1,0:T(8,128)(2,1)S(1)}, bf16[256,256]{1,0:T(8,128)(2,1)}, u32[]{:S(2)}) copy-start(bf16[256,256]{1,0:T(8,128)(2,1)} %constant.12.clone.y_hbm.refs_0_) | copy-start | bytes 393220
  0.0 4.5 %collective-permute-start = (bf16[16,32,128]{2,1,0:T(8,128)(2,1)}, bf16[16,32,128]{2,1,0:T(8,128)(2,1)S(1)}, u32[]{:S(2)}, u32[]{:S(2)}) collective-permute-start(bf16[16,32,128]{2,1,0:T(8,128)(2,1)} %own_ref.1), channel_id=1, source_target_pairs={{0,1},{1,0},{2,3},{3,2},{4,5},{5,4},{6,7},{7,6},{8,9},{9,8},{10,11... | collective-permute-start | bytes 393224 | tf_op jit(solution)/shard_map/ppermute | solution.py:384
  0.7 7.0 %collective-permute-start.9 = (bf16[16,32,128]{2,1,0:T(8,128)(2,1)}, bf16[16,32,128]{2,1,0:T(8,128)(2,1)S(1)}, u32[]{:S(2)}, u32[]{:S(2)}) collective-permute-start(bf16[16,32,128]{2,1,0:T(8,128)(2,1)} %tile_hbm), channel_id=1, source_target_pairs={{2,0},{4,2},{6,4},{8,6},{10,8},{12,10},{14,12},{15,14},{1,3},{3,5}... | collective-permute-start | bytes 393224 | tf_op jit(solution)/shard_map/ppermute | solution.py:384
  1.9 5.9 %collective-permute-start.10 = (bf16[16,32,128]{2,1,0:T(8,128)(2,1)}, bf16[16,32,128]{2,1,0:T(8,128)(2,1)S(1)}, u32[]{:S(2)}, u32[]{:S(2)}) collective-permute-start(bf16[16,32,128]{2,1,0:T(8,128)(2,1)} %tile_hbm), channel_id=1, source_target_pairs={{0,1},{1,0},{2,3},{3,2},{4,5},{5,4},{6,7},{7,6},{8,9},{9,8},{10,11... | collective-permute-start | bytes 393224 | tf_op jit(solution)/shard_map/ppermute | solution.py:384
  2.2 6.7 %collective-permute-start.1 = (bf16[16,32,128]{2,1,0:T(8,128)(2,1)}, bf16[16,32,128]{2,1,0:T(8,128)(2,1)S(1)}, u32[]{:S(2)}, u32[]{:S(2)}) collective-permute-start(bf16[16,32,128]{2,1,0:T(8,128)(2,1)} %own_ref.1), channel_id=1, source_target_pairs={{2,0},{4,2},{6,4},{8,6},{10,8},{12,10},{14,12},{15,14},{1,3},{3,5}... | collective-permute-start | bytes 393224 | tf_op jit(solution)/shard_map/ppermute | solution.py:384
  3.2 8.4 %collective-permute-start.3 = (bf16[16,32,128]{2,1,0:T(8,128)(2,1)}, bf16[16,32,128]{2,1,0:T(8,128)(2,1)S(1)}, u32[]{:S(2)}, u32[]{:S(2)}) collective-permute-start(bf16[16,32,128]{2,1,0:T(8,128)(2,1)} %own_ref.1), channel_id=1, source_target_pairs={{4,0},{6,2},{8,4},{10,6},{12,8},{14,10},{15,14},{13,12},{1,5},{3,7... | collective-permute-start | bytes 393224 | tf_op jit(solution)/shard_map/ppermute | solution.py:384
  4.5 7.1 %collective-permute-start.2 = (bf16[16,32,128]{2,1,0:T(8,128)(2,1)S(1)}, bf16[16,32,128]{2,1,0:T(8,128)(2,1)S(1)}, u32[]{:S(2)}, u32[]{:S(2)}) collective-permute-start(bf16[16,32,128]{2,1,0:T(8,128)(2,1)S(1)} %collective-permute-done.mate_ref), channel_id=1, source_target_pairs={{2,0},{4,2},{6,4},{8,6},{10,8},{12,10},{14,12},{15,14},{1,3},{3,5}... | collective-permute-start | bytes 393224 | tf_op jit(solution)/shard_map/ppermute | solution.py:384
  7.7 5.2 %collective-permute-start.4 = (bf16[16,32,128]{2,1,0:T(8,128)(2,1)S(1)}, bf16[16,32,128]{2,1,0:T(8,128)(2,1)S(1)}, u32[]{:S(2)}, u32[]{:S(2)}) collective-permute-start(bf16[16,32,128]{2,1,0:T(8,128)(2,1)S(1)} %collective-permute-done.mate_ref), channel_id=1, source_target_pairs={{4,0},{6,2},{8,4},{10,6},{12,8},{14,10},{15,14},{13,12},{1,5},{3,7... | collective-permute-start | bytes 393224 | tf_op jit(solution)/shard_map/ppermute | solution.py:384
  7.7 7.0 %copy-start.1 = (bf16[128,768]{1,0:T(8,128)(2,1)S(1)}, bf16[128,768]{1,0:T(8,128)(2,1)}, u32[]{:S(2)}) copy-start(bf16[128,768]{1,0:T(8,128)(2,1)} %constant.16.clone.z_inverse_ref) | copy-start | bytes 589828
  7.7 6.9 %copy-start.2 = (bf16[768,128]{1,0:T(8,128)(2,1)S(1)}, bf16[768,128]{1,0:T(8,128)(2,1)}, u32[]{:S(2)}) copy-start(bf16[768,128]{1,0:T(8,128)(2,1)} %constant.17.clone.y_inverse_ref) | copy-start | bytes 589828
  7.8 6.9 %copy-start.3 = (bf16[16,32,128]{2,1,0:T(8,128)(2,1)S(1)}, bf16[16,32,128]{2,1,0:T(8,128)(2,1)}, u32[]{:S(2)}) copy-start(bf16[16,32,128]{2,1,0:T(8,128)(2,1)} %own_ref.1) | copy-start | bytes 393220
  7.8 6.9 %copy-start.4 = (bf16[256,256]{1,0:T(8,128)(2,1)S(1)}, bf16[256,256]{1,0:T(8,128)(2,1)}, u32[]{:S(2)}) copy-start(bf16[256,256]{1,0:T(8,128)(2,1)} %constant.14.clone.y_high_ref) | copy-start | bytes 393220
  7.8 6.9 %copy-start.5 = (bf16[256,256]{1,0:T(8,128)(2,1)S(1)}, bf16[256,256]{1,0:T(8,128)(2,1)}, u32[]{:S(2)}) copy-start(bf16[256,256]{1,0:T(8,128)(2,1)} %constant.15.clone.y_low_ref) | copy-start | bytes 393220
  7.8 5.9 %collective-permute-start.11 = (bf16[16,32,128]{2,1,0:T(8,128)(2,1)S(1)}, bf16[16,32,128]{2,1,0:T(8,128)(2,1)S(1)}, u32[]{:S(2)}, u32[]{:S(2)}) collective-permute-start(bf16[16,32,128]{2,1,0:T(8,128)(2,1)S(1)} %collective-permute-done.9), channel_id=1, source_target_pairs={{0,1},{1,0},{2,3},{3,2},{4,5},{5,4},{6,7},{7,6},{8,9},{9,8},{10,11... | collective-permute-start | bytes 393224 | tf_op jit(solution)/shard_map/ppermute | solution.py:384
  8.9 5.5 %collective-permute-start.5 = (bf16[16,32,128]{2,1,0:T(8,128)(2,1)S(1)}, bf16[16,32,128]{2,1,0:T(8,128)(2,1)S(1)}, u32[]{:S(2)}, u32[]{:S(2)}) collective-permute-start(bf16[16,32,128]{2,1,0:T(8,128)(2,1)S(1)} %collective-permute-done.1.near_own_ref), channel_id=1, source_target_pairs={{0,1},{1,0},{2,3},{3,2},{4,5},{5,4},{6,7},{7,6},{8,9},{9,8},{10,11... | collective-permute-start | bytes 393224 | tf_op jit(solution)/shard_map/ppermute | solution.py:384
  11.5 2.8 %collective-permute-start.7 = (bf16[16,32,128]{2,1,0:T(8,128)(2,1)S(1)}, bf16[16,32,128]{2,1,0:T(8,128)(2,1)S(1)}, u32[]{:S(2)}, u32[]{:S(2)}) collective-permute-start(bf16[16,32,128]{2,1,0:T(8,128)(2,1)S(1)} %collective-permute-done.3.far_own_ref), channel_id=1, source_target_pairs={{0,1},{1,0},{2,3},{3,2},{4,5},{5,4},{6,7},{7,6},{8,9},{9,8},{10,11... | collective-permute-start | bytes 393224 | tf_op jit(solution)/shard_map/ppermute | solution.py:384
  11.6 2.8 %collective-permute-start.6 = (bf16[16,32,128]{2,1,0:T(8,128)(2,1)S(1)}, bf16[16,32,128]{2,1,0:T(8,128)(2,1)S(1)}, u32[]{:S(2)}, u32[]{:S(2)}) collective-permute-start(bf16[16,32,128]{2,1,0:T(8,128)(2,1)S(1)} %collective-permute-done.2.near_mate_ref), channel_id=1, source_target_pairs={{0,1},{1,0},{2,3},{3,2},{4,5},{5,4},{6,7},{7,6},{8,9},{9,8},{10,11... | collective-permute-start | bytes 393224 | tf_op jit(solution)/shard_map/ppermute | solution.py:384
  13.0 1.7 %collective-permute-start.8 = (bf16[16,32,128]{2,1,0:T(8,128)(2,1)S(1)}, bf16[16,32,128]{2,1,0:T(8,128)(2,1)S(1)}, u32[]{:S(2)}, u32[]{:S(2)}) collective-permute-start(bf16[16,32,128]{2,1,0:T(8,128)(2,1)S(1)} %collective-permute-done.4.far_mate_ref), channel_id=1, source_target_pairs={{0,1},{1,0},{2,3},{3,2},{4,5},{5,4},{6,7},{7,6},{8,9},{9,8},{10,11... | collective-permute-start | bytes 393224 | tf_op jit(solution)/shard_map/ppermute | solution.py:384
  22.2 2.4 %collective-permute-start.12 = (f32[256,128]{1,0:T(8,128)S(1)}, f32[256,128]{1,0:T(8,128)S(1)}, u32[]{:S(2)}, u32[]{:S(2)}) collective-permute-start(f32[256,128]{1,0:T(8,128)S(1)} %second_maps.1.own_ref), channel_id=1, source_target_pairs={{0,1},{1,0},{2,3},{3,2},{4,5},{5,4},{6,7},{7,6},{8,9},{9,8},{10,11... | collective-permute-start | bytes 393224 | tf_op jit(solution)/shard_map/ppermute | solution.py:384
  22.6 7.7 %collective-permute-start.13 = (f32[256,128]{1,0:T(8,128)S(1)}, f32[256,128]{1,0:T(8,128)S(1)}, u32[]{:S(2)}, u32[]{:S(2)}) collective-permute-start(f32[256,128]{1,0:T(8,128)S(1)} %second_maps.1.own_ref), channel_id=1, source_target_pairs={{1,2},{2,1},{3,4},{4,3},{5,6},{6,5},{7,8},{8,7},{9,10},{10,9},{11,... | collective-permute-start | bytes 393224 | tf_op jit(solution)/shard_map/ppermute | solution.py:384

commit v3 on v2

--- a/solution.py
+++ b/solution.py
@@ -40,16 +40,6 @@
     return real, imag
 
 
-def first_y_table():
-    real, imag = y_columns()
-    table = np.zeros((NY + STEP, 2, WY, HALF))
-    for j in range(WY):
-        table[j * STEP : j * STEP + WIN, 0, j] = real
-        table[j * STEP : j * STEP + WIN, 1, j] = imag
-    high, low = split_table(table[:NY].reshape(NY, 2 * LANES))
-    return np.concatenate([high, low], 0)
-
-
 def second_y_table():
     real, imag = y_columns()
     table = np.zeros((WY, WIN, 2, WY, HALF))
@@ -62,13 +52,6 @@
 def three_terms(table, axis):
     high, low = split_table(table)
     return np.concatenate([high, high, low], axis)
-
-
-def z_table():
-    angles = phase(np.outer(Z_ORDER, np.arange(ZS)))
-    four = np.eye(4)
-    cosine, sine = np.kron(four, np.cos(angles)), np.kron(four, np.sin(angles))
-    return three_terms(np.block([[cosine, sine], [-sine, cosine]]), 1)
 
 
 def z_inverse_table():
@@ -86,7 +69,7 @@
     imag[0] = 1.0 - 2.0 * (shifts % 2)
     eight = np.eye(WY)
     table = np.concatenate([np.kron(eight, real), np.kron(eight, imag)], 0)
-    return three_terms(table / (WIN * WIN), 0)
+    return three_terms(table / WIN**3, 0)
 
 
 def dot(a, b):
@@ -145,18 +128,106 @@
     return energy
 
 
-def finish_stage(energy, block):
-    rows, zero_lane = positions((8, LANES))
-    is_mean = zero_lane & (rows == 0)
-    means = jnp.where(is_mean, jnp.sum(block, 0) * (1.0 / WIN), 0.0)
-    centred = block - means[None]
-    total = energy + jnp.sum(jnp.where(is_mean[None], centred * centred, 0.0), 0)
-    total = jnp.broadcast_to(jnp.sum(total, 0, keepdims=True), (8, LANES))
+def times(value, turn):
+    real, imag = value
+    eighth = round(8 * turn) % 8
+    if abs(8 * turn - round(8 * turn)) > 1e-9:
+        cosine, sine = math.cos(2.0 * math.pi * turn), math.sin(2.0 * math.pi * turn)
+        return real * cosine - imag * sine, real * sine + imag * cosine
+    if eighth % 2:
+        half = math.sqrt(0.5)
+        real, imag = half * (real - imag), half * (real + imag)
+    quarter = eighth // 2
+    if quarter == 1:
+        return -imag, real
+    if quarter == 2:
+        return -real, -imag
+    if quarter == 3:
+        return imag, -real
+    return real, imag
+
+
+def plus(a, b):
+    return a[0] + b[0], a[1] + b[1]
+
+
+def minus(a, b):
+    return a[0] - b[0], a[1] - b[1]
+
+
+def fourier(values, sign):
+    count = len(values)
+    if count == 1:
+        return values
+    even, odd = fourier(values[0::2], sign), fourier(values[1::2], sign)
+    odd = [times(value, sign * k / count) for k, value in enumerate(odd)]
+    return [plus(a, b) for a, b in zip(even, odd)] + [minus(a, b) for a, b in zip(even, odd)]
+
+
+def x_fourier(values):
+    parts = [fourier([values(x + 8 * k) for k in range(4)], -1) for x in range(8)]
+    parts = [[times(v, -x * b / WIN) for b, v in enumerate(part)] for x, part in enumerate(parts)]
+    for b in range(4):
+        yield fourier([parts[x][b] for x in range(8)], -1)
+
+
+def special_lines(real_0, imag_0, real_16, imag_16):
+    lane = lax.broadcasted_iota(jnp.int32, (WIN, LANES), 1) % HALF
+    lines = jnp.where(lane == 0, real_0, 0.0)
+    for n, line in enumerate((imag_0, real_16, imag_16)):
+        lines = jnp.where(lane == n + 1, pltpu.roll(line, n + 1, 1), lines)
+    means = jnp.sum(lines, 0, keepdims=True) * (1.0 / WIN)
+    lines = jnp.where(lane == 0, lines - means, lines)
+    return lines, jnp.sum(jnp.where(lane == 0, lines * lines, 0.0), 0, keepdims=True)
+
+
+def variance(energy, mean_energy):
+    total = jnp.sum(energy, 0, keepdims=True) + mean_energy
+    total = jnp.broadcast_to(total, (8, LANES))
     group_row = lax.broadcasted_iota(jnp.int32, (LANES, LANES), 0) // HALF
     group_col = lax.broadcasted_iota(jnp.int32, (LANES, LANES), 1) // HALF
     same = (group_row == group_col).astype(F32)
     summed = jnp.dot(total, same, precision=lax.Precision.HIGHEST, preferred_element_type=F32)
-    return centred, summed * (1.0 / (ZS * WIN * WIN * ZS * WIN))
+    return summed * (1.0 / (ZS * WIN * WIN * ZS * WIN))
+
+
+def first_tables(y_ref, z_ref):
+    def halves(ref, rows, cols, value):
+        high = value.astype(BF16)
+        low = (value - high.astype(F32)).astype(BF16)
+        for n, part in enumerate((high, low) if cols is None else (high, high, low)):
+            if cols is None:
+                ref[n * NY : (n + 1) * NY, rows] = part
+            else:
+                start = n * 2 * LANES
+                ref[rows, start + cols.start : start + cols.stop] = part
+
+    row = lax.broadcasted_iota(jnp.int32, (WIN, LANES), 0)
+    lane = lax.broadcasted_iota(jnp.int32, (WIN, LANES), 1)
+    unit = 2.0 * math.pi / WIN
+
+    frequency = lane % HALF
+    turns = (frequency * (row + STEP * (lane // HALF))) % WIN
+    cosine = jnp.cos(turns.astype(F32) * unit)
+    sine = jnp.where(frequency == 0, 2.0 * (row % 2).astype(F32) - 1.0, jnp.sin(turns.astype(F32) * unit))
+    y = lax.broadcasted_iota(jnp.int32, (NY, LANES), 0)
+    offset = y - STEP * (lax.broadcasted_iota(jnp.int32, (NY, LANES), 1) // HALF)
+    inside = (offset >= 0) & (offset < WIN)
+    for n, part in enumerate((cosine, -sine)):
+        tall = jnp.concatenate([part] * (NY // WIN), 0)
+        halves(y_ref, slice(n * LANES, (n + 1) * LANES), None, jnp.where(inside, tall, 0.0))
+
+    order = jnp.where(row <= HALF, row, WIN + HALF - row)
+    turns = (order * (lane % ZS)) % WIN
+    cosine, sine = jnp.cos(turns.astype(F32) * unit), jnp.sin(turns.astype(F32) * unit)
+    y_lane = lax.broadcasted_iota(jnp.int32, (4 * ZS, LANES), 1)
+    same = lax.broadcasted_iota(jnp.int32, (4 * ZS, LANES), 0) // ZS == y_lane // ZS
+    blocks = [jnp.where(same, jnp.concatenate([v] * 4, 0), 0.0) for v in (cosine, sine)]
+    upper, lower = slice(0, LANES), slice(LANES, 2 * LANES)
+    halves(z_ref, upper, upper, blocks[0])
+    halves(z_ref, upper, lower, blocks[1])
+    halves(z_ref, lower, upper, -blocks[1])
+    halves(z_ref, lower, lower, blocks[0])
 
 
 def first_stage(tile, y_ref, z_ref, real_ref, imag_ref, energy_ref):
@@ -171,34 +242,76 @@
     energy_ref[...] = energy
 
 
-def low_kernel(tile_hbm, y_hbm, z_hbm, shift_x_hbm, shift_y_hbm, *refs):
-    *outs, shift_x_ref, shift_y_ref, tile_ref, y_ref, z_ref, sems = refs
+def low_kernel(
+    own_hbm,
+    shift_x_hbm,
+    shift_y_hbm,
+    real_ref,
+    imag_ref,
+    energy_ref,
+    y_ref,
+    z_ref,
+    shift_x_ref,
+    shift_y_ref,
+    own_ref,
+    sems,
+):
     copies = [
-        pltpu.make_async_copy(source, target, sems.at[n])
-        for n, (source, target) in enumerate(
-            (
-                (z_hbm, z_ref),
-                (y_hbm, y_ref),
-                (tile_hbm, tile_ref),
-                (shift_x_hbm, shift_x_ref),
-                (shift_y_hbm, shift_y_ref),
-            )
-        )
+        pltpu.make_async_copy(own_hbm, own_ref, sems.at[0]),
+        pltpu.make_async_copy(shift_x_hbm, shift_x_ref, sems.at[1]),
+        pltpu.make_async_copy(shift_y_hbm, shift_y_ref, sems.at[2]),
     ]
     for copy in copies:
         copy.start()
+    first_tables(y_ref, z_ref)
     for copy in copies:
         copy.wait()
-    first_stage(tile_ref[...], y_ref, z_ref, *outs)
-
-
-def high_kernel(even_ref, odd_ref, *refs):
+    first_stage(own_ref[...], y_ref, z_ref, real_ref, imag_ref, energy_ref)
+
+
+def high_kernel(
+    next_ref,
+    y_ref,
+    z_ref,
+    low_real_ref,
+    low_imag_ref,
+    low_energy_ref,
+    real_ref,
+    imag_ref,
+    lines_ref,
+    var_ref,
+    high_real_ref,
+    high_imag_ref,
+    high_energy_ref,
+):
     position = lax.axis_index("gx")
     inside = position < lax.axis_size("gx") - 1
-    odd = position % 2
-    use_even = jnp.where(inside & (odd == 0), 1.0, 0.0).astype(BF16)
-    use_odd = jnp.where(inside & (odd == 1), 1.0, 0.0).astype(BF16)
-    first_stage(even_ref[...] * use_even + odd_ref[...] * use_odd, *refs)
+    keep = jnp.where(inside, 1.0, 0.0).astype(BF16)
+    tile = next_ref[...] * keep
+    first_stage(tile, y_ref, z_ref, high_real_ref, high_imag_ref, high_energy_ref)
+
+    def eight_slots(block, carry):
+        where_z = pl.ds(pl.multiple_of(block * 8, 8), 8)
+
+        def value(x):
+            if x < STEP:
+                return low_real_ref[x, where_z], low_imag_ref[x, where_z]
+            return high_real_ref[x - STEP, where_z], high_imag_ref[x - STEP, where_z]
+
+        for b, column in enumerate(x_fourier(value)):
+            for a, (real, imag) in enumerate(column):
+                real_ref[8 * b + a, where_z] = real
+                imag_ref[8 * b + a, where_z] = imag
+        return carry
+
+    lax.fori_loop(0, ZS // 8, eight_slots, 0)
+    lines = [
+        jnp.concatenate([low[:, slot], high[:, slot]], 0)
+        for slot in (0, HALF)
+        for low, high in ((low_real_ref, high_real_ref), (low_imag_ref, high_imag_ref))
+    ]
+    lines_ref[...], mean_energy = special_lines(*lines)
+    var_ref[...] = variance(low_energy_ref[...] + high_energy_ref[...], mean_energy)
 
 
 def second_kernel(
@@ -214,12 +327,10 @@
     mate_near_mate_ref,
     mate_far_own_ref,
     mate_far_mate_ref,
-    low_real_ref,
-    low_imag_ref,
-    low_energy_ref,
-    high_real_ref,
-    high_imag_ref,
-    high_energy_ref,
+    first_real_ref,
+    first_imag_ref,
+    first_lines_ref,
+    first_var_ref,
     y_high_ref,
     y_low_ref,
     z_ref,
@@ -231,6 +342,7 @@
     imag_ref,
     cross_real_ref,
     cross_imag_ref,
+    twice_ref,
 ):
     position = lax.axis_index("gx")
     tiles = lax.axis_size("gx")
@@ -286,46 +398,54 @@
         )
 
     energy = lax.fori_loop(0, WIN // 8, eight_x, jnp.zeros((8, LANES), F32))
-    real_ref[:, 0:8], second_var = finish_stage(energy, real_ref[:, 0:8])
-    first_means = jnp.concatenate([low_real_ref[:, 0:8], high_real_ref[:, 0:8]], 0)
-    _, first_var = finish_stage(low_energy_ref[...] + high_energy_ref[...], first_means)
-
-    rows, zero_lane = positions((8, LANES))
-    special = zero_lane & (rows == 0)
-
     def eight_slots(block, carry):
         where_z = pl.ds(pl.multiple_of(block * 8, 8), 8)
-        alone = special & (block % 2 == 0)
-        for base in range(0, SR, 8):
-            rr = [None] * 8
-            ii = [None] * 8
-            ri = [None] * 8
-            for x in range(WIN):
-                fr_ref = low_real_ref if x < STEP else high_real_ref
-                fi_ref = low_imag_ref if x < STEP else high_imag_ref
-                fr = fr_ref[x % STEP, where_z]
-                fi = fi_ref[x % STEP, where_z]
-                for s in range(8):
-                    at = (x + base + s - SR // 2) % WIN
-                    gr = real_ref[at, where_z]
-                    gi = imag_ref[at, where_z]
-                    if x == 0:
-                        rr[s], ii[s], ri[s] = fr * gr, fi * gi, fr * gi - fi * gr
-                    else:
-                        rr[s] = rr[s] + fr * gr
-                        ii[s] = ii[s] + fi * gi
-                        ri[s] = ri[s] + fr * gi - fi * gr
-            for s in range(8):
-                cross_real_ref[base + s, where_z] = jnp.where(alone, rr[s], rr[s] + ii[s])
-                cross_imag_ref[base + s, where_z] = jnp.where(alone, ii[s], ri[s])
+
+        def value(x):
+            return real_ref[x, where_z], imag_ref[x, where_z]
+
+        columns = []
+        for b, column in enumerate(x_fourier(value)):
+            cross = []
+            for a, (gr, gi) in enumerate(column):
+                fr, fi = first_real_ref[8 * b + a, where_z], first_imag_ref[8 * b + a, where_z]
+                cross.append((fr * gr + fi * gi, fr * gi - fi * gr))
+            column = fourier(cross, 1)
+            columns.append([times(v, b * s / WIN) for s, v in enumerate(column)])
+        for s in range(8):
+            u = [column[s] for column in columns]
+            even, odd = plus(u[0], u[2]), plus(u[1], u[3])
+            here = plus(even, odd)
+            even, odd = minus(u[0], u[2]), times(minus(u[1], u[3]), -0.25)
+            back = plus(even, odd)
+            cross_real_ref[8 + s, where_z], cross_imag_ref[8 + s, where_z] = here
+            cross_real_ref[s, where_z], cross_imag_ref[s, where_z] = back
         return carry
 
     lax.fori_loop(0, ZS // 8, eight_slots, 0)
 
+    lines, mean_energy = special_lines(
+        real_ref[:, 0], imag_ref[:, 0], real_ref[:, HALF], imag_ref[:, HALF]
+    )
+    second_var = variance(energy, mean_energy)
+    twice_ref[0:WIN] = lines
+    twice_ref[WIN : 2 * WIN] = lines
+    first_lines = first_lines_ref[...] * float(WIN)
+    sums = []
+    for s in range(SR):
+        shift = (s - SR // 2) % WIN
+        sums.append(
+            jnp.sum(first_lines * twice_ref[shift : shift + WIN], 0, keepdims=True)
+        )
+    sums = jnp.concatenate(sums, 0)
+    alone = [sums] + [pltpu.roll(sums, LANES - n, 1) for n in range(1, 4)]
+    alone = [v.reshape(SR, 1, LANES) for v in alone]
+
     rows, zero_lane = positions((4, 8, LANES))
+    special = zero_lane & (rows == 0)
     mixed = [zero_lane & (rows != 0), zero_lane]
     scale = 1.0 / (
-        WIN**1.5 * (jnp.sqrt(first_var + 1e-6) * jnp.sqrt(second_var + 1e-6))
+        WIN**1.5 * (jnp.sqrt(first_var_ref[...] + 1e-6) * jnp.sqrt(second_var + 1e-6))
     )
     for start in range(0, SR, 8):
         columns = []
@@ -339,6 +459,11 @@
                 ur, ui = cross_real_ref[where_x, up], cross_imag_ref[where_x, up]
                 dr, di = cross_real_ref[where_x, down], cross_imag_ref[where_x, down]
                 mask = mixed[group]
+                if group == 0:
+                    ur, ui, dr, di = (
+                        jnp.where(special, line[where_x], v)
+                        for line, v in zip(alone, (ur, ui, dr, di))
+                    )
                 real[group] = jnp.where(mask, ur - di, ur)
                 imag[group] = jnp.where(mask, ui + dr, ui)
                 real[group + 2] = jnp.where(mask, ur + di, dr)
@@ -391,20 +516,25 @@
     far += [(2 * q - 3, 2 * q + 1) for q in range(2, chips)] + [(0, 1), (2, 3)]
     across = [(i, i + 1 if i % 2 else i - 1) for i in range(1, last)] + [(0, 0), (last, last)]
 
-    near_first = send(first_volume, near)
+    next_tile = send(first_volume, [((i + 1) % size, i) for i in range(size)])
     near_own = send(second_volume, near)
     mate_tile = send(second_volume, mates)
+    far_own = send(second_volume, far)
+    mate_first = send(first_volume, mates)
+    low_tile = first_volume
     low_tile, mate_tile = lax.optimization_barrier((first_volume, mate_tile))
     near_mate = send(mate_tile, near)
-    far_own = send(second_volume, far)
     far_mate = send(mate_tile, far)
-    mate_first = send(first_volume, mates)
-
-    tables = (first_y_table(), z_table())
-    spectrum = jax.ShapeDtypeStruct((STEP, ZS, LANES), F32)
-
-    def first_spectra(kernel, specs, scratch, more_out, *operands):
-        outs = (spectrum, spectrum, jax.ShapeDtypeStruct((8, LANES), F32), *more_out)
+
+    half = jax.ShapeDtypeStruct((STEP, ZS, LANES), F32)
+    whole = jax.ShapeDtypeStruct((WIN, ZS, LANES), F32)
+    lines = jax.ShapeDtypeStruct((WIN, LANES), F32)
+    row = jax.ShapeDtypeStruct((8, LANES), F32)
+    y_table = jax.ShapeDtypeStruct((2 * NY, 2 * LANES), BF16)
+    z_table = jax.ShapeDtypeStruct((2 * LANES, 6 * LANES), BF16)
+    shifts = [jax.ShapeDtypeStruct(v.shape, v.dtype) for v in (shift_x, shift_y)]
+
+    def first_spectra(kernel, specs, outs, scratch, *operands):
         return pl.pallas_call(
             kernel,
             out_shape=outs,
@@ -418,25 +548,35 @@
             name="first_spectra",
         )(*operands)
 
-    scratch = [pltpu.VMEM(v.shape, BF16) for v in (first_volume, *tables)]
-    scratch.append(pltpu.SemaphoreType.DMA((5,)))
-    in_hbm = [
-        pltpu.with_memory_space_constraint(jnp.asarray(v), pltpu.HBM)
-        for v in (low_tile, *tables, shift_x, shift_y)
-    ]
-    shifts = [jax.ShapeDtypeStruct(v.shape, v.dtype) for v in (shift_x, shift_y)]
-    *low_part, shift_x, shift_y = first_spectra(low_kernel, [HBM] * 5, scratch, shifts, *in_hbm)
-    near_first, *low_part = lax.optimization_barrier((near_first, *low_part))
-    mate_near_first = send(near_first, mates)
+    *low_part, y_table, z_table, shift_x, shift_y = first_spectra(
+        low_kernel,
+        [HBM] * 3,
+        (half, half, row, y_table, z_table, *shifts),
+        [pltpu.VMEM(first_volume.shape, BF16), pltpu.SemaphoreType.DMA((3,))],
+        *(
+            pltpu.with_memory_space_constraint(v, pltpu.HBM)
+            for v in (first_volume, shift_x, shift_y)
+        ),
+    )
+    near_own, *low_part = lax.optimization_barrier((near_own, *low_part))
+    first_part = first_spectra(
+        high_kernel,
+        [VMEM] * 6,
+        (whole, whole, lines, row),
+        [pltpu.VMEM(v.shape, F32) for v in (half, half, row)],
+        next_tile,
+        y_table,
+        z_table,
+        *low_part,
+    )
     side = (near_own, near_mate, far_own, far_mate)
     mate_side = [send(tile, mates) for tile in side]
-    high_part = first_spectra(high_kernel, [VMEM] * 4, [], [], mate_first, mate_near_first, *tables)
 
     y_high, y_low = second_y_table()
     maps = pl.pallas_call(
         second_kernel,
         out_shape=jax.ShapeDtypeStruct((SR * SR, LANES), F32),
-        in_specs=[VMEM] * 23,
+        in_specs=[VMEM] * 21,
         out_specs=VMEM,
         scratch_shapes=[
             pltpu.VMEM((10 * STEP, ZS, NY), BF16),
@@ -444,6 +584,7 @@
             pltpu.VMEM((WIN, ZS, LANES), F32),
             pltpu.VMEM((SR, ZS, LANES), F32),
             pltpu.VMEM((SR, ZS, LANES), F32),
+            pltpu.VMEM((2 * WIN, LANES), F32),
         ],
         compiler_params=params(),
         name="second_maps",
@@ -454,11 +595,10 @@
         mate_tile,
         *side,
         *mate_side,
-        *low_part,
-        *high_part,
+        *first_part,
         y_high,
         y_low,
-        z_table(),
+        z_table,
         z_inverse_table(),
         y_inverse_table(),
     )

time: 31.2 us -> 27.7 us (0.89)
  Pallas kernels: 10.6 us -> 8.78 us
  starting transfers between devices: 14.2 us -> 12.7 us
    pallas_call x1, Pallas kernels: 7.43 us -> 4.77 us  [local(): pl.pallas_call(second_kernel, out_shape=jax.ShapeDtypeStruct((SR * SR, LA...]
    ppermute x14 -> x12, starting transfers between devices: 14.2 us -> 12.7 us  [send(): return lax.ppermute(value, 'gx', pairs)]
    pallas_call x2, Pallas kernels: 2.38 us -> 3.22 us  [first_spectra(): pl.pallas_call(kernel, out_shape=outs, in_specs=specs, out_specs=(VMEM,)...]
    ppermute x14 -> x12, waiting for transfers between devices: 6.1 us -> 5.91 us  [send(): return lax.ppermute(value, 'gx', pairs)]
  transfers between devices with their start and end apart: 14 -> 12, of which waited for: 2 -> 2; matrix products, arithmetic and copies ran while one was open for 0% -> 0% of each run, Pallas kernels for 8% -> 12%
where the time goes in v3:
time: 27.7 us; the launch traced here: 27.5 us
  starting transfers between devices  12.7 us (46%)
  Pallas kernels  8.78 us (32%)
  waiting for transfers between devices  5.91 us (21%)
    ppermute x12, starting transfers between devices, send(): return lax.ppermute(value, 'gx', pairs)  12.7 us
    ppermute x12, waiting for transfers between devices, send(): return lax.ppermute(value, 'gx', pairs)  5.91 us
    pallas_call x1, Pallas kernels, local(): pl.pallas_call(second_kernel, out_shape=jax.ShapeDtypeStruct((SR * SR, LA...  4.77 us
    pallas_call x2, Pallas kernels, first_spectra(): pl.pallas_call(kernel, out_shape=outs, in_specs=specs, out_specs=(VMEM,)...  3.22 us
    pallas_call x1, Pallas kernels, local(): pl.pallas_call(product_kernel, out_shape=jax.ShapeDtypeStruct((SR * SR, L...  0.79 us
  transfers between devices with their start and end apart: 12, of which 2 were waited for; matrix products, arithmetic and copies ran while one was open for 0% of the time, Pallas kernels for 12%

profile of v3, /device:TPU:9, one launch (start us, length us, event | category | flops | bytes accessed | tf_op | source)
XLA Modules:
  0.0 27.5 jit_solution(13378511194356839138)
XLA Ops:
  0.0 0.7 %collective-permute-start = (bf16[16,32,128]{2,1,0:T(8,128)(2,1)}, bf16[16,32,128]{2,1,0:T(8,128)(2,1)S(1)}, u32[]{:S(2)}, u32[]{:S(2)}) collective-permute-start(bf16[16,32,128]{2,1,0:T(8,128)(2,1)} %own_ref.1), channel_id=1, source_target_pairs={{0,1},{1,0},{2,3},{3,2},{4,5},{5,4},{6,7},{7,6},{8,9},{9,8},{10,11... | collective-permute-start | bytes 393224 | tf_op jit(solution)/shard_map/ppermute | solution.py:509
  0.7 1.2 %collective-permute-start.1 = (bf16[16,32,128]{2,1,0:T(8,128)(2,1)}, bf16[16,32,128]{2,1,0:T(8,128)(2,1)S(1)}, u32[]{:S(2)}, u32[]{:S(2)}) collective-permute-start(bf16[16,32,128]{2,1,0:T(8,128)(2,1)} %own_ref.1), channel_id=1, source_target_pairs={{2,0},{4,2},{6,4},{8,6},{10,8},{12,10},{14,12},{15,14},{1,3},{3,5}... | collective-permute-start | bytes 393224 | tf_op jit(solution)/shard_map/ppermute | solution.py:509
  1.9 1.3 %collective-permute-start.3 = (bf16[16,32,128]{2,1,0:T(8,128)(2,1)}, bf16[16,32,128]{2,1,0:T(8,128)(2,1)S(1)}, u32[]{:S(2)}, u32[]{:S(2)}) collective-permute-start(bf16[16,32,128]{2,1,0:T(8,128)(2,1)} %own_ref.1), channel_id=1, source_target_pairs={{4,0},{6,2},{8,4},{10,6},{12,8},{14,10},{15,14},{13,12},{1,5},{3,7... | collective-permute-start | bytes 393224 | tf_op jit(solution)/shard_map/ppermute | solution.py:509
  3.2 0.0 collective-permute-start.9
  3.2 0.0 collective-permute-done.mate_ref
  3.2 1.2 %collective-permute-start.2 = (bf16[16,32,128]{2,1,0:T(8,128)(2,1)S(1)}, bf16[16,32,128]{2,1,0:T(8,128)(2,1)S(1)}, u32[]{:S(2)}, u32[]{:S(2)}) collective-permute-start(bf16[16,32,128]{2,1,0:T(8,128)(2,1)S(1)} %collective-permute-done.mate_ref), channel_id=1, source_target_pairs={{2,0},{4,2},{6,4},{8,6},{10,8},{12,10},{14,12},{15,14},{1,3},{3,5}... | collective-permute-start | bytes 393224 | tf_op jit(solution)/shard_map/ppermute | solution.py:509
  4.5 0.1 collective-permute-start.4
  4.5 1.6 %first_spectra.2 = (f32[16,32,128]{2,1,0:T(8,128)S(1)}, f32[16,32,128]{2,1,0:T(8,128)S(1)}, f32[8,128]{1,0:T(8,128)S(1)}, bf16[256,256]{1,0:T(8,128)(2,1)S(1)}, ...) custom-call(bf16[16,32,128]{2,1,0:T(8,128)(2,1)} %own_hbm.1, s32[1,8]{1,0:T(1,128)} %shift_x_hbm.1, ...), custom_call_target="tpu_custom_call" | custom-call | flops 2000000000 | bytes 2000000 | tf_op jit(solution)/shard_map/first_spectra/pallas_call | solution.py:538
  6.1 0.0 collective-permute-done.1.near_own_ref
  6.1 1.8 %collective-permute-start.5 = (bf16[16,32,128]{2,1,0:T(8,128)(2,1)S(1)}, bf16[16,32,128]{2,1,0:T(8,128)(2,1)S(1)}, u32[]{:S(2)}, u32[]{:S(2)}) collective-permute-start(bf16[16,32,128]{2,1,0:T(8,128)(2,1)S(1)} %collective-permute-done.1.near_own_ref), channel_id=1, source_target_pairs={{0,1},{1,0},{2,3},{3,2},{4,5},{5,4},{6,7},{7,6},{8,9},{9,8},{10,11... | collective-permute-start | bytes 393224 | tf_op jit(solution)/shard_map/ppermute | solution.py:509
  8.0 0.0 collective-permute-done.3.far_own_ref
  8.0 0.2 collective-permute-start.7
  8.2 0.3 %collective-permute-done.2.near_mate_ref = bf16[16,32,128]{2,1,0:T(8,128)(2,1)S(1)} collective-permute-done((bf16[16,32,128]{2,1,0:T(8,128)(2,1)S(1)}, bf16[16,32,128]{2,1,0:T(8,128)(2,1)S(1)}, u32[]{:S(2)}, u32[]{:S(2)}) %collective-permute-start.2) | collective-permute-done | bytes 131104 | tf_op jit(solution)/shard_map/ppermute | solution.py:509
  8.6 2.9 %collective-permute-start.6 = (bf16[16,32,128]{2,1,0:T(8,128)(2,1)S(1)}, bf16[16,32,128]{2,1,0:T(8,128)(2,1)S(1)}, u32[]{:S(2)}, u32[]{:S(2)}) collective-permute-start(bf16[16,32,128]{2,1,0:T(8,128)(2,1)S(1)} %collective-permute-done.2.near_mate_ref), channel_id=1, source_target_pairs={{0,1},{1,0},{2,3},{3,2},{4,5},{5,4},{6,7},{7,6},{8,9},{9,8},{10,11... | collective-permute-start | bytes 393224 | tf_op jit(solution)/shard_map/ppermute | solution.py:509
  11.5 0.0 collective-permute-done.4.far_mate_ref
  11.5 1.0 %collective-permute-start.8 = (bf16[16,32,128]{2,1,0:T(8,128)(2,1)S(1)}, bf16[16,32,128]{2,1,0:T(8,128)(2,1)S(1)}, u32[]{:S(2)}, u32[]{:S(2)}) collective-permute-start(bf16[16,32,128]{2,1,0:T(8,128)(2,1)S(1)} %collective-permute-done.4.far_mate_ref), channel_id=1, source_target_pairs={{0,1},{1,0},{2,3},{3,2},{4,5},{5,4},{6,7},{7,6},{8,9},{9,8},{10,11... | collective-permute-start | bytes 393224 | tf_op jit(solution)/shard_map/ppermute | solution.py:509
  12.4 0.0 collective-permute-done.9.next_ref
  12.4 0.0 copy-start.3
  12.5 0.0 copy-start.4
  12.5 1.6 %first_spectra.3 = (f32[32,32,128]{2,1,0:T(8,128)S(1)}, f32[32,32,128]{2,1,0:T(8,128)S(1)}, f32[32,128]{1,0:T(8,128)S(1)}, f32[8,128]{1,0:T(8,128)S(1)}) custom-call(bf16[16,32,128]{2,1,0:T(8,128)(2,1)S(1)} %collective-permute-done.9.next_ref, bf16[256,256]{1,0:T(8,128)(2,1)S(1)} %get-tuple-element.28.y_ref, bf16[256,768]{1,0:T(8,128)(2,1)S(1)} %get-tuple-element.29.z_ref, ...), custom_call_target="tpu_custom_call" | custom-call | flops 2000000000 | bytes 2000000 | tf_op jit(solution)/shard_map/first_spectra/pallas_call | solution.py:538
  14.1 0.0 collective-permute-done.5.mate_near_own_ref
  14.1 0.0 collective-permute-done.7.mate_far_own_ref
  14.1 0.0 collective-permute-done.6.mate_near_mate_ref
  14.1 0.0 collective-permute-done.8.mate_far_mate_ref
  14.1 0.0 copy-done
  14.2 0.0 copy-done.1
  14.2 4.8 %second_maps.1.own_ref = f32[256,128]{1,0:T(8,128)S(1)} custom-call(s32[1,8]{1,0:T(1,128)S(1)} %get-tuple-element.21.shift_x_ref, s32[1,8]{1,0:T(1,128)S(1)} %get-tuple-element.22.shift_y_ref, bf16[16,32,128]{2,1,0:T(8,128)(2,1)S(1)} %copy-done.2, bf16[16,32,128]{2,1,0:T(8,128)(2,1)S(1)} %collective-permute-done.mate_ref, ...), custom_call_target="tpu_custom_call" | custom-call | tf_op jit(solution)/shard_map/second_maps/pallas_call | solution.py:576
  19.0 0.1 collective-permute-start.10
  19.1 2.1 %collective-permute-start.11 = (f32[256,128]{1,0:T(8,128)S(1)}, f32[256,128]{1,0:T(8,128)S(1)}, u32[]{:S(2)}, u32[]{:S(2)}) collective-permute-start(f32[256,128]{1,0:T(8,128)S(1)} %second_maps.1.own_ref), channel_id=1, source_target_pairs={{1,2},{2,1},{3,4},{4,3},{5,6},{6,5},{7,8},{8,7},{9,10},{10,9},{11,... | collective-permute-start | bytes 393224 | tf_op jit(solution)/shard_map/ppermute | solution.py:509
  21.2 0.0 collective-permute-done.10.mate_ref
  21.2 5.5 %collective-permute-done.11.other_ref = f32[256,128]{1,0:T(8,128)S(1)} collective-permute-done((f32[256,128]{1,0:T(8,128)S(1)}, f32[256,128]{1,0:T(8,128)S(1)}, u32[]{:S(2)}, u32[]{:S(2)}) %collective-permute-start.11) | collective-permute-done | bytes 131104 | tf_op jit(solution)/shard_map/ppermute | solution.py:509
  26.7 0.8 %product.1 = f32[256,128]{1,0:T(8,128)} custom-call(f32[256,128]{1,0:T(8,128)S(1)} %second_maps.1.own_ref, f32[256,128]{1,0:T(8,128)S(1)} %collective-permute-done.10.mate_ref, f32[256,128]{1,0:T(8,128)S(1)} %collective-permute-done.11.other_ref), custom_call_target="tpu_custom_call" | custom-call | tf_op jit(solution)/shard_map/product/pallas_call | solution.py:608
  (6 shorter events, 0.0 us)
Async XLA Ops:
  0.0 3.2 %collective-permute-start = (bf16[16,32,128]{2,1,0:T(8,128)(2,1)}, bf16[16,32,128]{2,1,0:T(8,128)(2,1)S(1)}, u32[]{:S(2)}, u32[]{:S(2)}) collective-permute-start(bf16[16,32,128]{2,1,0:T(8,128)(2,1)} %own_ref.1), channel_id=1, source_target_pairs={{0,1},{1,0},{2,3},{3,2},{4,5},{5,4},{6,7},{7,6},{8,9},{9,8},{10,11... | collective-permute-start | bytes 393224 | tf_op jit(solution)/shard_map/ppermute | solution.py:509
  0.7 5.5 %collective-permute-start.1 = (bf16[16,32,128]{2,1,0:T(8,128)(2,1)}, bf16[16,32,128]{2,1,0:T(8,128)(2,1)S(1)}, u32[]{:S(2)}, u32[]{:S(2)}) collective-permute-start(bf16[16,32,128]{2,1,0:T(8,128)(2,1)} %own_ref.1), channel_id=1, source_target_pairs={{2,0},{4,2},{6,4},{8,6},{10,8},{12,10},{14,12},{15,14},{1,3},{3,5}... | collective-permute-start | bytes 393224 | tf_op jit(solution)/shard_map/ppermute | solution.py:509
  1.9 6.1 %collective-permute-start.3 = (bf16[16,32,128]{2,1,0:T(8,128)(2,1)}, bf16[16,32,128]{2,1,0:T(8,128)(2,1)S(1)}, u32[]{:S(2)}, u32[]{:S(2)}) collective-permute-start(bf16[16,32,128]{2,1,0:T(8,128)(2,1)} %own_ref.1), channel_id=1, source_target_pairs={{4,0},{6,2},{8,4},{10,6},{12,8},{14,10},{15,14},{13,12},{1,5},{3,7... | collective-permute-start | bytes 393224 | tf_op jit(solution)/shard_map/ppermute | solution.py:509
  3.2 9.2 %collective-permute-start.9 = (bf16[16,32,128]{2,1,0:T(8,128)(2,1)}, bf16[16,32,128]{2,1,0:T(8,128)(2,1)S(1)}, u32[]{:S(2)}, u32[]{:S(2)}) collective-permute-start(bf16[16,32,128]{2,1,0:T(8,128)(2,1)} %own_hbm.1), channel_id=1, source_target_pairs={{1,0},{2,1},{3,2},{4,3},{5,4},{6,5},{7,6},{8,7},{9,8},{10,9},{11,1... | collective-permute-start | bytes 393224 | tf_op jit(solution)/shard_map/ppermute | solution.py:509
  3.2 5.3 %collective-permute-start.2 = (bf16[16,32,128]{2,1,0:T(8,128)(2,1)S(1)}, bf16[16,32,128]{2,1,0:T(8,128)(2,1)S(1)}, u32[]{:S(2)}, u32[]{:S(2)}) collective-permute-start(bf16[16,32,128]{2,1,0:T(8,128)(2,1)S(1)} %collective-permute-done.mate_ref), channel_id=1, source_target_pairs={{2,0},{4,2},{6,4},{8,6},{10,8},{12,10},{14,12},{15,14},{1,3},{3,5}... | collective-permute-start | bytes 393224 | tf_op jit(solution)/shard_map/ppermute | solution.py:509
  4.5 7.0 %collective-permute-start.4 = (bf16[16,32,128]{2,1,0:T(8,128)(2,1)S(1)}, bf16[16,32,128]{2,1,0:T(8,128)(2,1)S(1)}, u32[]{:S(2)}, u32[]{:S(2)}) collective-permute-start(bf16[16,32,128]{2,1,0:T(8,128)(2,1)S(1)} %collective-permute-done.mate_ref), channel_id=1, source_target_pairs={{4,0},{6,2},{8,4},{10,6},{12,8},{14,10},{15,14},{13,12},{1,5},{3,7... | collective-permute-start | bytes 393224 | tf_op jit(solution)/shard_map/ppermute | solution.py:509
  6.1 8.0 %collective-permute-start.5 = (bf16[16,32,128]{2,1,0:T(8,128)(2,1)S(1)}, bf16[16,32,128]{2,1,0:T(8,128)(2,1)S(1)}, u32[]{:S(2)}, u32[]{:S(2)}) collective-permute-start(bf16[16,32,128]{2,1,0:T(8,128)(2,1)S(1)} %collective-permute-done.1.near_own_ref), channel_id=1, source_target_pairs={{0,1},{1,0},{2,3},{3,2},{4,5},{5,4},{6,7},{7,6},{8,9},{9,8},{10,11... | collective-permute-start | bytes 393224 | tf_op jit(solution)/shard_map/ppermute | solution.py:509
  8.0 6.1 %collective-permute-start.7 = (bf16[16,32,128]{2,1,0:T(8,128)(2,1)S(1)}, bf16[16,32,128]{2,1,0:T(8,128)(2,1)S(1)}, u32[]{:S(2)}, u32[]{:S(2)}) collective-permute-start(bf16[16,32,128]{2,1,0:T(8,128)(2,1)S(1)} %collective-permute-done.3.far_own_ref), channel_id=1, source_target_pairs={{0,1},{1,0},{2,3},{3,2},{4,5},{5,4},{6,7},{7,6},{8,9},{9,8},{10,11... | collective-permute-start | bytes 393224 | tf_op jit(solution)/shard_map/ppermute | solution.py:509
  8.6 5.6 %collective-permute-start.6 = (bf16[16,32,128]{2,1,0:T(8,128)(2,1)S(1)}, bf16[16,32,128]{2,1,0:T(8,128)(2,1)S(1)}, u32[]{:S(2)}, u32[]{:S(2)}) collective-permute-start(bf16[16,32,128]{2,1,0:T(8,128)(2,1)S(1)} %collective-permute-done.2.near_mate_ref), channel_id=1, source_target_pairs={{0,1},{1,0},{2,3},{3,2},{4,5},{5,4},{6,7},{7,6},{8,9},{9,8},{10,11... | collective-permute-start | bytes 393224 | tf_op jit(solution)/shard_map/ppermute | solution.py:509
  11.5 2.7 %collective-permute-start.8 = (bf16[16,32,128]{2,1,0:T(8,128)(2,1)S(1)}, bf16[16,32,128]{2,1,0:T(8,128)(2,1)S(1)}, u32[]{:S(2)}, u32[]{:S(2)}) collective-permute-start(bf16[16,32,128]{2,1,0:T(8,128)(2,1)S(1)} %collective-permute-done.4.far_mate_ref), channel_id=1, source_target_pairs={{0,1},{1,0},{2,3},{3,2},{4,5},{5,4},{6,7},{7,6},{8,9},{9,8},{10,11... | collective-permute-start | bytes 393224 | tf_op jit(solution)/shard_map/ppermute | solution.py:509
  12.4 1.7 %copy-start = (bf16[128,768]{1,0:T(8,128)(2,1)S(1)}, bf16[128,768]{1,0:T(8,128)(2,1)}, u32[]{:S(2)}) copy-start(bf16[128,768]{1,0:T(8,128)(2,1)} %constant.10.clone.z_inverse_ref) | copy-start | bytes 589828
  12.4 1.7 %copy-start.1 = (bf16[768,128]{1,0:T(8,128)(2,1)S(1)}, bf16[768,128]{1,0:T(8,128)(2,1)}, u32[]{:S(2)}) copy-start(bf16[768,128]{1,0:T(8,128)(2,1)} %constant.11.clone.y_inverse_ref) | copy-start | bytes 589828
  12.4 1.7 %copy-start.2 = (bf16[16,32,128]{2,1,0:T(8,128)(2,1)S(1)}, bf16[16,32,128]{2,1,0:T(8,128)(2,1)}, u32[]{:S(2)}) copy-start(bf16[16,32,128]{2,1,0:T(8,128)(2,1)} %own_ref.1) | copy-start | bytes 393220
  12.4 1.7 %copy-start.3 = (bf16[256,256]{1,0:T(8,128)(2,1)S(1)}, bf16[256,256]{1,0:T(8,128)(2,1)}, u32[]{:S(2)}) copy-start(bf16[256,256]{1,0:T(8,128)(2,1)} %constant.8.clone.y_high_ref) | copy-start | bytes 393220
  12.5 1.7 %copy-start.4 = (bf16[256,256]{1,0:T(8,128)(2,1)S(1)}, bf16[256,256]{1,0:T(8,128)(2,1)}, u32[]{:S(2)}) copy-start(bf16[256,256]{1,0:T(8,128)(2,1)} %constant.9.clone.y_low_ref) | copy-start | bytes 393220
  19.0 2.2 %collective-permute-start.10 = (f32[256,128]{1,0:T(8,128)S(1)}, f32[256,128]{1,0:T(8,128)S(1)}, u32[]{:S(2)}, u32[]{:S(2)}) collective-permute-start(f32[256,128]{1,0:T(8,128)S(1)} %second_maps.1.own_ref), channel_id=1, source_target_pairs={{0,1},{1,0},{2,3},{3,2},{4,5},{5,4},{6,7},{7,6},{8,9},{9,8},{10,11... | collective-permute-start | bytes 393224 | tf_op jit(solution)/shard_map/ppermute | solution.py:509
  19.1 7.7 %collective-permute-start.11 = (f32[256,128]{1,0:T(8,128)S(1)}, f32[256,128]{1,0:T(8,128)S(1)}, u32[]{:S(2)}, u32[]{:S(2)}) collective-permute-start(f32[256,128]{1,0:T(8,128)S(1)} %second_maps.1.own_ref), channel_id=1, source_target_pairs={{1,2},{2,1},{3,4},{4,3},{5,6},{6,5},{7,8},{8,7},{9,10},{10,9},{11,... | collective-permute-start | bytes 393224 | tf_op jit(solution)/shard_map/ppermute | solution.py:509

commit v4 on v3

--- a/solution.py
+++ b/solution.py
@@ -243,7 +243,7 @@
 
 
 def low_kernel(
-    own_hbm,
+    tile_ref,
     shift_x_hbm,
     shift_y_hbm,
     real_ref,
@@ -251,26 +251,28 @@
     energy_ref,
     y_ref,
     z_ref,
+    shifts_ref,
     shift_x_ref,
     shift_y_ref,
-    own_ref,
     sems,
 ):
     copies = [
-        pltpu.make_async_copy(own_hbm, own_ref, sems.at[0]),
-        pltpu.make_async_copy(shift_x_hbm, shift_x_ref, sems.at[1]),
-        pltpu.make_async_copy(shift_y_hbm, shift_y_ref, sems.at[2]),
+        pltpu.make_async_copy(shift_x_hbm, shift_x_ref, sems.at[0]),
+        pltpu.make_async_copy(shift_y_hbm, shift_y_ref, sems.at[1]),
     ]
     for copy in copies:
         copy.start()
     first_tables(y_ref, z_ref)
+    first_stage(tile_ref[...], y_ref, z_ref, real_ref, imag_ref, energy_ref)
     for copy in copies:
         copy.wait()
-    first_stage(own_ref[...], y_ref, z_ref, real_ref, imag_ref, energy_ref)
+    shifts_ref[0:1] = shift_x_ref[...]
+    shifts_ref[1:2] = shift_y_ref[...]
 
 
 def high_kernel(
     next_ref,
+    own_ref,
     y_ref,
     z_ref,
     low_real_ref,
@@ -285,14 +287,14 @@
     high_energy_ref,
 ):
     position = lax.axis_index("gx")
-    inside = position < lax.axis_size("gx") - 1
-    keep = jnp.where(inside, 1.0, 0.0).astype(BF16)
-    tile = next_ref[...] * keep
+    odd = position % 2
+    inside = position < lax.axis_size("gx") - 2
+    use_next = jnp.where(inside & (odd == 0), 1.0, 0.0).astype(BF16)
+    use_own = odd.astype(BF16)
+    tile = next_ref[...] * use_next + own_ref[...] * use_own
     first_stage(tile, y_ref, z_ref, high_real_ref, high_imag_ref, high_energy_ref)
 
-    def eight_slots(block, carry):
-        where_z = pl.ds(pl.multiple_of(block * 8, 8), 8)
-
+    def eight_slots(where_z):
         def value(x):
             if x < STEP:
                 return low_real_ref[x, where_z], low_imag_ref[x, where_z]
@@ -302,9 +304,9 @@
             for a, (real, imag) in enumerate(column):
                 real_ref[8 * b + a, where_z] = real
                 imag_ref[8 * b + a, where_z] = imag
-        return carry
-
-    lax.fori_loop(0, ZS // 8, eight_slots, 0)
+
+    for start in range(0, ZS, 8):
+        eight_slots(slice(start, start + 8))
     lines = [
         jnp.concatenate([low[:, slot], high[:, slot]], 0)
         for slot in (0, HALF)
@@ -315,8 +317,7 @@
 
 
 def second_kernel(
-    shift_x_ref,
-    shift_y_ref,
+    shifts_ref,
     own_ref,
     mate_ref,
     near_own_ref,
@@ -349,9 +350,9 @@
     odd = position % 2
     even = 1 - odd
     tiles_below = position - odd - 4
-    shifts_x, shifts_y = shift_x_ref[...], shift_y_ref[...]
-    starts_x = [shifts_x[0, j] + STEP * (4 + odd) for j in range(WY)]
-    starts_y = [shifts_y[0, j] + STEP * j for j in range(WY)]
+    shifts = shifts_ref[...]
+    starts_x = [shifts[0, j] + STEP * (4 + even) for j in range(WY)]
+    starts_y = [shifts[1, j] + STEP * j for j in range(WY)]
     tiles_at = (
         (own_ref, 4 + odd),
         (mate_ref, 4 + even),
@@ -374,8 +375,7 @@
 
     lane = lax.broadcasted_iota(jnp.int32, (1, LANES), 1)
 
-    def eight_x(step, energy):
-        start = step * 8
+    def eight_x(start, energy):
         packs = []
         for half in range(2):
             total = None
@@ -397,10 +397,10 @@
             values[: 4 * ZS], values[4 * ZS :], z_ref, real_ref, imag_ref, start
         )
 
-    energy = lax.fori_loop(0, WIN // 8, eight_x, jnp.zeros((8, LANES), F32))
-    def eight_slots(block, carry):
-        where_z = pl.ds(pl.multiple_of(block * 8, 8), 8)
-
+    energy = jnp.zeros((8, LANES), F32)
+    for start in range(0, WIN, 8):
+        energy = eight_x(start, energy)
+    def eight_slots(where_z):
         def value(x):
             return real_ref[x, where_z], imag_ref[x, where_z]
 
@@ -420,9 +420,9 @@
             back = plus(even, odd)
             cross_real_ref[8 + s, where_z], cross_imag_ref[8 + s, where_z] = here
             cross_real_ref[s, where_z], cross_imag_ref[s, where_z] = back
-        return carry
-
-    lax.fori_loop(0, ZS // 8, eight_slots, 0)
+
+    for start in range(0, ZS, 8):
+        eight_slots(slice(start, start + 8))
 
     lines, mean_energy = special_lines(
         real_ref[:, 0], imag_ref[:, 0], real_ref[:, HALF], imag_ref[:, HALF]
@@ -482,7 +482,7 @@
             out_ref[where_out] = values * scale[0:1]
 
 
-def product_kernel(own_ref, mate_ref, other_ref, out_ref):
+def product_kernel(made_ref, own_ref, other_ref, out_ref):
     position = lax.axis_index("gx")
     edge = (position == 0) | (position == lax.axis_size("gx") - 1)
     own = own_ref[...]
@@ -490,7 +490,7 @@
     below = jnp.where(lane < SR, 1.0, pltpu.roll(own, SR, 1))
     above = jnp.where(lane >= LANES - SR, 1.0, pltpu.roll(own, LANES - SR, 1))
     other = jnp.where(edge, 1.0, other_ref[...])
-    out_ref[...] = own * mate_ref[...] * other * below * above
+    out_ref[...] = own * made_ref[...] * other * below * above
 
 
 def params():
@@ -514,15 +514,11 @@
     near += [(2 * q - 1, 2 * q + 1) for q in range(1, chips)] + [(0, 1)]
     far = [(2 * q + 4, 2 * q) for q in range(chips - 2)] + [(last, last - 1), (last - 2, last - 3)]
     far += [(2 * q - 3, 2 * q + 1) for q in range(2, chips)] + [(0, 1), (2, 3)]
-    across = [(i, i + 1 if i % 2 else i - 1) for i in range(1, last)] + [(0, 0), (last, last)]
-
-    next_tile = send(first_volume, [((i + 1) % size, i) for i in range(size)])
     near_own = send(second_volume, near)
     mate_tile = send(second_volume, mates)
     far_own = send(second_volume, far)
+    near_first = send(first_volume, near)
     mate_first = send(first_volume, mates)
-    low_tile = first_volume
-    low_tile, mate_tile = lax.optimization_barrier((first_volume, mate_tile))
     near_mate = send(mate_tile, near)
     far_mate = send(mate_tile, far)
 
@@ -532,7 +528,7 @@
     row = jax.ShapeDtypeStruct((8, LANES), F32)
     y_table = jax.ShapeDtypeStruct((2 * NY, 2 * LANES), BF16)
     z_table = jax.ShapeDtypeStruct((2 * LANES, 6 * LANES), BF16)
-    shifts = [jax.ShapeDtypeStruct(v.shape, v.dtype) for v in (shift_x, shift_y)]
+    shifts = jax.ShapeDtypeStruct((2, WY), shift_x.dtype)
 
     def first_spectra(kernel, specs, outs, scratch, *operands):
         return pl.pallas_call(
@@ -548,23 +544,23 @@
             name="first_spectra",
         )(*operands)
 
-    *low_part, y_table, z_table, shift_x, shift_y = first_spectra(
+    *low_part, y_table, z_table, shifts = first_spectra(
         low_kernel,
-        [HBM] * 3,
-        (half, half, row, y_table, z_table, *shifts),
-        [pltpu.VMEM(first_volume.shape, BF16), pltpu.SemaphoreType.DMA((3,))],
-        *(
-            pltpu.with_memory_space_constraint(v, pltpu.HBM)
-            for v in (first_volume, shift_x, shift_y)
-        ),
+        [VMEM] + [HBM] * 2,
+        (half, half, row, y_table, z_table, shifts),
+        [pltpu.VMEM(v.shape, v.dtype) for v in (shift_x, shift_y)]
+        + [pltpu.SemaphoreType.DMA((2,))],
+        mate_first,
+        *(pltpu.with_memory_space_constraint(v, pltpu.HBM) for v in (shift_x, shift_y)),
     )
     near_own, *low_part = lax.optimization_barrier((near_own, *low_part))
     first_part = first_spectra(
         high_kernel,
-        [VMEM] * 6,
+        [VMEM] * 7,
         (whole, whole, lines, row),
         [pltpu.VMEM(v.shape, F32) for v in (half, half, row)],
-        next_tile,
+        near_first,
+        first_volume,
         y_table,
         z_table,
         *low_part,
@@ -576,7 +572,7 @@
     maps = pl.pallas_call(
         second_kernel,
         out_shape=jax.ShapeDtypeStruct((SR * SR, LANES), F32),
-        in_specs=[VMEM] * 21,
+        in_specs=[VMEM] * 20,
         out_specs=VMEM,
         scratch_shapes=[
             pltpu.VMEM((10 * STEP, ZS, NY), BF16),
@@ -589,8 +585,7 @@
         compiler_params=params(),
         name="second_maps",
     )(
-        shift_x,
-        shift_y,
+        send(shifts, mates),
         second_volume,
         mate_tile,
         *side,
@@ -603,8 +598,8 @@
         y_inverse_table(),
     )
 
-    other_maps = send(maps, across)
-    mate_maps = send(maps, mates)
+    own_maps = send(maps, mates)
+    other_maps = send(maps, [(b, a) for a, b in near])
     product = pl.pallas_call(
         product_kernel,
         out_shape=jax.ShapeDtypeStruct((SR * SR, LANES), F32),
@@ -612,7 +607,7 @@
         out_specs=VMEM,
         compiler_params=params(),
         name="product",
-    )(maps, mate_maps, other_maps)
+    )(maps, own_maps, other_maps)
     return product.reshape(1, SR, SR, LANES)
 
 

time: 27.7 us -> 25.7 us (0.928)
  the two profiles are of different devices: /device:TPU:9 before, /device:TPU:0 now
where the time goes in v4:
time: 25.7 us; the launch traced here: 25.5 us
  starting transfers between devices  12.3 us (48%)
  waiting for transfers between devices  6.57 us (26%)
  Pallas kernels  6.5 us (25%)
    ppermute x14, starting transfers between devices, send(): return lax.ppermute(value, 'gx', pairs)  12.3 us
    ppermute x14, waiting for transfers between devices, send(): return lax.ppermute(value, 'gx', pairs)  6.57 us
    pallas_call x1, Pallas kernels, local(): pl.pallas_call(second_kernel, out_shape=jax.ShapeDtypeStruct((SR * SR, LA...  3.39 us
    pallas_call x2, Pallas kernels, first_spectra(): pl.pallas_call(kernel, out_shape=outs, in_specs=specs, out_specs=(VMEM,)...  2.32 us
    pallas_call x1, Pallas kernels, local(): pl.pallas_call(product_kernel, out_shape=jax.ShapeDtypeStruct((SR * SR, L...  0.79 us
  transfers between devices with their start and end apart: 14, of which 3 were waited for; matrix products, arithmetic and copies ran while one was open for 0% of the time, Pallas kernels for 9%

profile of v4, /device:TPU:0, one launch (start us, length us, event | category | flops | bytes accessed | tf_op | source)
XLA Modules:
  0.0 25.5 jit_solution(12733588026635779330)
XLA Ops:
  0.0 0.5 %collective-permute-start.2 = (bf16[16,32,128]{2,1,0:T(8,128)(2,1)}, bf16[16,32,128]{2,1,0:T(8,128)(2,1)S(1)}, u32[]{:S(2)}, u32[]{:S(2)}) collective-permute-start(bf16[16,32,128]{2,1,0:T(8,128)(2,1)} %own_ref.3), channel_id=1, source_target_pairs={{0,1},{1,0},{2,3},{3,2},{4,5},{5,4},{6,7},{7,6},{8,9},{9,8},{10,11... | collective-permute-start | bytes 393224 | tf_op jit(solution)/shard_map/ppermute | solution.py:509
  0.5 0.1 collective-permute-start
  0.5 0.4 %collective-permute-start.3 = (bf16[16,32,128]{2,1,0:T(8,128)(2,1)}, bf16[16,32,128]{2,1,0:T(8,128)(2,1)S(1)}, u32[]{:S(2)}, u32[]{:S(2)}) collective-permute-start(bf16[16,32,128]{2,1,0:T(8,128)(2,1)} %own_ref.3), channel_id=1, source_target_pairs={{2,0},{4,2},{6,4},{8,6},{10,8},{12,10},{14,12},{15,14},{1,3},{3,5}... | collective-permute-start | bytes 393224 | tf_op jit(solution)/shard_map/ppermute | solution.py:509
  1.0 2.3 %collective-permute-start.11 = (bf16[16,32,128]{2,1,0:T(8,128)(2,1)}, bf16[16,32,128]{2,1,0:T(8,128)(2,1)S(1)}, u32[]{:S(2)}, u32[]{:S(2)}) collective-permute-start(bf16[16,32,128]{2,1,0:T(8,128)(2,1)} %own_ref.2), channel_id=1, source_target_pairs={{2,0},{4,2},{6,4},{8,6},{10,8},{12,10},{14,12},{15,14},{1,3},{3,5}... | collective-permute-start | bytes 393224 | tf_op jit(solution)/shard_map/ppermute | solution.py:509
  3.3 1.2 %collective-permute-start.5 = (bf16[16,32,128]{2,1,0:T(8,128)(2,1)}, bf16[16,32,128]{2,1,0:T(8,128)(2,1)S(1)}, u32[]{:S(2)}, u32[]{:S(2)}) collective-permute-start(bf16[16,32,128]{2,1,0:T(8,128)(2,1)} %own_ref.3), channel_id=1, source_target_pairs={{4,0},{6,2},{8,4},{10,6},{12,8},{14,10},{15,14},{13,12},{1,5},{3,7... | collective-permute-start | bytes 393224 | tf_op jit(solution)/shard_map/ppermute | solution.py:509
  4.5 0.0 collective-permute-done.2.mate_ref
  4.5 1.3 %collective-permute-start.6 = (bf16[16,32,128]{2,1,0:T(8,128)(2,1)S(1)}, bf16[16,32,128]{2,1,0:T(8,128)(2,1)S(1)}, u32[]{:S(2)}, u32[]{:S(2)}) collective-permute-start(bf16[16,32,128]{2,1,0:T(8,128)(2,1)S(1)} %collective-permute-done.2.mate_ref), channel_id=1, source_target_pairs={{4,0},{6,2},{8,4},{10,6},{12,8},{14,10},{15,14},{13,12},{1,5},{3,7... | collective-permute-start | bytes 393224 | tf_op jit(solution)/shard_map/ppermute | solution.py:509
  5.8 0.0 collective-permute-done.tile_ref
  5.8 1.3 %collective-permute-start.4 = (bf16[16,32,128]{2,1,0:T(8,128)(2,1)S(1)}, bf16[16,32,128]{2,1,0:T(8,128)(2,1)S(1)}, u32[]{:S(2)}, u32[]{:S(2)}) collective-permute-start(bf16[16,32,128]{2,1,0:T(8,128)(2,1)S(1)} %collective-permute-done.2.mate_ref), channel_id=1, source_target_pairs={{2,0},{4,2},{6,4},{8,6},{10,8},{12,10},{14,12},{15,14},{1,3},{3,5}... | collective-permute-start | bytes 393224 | tf_op jit(solution)/shard_map/ppermute | solution.py:509
  7.1 0.8 %first_spectra.2 = (f32[16,32,128]{2,1,0:T(8,128)S(1)}, f32[16,32,128]{2,1,0:T(8,128)S(1)}, f32[8,128]{1,0:T(8,128)S(1)}, bf16[256,256]{1,0:T(8,128)(2,1)S(1)}, ...) custom-call(bf16[16,32,128]{2,1,0:T(8,128)(2,1)S(1)} %collective-permute-done.tile_ref, s32[1,8]{1,0:T(1,128)} %shift_x_hbm.1, ...), custom_call_target="tpu_custom_call" | custom-call | flops 2000000000 | bytes 2000000 | tf_op jit(solution)/shard_map/first_spectra/pallas_call | solution.py:534
  7.9 0.0 collective-permute-done.3.near_own_ref
  7.9 1.3 %collective-permute-start.7 = (bf16[16,32,128]{2,1,0:T(8,128)(2,1)S(1)}, bf16[16,32,128]{2,1,0:T(8,128)(2,1)S(1)}, u32[]{:S(2)}, u32[]{:S(2)}) collective-permute-start(bf16[16,32,128]{2,1,0:T(8,128)(2,1)S(1)} %collective-permute-done.3.near_own_ref), channel_id=1, source_target_pairs={{0,1},{1,0},{2,3},{3,2},{4,5},{5,4},{6,7},{7,6},{8,9},{9,8},{10,11... | collective-permute-start | bytes 393224 | tf_op jit(solution)/shard_map/ppermute | solution.py:509
  9.2 0.0 collective-permute-done.11.next_ref
  9.2 0.5 %collective-permute-start.1 = (s32[2,8]{1,0:T(2,128)S(1)}, s32[2,8]{1,0:T(2,128)S(1)}, u32[]{:S(2)}, u32[]{:S(2)}) collective-permute-start(s32[2,8]{1,0:T(2,128)S(1)} %get-tuple-element.19), channel_id=1, source_target_pairs={{0,1},{1,0},{2,3},{3,2},{4,5},{5,4},{6,7},{7,6},{8,9},{9,8},{10,11... | collective-permute-start | bytes 200 | tf_op jit(solution)/shard_map/ppermute | solution.py:509
  9.7 1.2 %collective-permute-done.5.far_own_ref = bf16[16,32,128]{2,1,0:T(8,128)(2,1)S(1)} collective-permute-done((bf16[16,32,128]{2,1,0:T(8,128)(2,1)}, bf16[16,32,128]{2,1,0:T(8,128)(2,1)S(1)}, u32[]{:S(2)}, u32[]{:S(2)}) %collective-permute-start.5) | collective-permute-done | bytes 131104 | tf_op jit(solution)/shard_map/ppermute | solution.py:509
  11.0 0.0 collective-permute-start.9
  11.0 1.4 %collective-permute-done.6.far_mate_ref = bf16[16,32,128]{2,1,0:T(8,128)(2,1)S(1)} collective-permute-done((bf16[16,32,128]{2,1,0:T(8,128)(2,1)S(1)}, bf16[16,32,128]{2,1,0:T(8,128)(2,1)S(1)}, u32[]{:S(2)}, u32[]{:S(2)}) %collective-permute-start.6) | collective-permute-done | bytes 131104 | tf_op jit(solution)/shard_map/ppermute | solution.py:509
  12.4 0.0 collective-permute-start.10
  12.4 0.0 collective-permute-done.4.near_mate_ref
  12.4 0.5 %collective-permute-start.8 = (bf16[16,32,128]{2,1,0:T(8,128)(2,1)S(1)}, bf16[16,32,128]{2,1,0:T(8,128)(2,1)S(1)}, u32[]{:S(2)}, u32[]{:S(2)}) collective-permute-start(bf16[16,32,128]{2,1,0:T(8,128)(2,1)S(1)} %collective-permute-done.4.near_mate_ref), channel_id=1, source_target_pairs={{0,1},{1,0},{2,3},{3,2},{4,5},{5,4},{6,7},{7,6},{8,9},{9,8},{10,11... | collective-permute-start | bytes 393224 | tf_op jit(solution)/shard_map/ppermute | solution.py:509
  12.9 0.0 copy-start.3
  12.9 0.0 copy-start.4
  12.9 1.5 %first_spectra.3 = (f32[32,32,128]{2,1,0:T(8,128)S(1)}, f32[32,32,128]{2,1,0:T(8,128)S(1)}, f32[32,128]{1,0:T(8,128)S(1)}, f32[8,128]{1,0:T(8,128)S(1)}) custom-call(bf16[16,32,128]{2,1,0:T(8,128)(2,1)S(1)} %collective-permute-done.11.next_ref, bf16[16,32,128]{2,1,0:T(8,128)(2,1)S(1)} %copy-done.5, bf16[256,256]{1,0:T(8,128)(2,1)S(1)} %get-tuple-element.24.y_ref, ...), custom_call_target="tpu_custom_call" | custom-call | flops 2000000000 | bytes 2000000 | tf_op jit(solution)/shard_map/first_spectra/pallas_call | solution.py:534
  14.4 0.0 collective-permute-done.1.shifts_ref
  14.4 0.0 collective-permute-done.7.mate_near_own_ref
  14.4 0.0 collective-permute-done.9.mate_far_own_ref
  14.5 0.0 collective-permute-done.8.mate_near_mate_ref
  14.5 3.4 %second_maps.1.made_ref = f32[256,128]{1,0:T(8,128)S(1)} custom-call(s32[2,8]{1,0:T(2,128)S(1)} %collective-permute-done.1.shifts_ref, bf16[16,32,128]{2,1,0:T(8,128)(2,1)S(1)} %copy-done.2, bf16[16,32,128]{2,1,0:T(8,128)(2,1)S(1)} %collective-permute-done.2.mate_ref, bf16[16,32,128]{2,1,0:T(8,128)(2,1)S(1)} %collective-permute-done.3.near_own_ref, ...), custom_call_target="tpu_custom_call" | custom-call | tf_op jit(solution)/shard_map/second_maps/pallas_call | solution.py:572
  17.9 0.1 collective-permute-start.12
  18.0 2.8 %collective-permute-start.13 = (f32[256,128]{1,0:T(8,128)S(1)}, f32[256,128]{1,0:T(8,128)S(1)}, u32[]{:S(2)}, u32[]{:S(2)}) collective-permute-start(f32[256,128]{1,0:T(8,128)S(1)} %second_maps.1.made_ref), channel_id=1, source_target_pairs={{0,2},{2,4},{4,6},{6,8},{8,10},{10,12},{12,14},{14,15},{3,1},{5,3}... | collective-permute-start | bytes 393224 | tf_op jit(solution)/shard_map/ppermute | solution.py:509
  20.8 3.9 %collective-permute-done.13.other_ref = f32[256,128]{1,0:T(8,128)S(1)} collective-permute-done((f32[256,128]{1,0:T(8,128)S(1)}, f32[256,128]{1,0:T(8,128)S(1)}, u32[]{:S(2)}, u32[]{:S(2)}) %collective-permute-start.13) | collective-permute-done | bytes 131104 | tf_op jit(solution)/shard_map/ppermute | solution.py:509
  24.7 0.8 %product.1 = f32[256,128]{1,0:T(8,128)} custom-call(f32[256,128]{1,0:T(8,128)S(1)} %second_maps.1.made_ref, f32[256,128]{1,0:T(8,128)S(1)} %collective-permute-done.12.own_ref, f32[256,128]{1,0:T(8,128)S(1)} %collective-permute-done.13.other_ref), custom_call_target="tpu_custom_call" | custom-call | tf_op jit(solution)/shard_map/product/pallas_call | solution.py:603
  (12 shorter events, 0.0 us)
Async XLA Ops:
  0.0 12.9 %copy-start.5 = (bf16[16,32,128]{2,1,0:T(8,128)(2,1)S(1)}, bf16[16,32,128]{2,1,0:T(8,128)(2,1)}, u32[]{:S(2)}) copy-start(bf16[16,32,128]{2,1,0:T(8,128)(2,1)} %own_ref.2) | copy-start | bytes 393220
  0.0 4.5 %collective-permute-start.2 = (bf16[16,32,128]{2,1,0:T(8,128)(2,1)}, bf16[16,32,128]{2,1,0:T(8,128)(2,1)S(1)}, u32[]{:S(2)}, u32[]{:S(2)}) collective-permute-start(bf16[16,32,128]{2,1,0:T(8,128)(2,1)} %own_ref.3), channel_id=1, source_target_pairs={{0,1},{1,0},{2,3},{3,2},{4,5},{5,4},{6,7},{7,6},{8,9},{9,8},{10,11... | collective-permute-start | bytes 393224 | tf_op jit(solution)/shard_map/ppermute | solution.py:509
  0.5 5.4 %collective-permute-start = (bf16[16,32,128]{2,1,0:T(8,128)(2,1)}, bf16[16,32,128]{2,1,0:T(8,128)(2,1)S(1)}, u32[]{:S(2)}, u32[]{:S(2)}) collective-permute-start(bf16[16,32,128]{2,1,0:T(8,128)(2,1)} %own_ref.2), channel_id=1, source_target_pairs={{0,1},{1,0},{2,3},{3,2},{4,5},{5,4},{6,7},{7,6},{8,9},{9,8},{10,11... | collective-permute-start | bytes 393224 | tf_op jit(solution)/shard_map/ppermute | solution.py:509
  0.5 7.4 %collective-permute-start.3 = (bf16[16,32,128]{2,1,0:T(8,128)(2,1)}, bf16[16,32,128]{2,1,0:T(8,128)(2,1)S(1)}, u32[]{:S(2)}, u32[]{:S(2)}) collective-permute-start(bf16[16,32,128]{2,1,0:T(8,128)(2,1)} %own_ref.3), channel_id=1, source_target_pairs={{2,0},{4,2},{6,4},{8,6},{10,8},{12,10},{14,12},{15,14},{1,3},{3,5}... | collective-permute-start | bytes 393224 | tf_op jit(solution)/shard_map/ppermute | solution.py:509
  1.0 8.3 %collective-permute-start.11 = (bf16[16,32,128]{2,1,0:T(8,128)(2,1)}, bf16[16,32,128]{2,1,0:T(8,128)(2,1)S(1)}, u32[]{:S(2)}, u32[]{:S(2)}) collective-permute-start(bf16[16,32,128]{2,1,0:T(8,128)(2,1)} %own_ref.2), channel_id=1, source_target_pairs={{2,0},{4,2},{6,4},{8,6},{10,8},{12,10},{14,12},{15,14},{1,3},{3,5}... | collective-permute-start | bytes 393224 | tf_op jit(solution)/shard_map/ppermute | solution.py:509
  3.3 7.7 %collective-permute-start.5 = (bf16[16,32,128]{2,1,0:T(8,128)(2,1)}, bf16[16,32,128]{2,1,0:T(8,128)(2,1)S(1)}, u32[]{:S(2)}, u32[]{:S(2)}) collective-permute-start(bf16[16,32,128]{2,1,0:T(8,128)(2,1)} %own_ref.3), channel_id=1, source_target_pairs={{4,0},{6,2},{8,4},{10,6},{12,8},{14,10},{15,14},{13,12},{1,5},{3,7... | collective-permute-start | bytes 393224 | tf_op jit(solution)/shard_map/ppermute | solution.py:509
  4.5 7.8 %collective-permute-start.6 = (bf16[16,32,128]{2,1,0:T(8,128)(2,1)S(1)}, bf16[16,32,128]{2,1,0:T(8,128)(2,1)S(1)}, u32[]{:S(2)}, u32[]{:S(2)}) collective-permute-start(bf16[16,32,128]{2,1,0:T(8,128)(2,1)S(1)} %collective-permute-done.2.mate_ref), channel_id=1, source_target_pairs={{4,0},{6,2},{8,4},{10,6},{12,8},{14,10},{15,14},{13,12},{1,5},{3,7... | collective-permute-start | bytes 393224 | tf_op jit(solution)/shard_map/ppermute | solution.py:509
  5.8 6.6 %collective-permute-start.4 = (bf16[16,32,128]{2,1,0:T(8,128)(2,1)S(1)}, bf16[16,32,128]{2,1,0:T(8,128)(2,1)S(1)}, u32[]{:S(2)}, u32[]{:S(2)}) collective-permute-start(bf16[16,32,128]{2,1,0:T(8,128)(2,1)S(1)} %collective-permute-done.2.mate_ref), channel_id=1, source_target_pairs={{2,0},{4,2},{6,4},{8,6},{10,8},{12,10},{14,12},{15,14},{1,3},{3,5}... | collective-permute-start | bytes 393224 | tf_op jit(solution)/shard_map/ppermute | solution.py:509
  7.9 6.5 %collective-permute-start.7 = (bf16[16,32,128]{2,1,0:T(8,128)(2,1)S(1)}, bf16[16,32,128]{2,1,0:T(8,128)(2,1)S(1)}, u32[]{:S(2)}, u32[]{:S(2)}) collective-permute-start(bf16[16,32,128]{2,1,0:T(8,128)(2,1)S(1)} %collective-permute-done.3.near_own_ref), channel_id=1, source_target_pairs={{0,1},{1,0},{2,3},{3,2},{4,5},{5,4},{6,7},{7,6},{8,9},{9,8},{10,11... | collective-permute-start | bytes 393224 | tf_op jit(solution)/shard_map/ppermute | solution.py:509
  9.2 5.2 %collective-permute-start.1 = (s32[2,8]{1,0:T(2,128)S(1)}, s32[2,8]{1,0:T(2,128)S(1)}, u32[]{:S(2)}, u32[]{:S(2)}) collective-permute-start(s32[2,8]{1,0:T(2,128)S(1)} %get-tuple-element.19), channel_id=1, source_target_pairs={{0,1},{1,0},{2,3},{3,2},{4,5},{5,4},{6,7},{7,6},{8,9},{9,8},{10,11... | collective-permute-start | bytes 200 | tf_op jit(solution)/shard_map/ppermute | solution.py:509
  11.0 3.5 %collective-permute-start.9 = (bf16[16,32,128]{2,1,0:T(8,128)(2,1)S(1)}, bf16[16,32,128]{2,1,0:T(8,128)(2,1)S(1)}, u32[]{:S(2)}, u32[]{:S(2)}) collective-permute-start(bf16[16,32,128]{2,1,0:T(8,128)(2,1)S(1)} %collective-permute-done.5.far_own_ref), channel_id=1, source_target_pairs={{0,1},{1,0},{2,3},{3,2},{4,5},{5,4},{6,7},{7,6},{8,9},{9,8},{10,11... | collective-permute-start | bytes 393224 | tf_op jit(solution)/shard_map/ppermute | solution.py:509
  12.4 2.1 %collective-permute-start.10 = (bf16[16,32,128]{2,1,0:T(8,128)(2,1)S(1)}, bf16[16,32,128]{2,1,0:T(8,128)(2,1)S(1)}, u32[]{:S(2)}, u32[]{:S(2)}) collective-permute-start(bf16[16,32,128]{2,1,0:T(8,128)(2,1)S(1)} %collective-permute-done.6.far_mate_ref), channel_id=1, source_target_pairs={{0,1},{1,0},{2,3},{3,2},{4,5},{5,4},{6,7},{7,6},{8,9},{9,8},{10,11... | collective-permute-start | bytes 393224 | tf_op jit(solution)/shard_map/ppermute | solution.py:509
  12.4 2.1 %collective-permute-start.8 = (bf16[16,32,128]{2,1,0:T(8,128)(2,1)S(1)}, bf16[16,32,128]{2,1,0:T(8,128)(2,1)S(1)}, u32[]{:S(2)}, u32[]{:S(2)}) collective-permute-start(bf16[16,32,128]{2,1,0:T(8,128)(2,1)S(1)} %collective-permute-done.4.near_mate_ref), channel_id=1, source_target_pairs={{0,1},{1,0},{2,3},{3,2},{4,5},{5,4},{6,7},{7,6},{8,9},{9,8},{10,11... | collective-permute-start | bytes 393224 | tf_op jit(solution)/shard_map/ppermute | solution.py:509
  12.9 1.6 %copy-start = (bf16[128,768]{1,0:T(8,128)(2,1)S(1)}, bf16[128,768]{1,0:T(8,128)(2,1)}, u32[]{:S(2)}) copy-start(bf16[128,768]{1,0:T(8,128)(2,1)} %constant.10.clone.z_inverse_ref) | copy-start | bytes 589828
  12.9 1.6 %copy-start.1 = (bf16[768,128]{1,0:T(8,128)(2,1)S(1)}, bf16[768,128]{1,0:T(8,128)(2,1)}, u32[]{:S(2)}) copy-start(bf16[768,128]{1,0:T(8,128)(2,1)} %constant.11.clone.y_inverse_ref) | copy-start | bytes 589828
  12.9 1.6 %copy-start.2 = (bf16[16,32,128]{2,1,0:T(8,128)(2,1)S(1)}, bf16[16,32,128]{2,1,0:T(8,128)(2,1)}, u32[]{:S(2)}) copy-start(bf16[16,32,128]{2,1,0:T(8,128)(2,1)} %own_ref.3) | copy-start | bytes 393220
  12.9 1.6 %copy-start.3 = (bf16[256,256]{1,0:T(8,128)(2,1)S(1)}, bf16[256,256]{1,0:T(8,128)(2,1)}, u32[]{:S(2)}) copy-start(bf16[256,256]{1,0:T(8,128)(2,1)} %constant.8.clone.y_high_ref) | copy-start | bytes 393220
  12.9 1.6 %copy-start.4 = (bf16[256,256]{1,0:T(8,128)(2,1)S(1)}, bf16[256,256]{1,0:T(8,128)(2,1)}, u32[]{:S(2)}) copy-start(bf16[256,256]{1,0:T(8,128)(2,1)} %constant.9.clone.y_low_ref) | copy-start | bytes 393220
  17.9 2.9 %collective-permute-start.12 = (f32[256,128]{1,0:T(8,128)S(1)}, f32[256,128]{1,0:T(8,128)S(1)}, u32[]{:S(2)}, u32[]{:S(2)}) collective-permute-start(f32[256,128]{1,0:T(8,128)S(1)} %second_maps.1.made_ref), channel_id=1, source_target_pairs={{0,1},{1,0},{2,3},{3,2},{4,5},{5,4},{6,7},{7,6},{8,9},{9,8},{10,11... | collective-permute-start | bytes 393224 | tf_op jit(solution)/shard_map/ppermute | solution.py:509
  18.0 6.7 %collective-permute-start.13 = (f32[256,128]{1,0:T(8,128)S(1)}, f32[256,128]{1,0:T(8,128)S(1)}, u32[]{:S(2)}, u32[]{:S(2)}) collective-permute-start(f32[256,128]{1,0:T(8,128)S(1)} %second_maps.1.made_ref), channel_id=1, source_target_pairs={{0,2},{2,4},{4,6},{6,8},{8,10},{10,12},{12,14},{14,15},{3,1},{5,3}... | collective-permute-start | bytes 393224 | tf_op jit(solution)/shard_map/ppermute | solution.py:509

commit v5 on v4

--- a/solution.py
+++ b/solution.py
@@ -327,7 +327,6 @@
     mate_near_own_ref,
     mate_near_mate_ref,
     mate_far_own_ref,
-    mate_far_mate_ref,
     first_real_ref,
     first_imag_ref,
     first_lines_ref,
@@ -363,7 +362,6 @@
         (mate_near_own_ref, 3 + 3 * odd),
         (mate_near_mate_ref, 2 + 5 * odd),
         (mate_far_own_ref, 1 + 7 * odd),
-        (mate_far_mate_ref, 9 * odd),
     )
     for tile_ref, at in tiles_at:
         region_ref[pl.ds(at * STEP, STEP)] = tile_ref[...]
@@ -447,6 +445,7 @@
     scale = 1.0 / (
         WIN**1.5 * (jnp.sqrt(first_var_ref[...] + 1e-6) * jnp.sqrt(second_var + 1e-6))
     )
+    pairs = []
     for start in range(0, SR, 8):
         columns = []
         for quarter in range(start, start + 8, 4):
@@ -477,12 +476,12 @@
         for h in range(2):
             lanes = slice(h * LANES, (h + 1) * LANES)
             pair = jnp.concatenate([slots[: 4 * SR, lanes], slots[4 * SR :, lanes]], 1)
-            values = dot(split(pair, 1), y_inverse_ref[...])
-            where_out = slice((start + 4 * h) * SR, (start + 4 * h + 4) * SR)
-            out_ref[where_out] = values * scale[0:1]
-
-
-def product_kernel(made_ref, own_ref, other_ref, out_ref):
+            pairs.append(pair)
+    values = dot(split(jnp.concatenate(pairs, 0), 1), y_inverse_ref[...])
+    out_ref[...] = values * scale[0:1]
+
+
+def product_kernel(made_ref, other_ref, own_ref, out_ref):
     position = lax.axis_index("gx")
     edge = (position == 0) | (position == lax.axis_size("gx") - 1)
     own = own_ref[...]
@@ -554,6 +553,7 @@
         *(pltpu.with_memory_space_constraint(v, pltpu.HBM) for v in (shift_x, shift_y)),
     )
     near_own, *low_part = lax.optimization_barrier((near_own, *low_part))
+    near_first, far_mate = lax.optimization_barrier((near_first, far_mate))
     first_part = first_spectra(
         high_kernel,
         [VMEM] * 7,
@@ -566,13 +566,13 @@
         *low_part,
     )
     side = (near_own, near_mate, far_own, far_mate)
-    mate_side = [send(tile, mates) for tile in side]
+    mate_side = [send(tile, mates) for tile in side[:3]]
 
     y_high, y_low = second_y_table()
     maps = pl.pallas_call(
         second_kernel,
         out_shape=jax.ShapeDtypeStruct((SR * SR, LANES), F32),
-        in_specs=[VMEM] * 20,
+        in_specs=[VMEM] * 19,
         out_specs=VMEM,
         scratch_shapes=[
             pltpu.VMEM((10 * STEP, ZS, NY), BF16),
@@ -607,7 +607,7 @@
         out_specs=VMEM,
         compiler_params=params(),
         name="product",
-    )(maps, own_maps, other_maps)
+    )(maps, other_maps, own_maps)
     return product.reshape(1, SR, SR, LANES)
 
 

time: 25.7 us -> 24.9 us (0.969)
  starting transfers between devices: 12.3 us -> 11.8 us
    ppermute x14 -> x13, starting transfers between devices: 12.3 us -> 11.8 us  [send(): return lax.ppermute(value, 'gx', pairs)]
    ppermute x14 -> x13, waiting for transfers between devices: 6.57 us -> 6.57 us  [send(): return lax.ppermute(value, 'gx', pairs)]
  transfers between devices with their start and end apart: 14 -> 13, of which waited for: 3 -> 3; matrix products, arithmetic and copies ran while one was open for 0% -> 0% of each run, Pallas kernels for 9% -> 9%
where the time goes in v5:
time: 24.9 us; the launch traced here: 24.8 us
  starting transfers between devices  11.8 us (47%)
  waiting for transfers between devices  6.57 us (26%)
  Pallas kernels  6.26 us (25%)
    ppermute x13, starting transfers between devices, send(): return lax.ppermute(value, 'gx', pairs)  11.8 us
    ppermute x13, waiting for transfers between devices, send(): return lax.ppermute(value, 'gx', pairs)  6.57 us
    pallas_call x1, Pallas kernels, local(): pl.pallas_call(second_kernel, out_shape=jax.ShapeDtypeStruct((SR * SR, LA...  3.15 us
    pallas_call x2, Pallas kernels, first_spectra(): pl.pallas_call(kernel, out_shape=outs, in_specs=specs, out_specs=(VMEM,)...  2.32 us
    pallas_call x1, Pallas kernels, local(): pl.pallas_call(product_kernel, out_shape=jax.ShapeDtypeStruct((SR * SR, L...  0.79 us
  transfers between devices with their start and end apart: 13, of which 3 were waited for; matrix products, arithmetic and copies ran while one was open for 0% of the time, Pallas kernels for 9%

profile of v5, /device:TPU:0, one launch (start us, length us, event | category | flops | bytes accessed | tf_op | source)
XLA Modules:
  0.0 24.8 jit_solution(6999926090100858889)
XLA Ops:
  0.0 0.5 %collective-permute-start.2 = (bf16[16,32,128]{2,1,0:T(8,128)(2,1)}, bf16[16,32,128]{2,1,0:T(8,128)(2,1)S(1)}, u32[]{:S(2)}, u32[]{:S(2)}) collective-permute-start(bf16[16,32,128]{2,1,0:T(8,128)(2,1)} %own_ref.3), channel_id=1, source_target_pairs={{0,1},{1,0},{2,3},{3,2},{4,5},{5,4},{6,7},{7,6},{8,9},{9,8},{10,11... | collective-permute-start | bytes 393224 | tf_op jit(solution)/shard_map/ppermute | solution.py:508
  0.5 0.1 collective-permute-start
  0.5 0.4 %collective-permute-start.3 = (bf16[16,32,128]{2,1,0:T(8,128)(2,1)}, bf16[16,32,128]{2,1,0:T(8,128)(2,1)S(1)}, u32[]{:S(2)}, u32[]{:S(2)}) collective-permute-start(bf16[16,32,128]{2,1,0:T(8,128)(2,1)} %own_ref.3), channel_id=1, source_target_pairs={{2,0},{4,2},{6,4},{8,6},{10,8},{12,10},{14,12},{15,14},{1,3},{3,5}... | collective-permute-start | bytes 393224 | tf_op jit(solution)/shard_map/ppermute | solution.py:508
  1.0 2.3 %collective-permute-start.6 = (bf16[16,32,128]{2,1,0:T(8,128)(2,1)}, bf16[16,32,128]{2,1,0:T(8,128)(2,1)S(1)}, u32[]{:S(2)}, u32[]{:S(2)}) collective-permute-start(bf16[16,32,128]{2,1,0:T(8,128)(2,1)} %own_ref.2), channel_id=1, source_target_pairs={{2,0},{4,2},{6,4},{8,6},{10,8},{12,10},{14,12},{15,14},{1,3},{3,5}... | collective-permute-start | bytes 393224 | tf_op jit(solution)/shard_map/ppermute | solution.py:508
  3.3 1.2 %collective-permute-start.5 = (bf16[16,32,128]{2,1,0:T(8,128)(2,1)}, bf16[16,32,128]{2,1,0:T(8,128)(2,1)S(1)}, u32[]{:S(2)}, u32[]{:S(2)}) collective-permute-start(bf16[16,32,128]{2,1,0:T(8,128)(2,1)} %own_ref.3), channel_id=1, source_target_pairs={{4,0},{6,2},{8,4},{10,6},{12,8},{14,10},{15,14},{13,12},{1,5},{3,7... | collective-permute-start | bytes 393224 | tf_op jit(solution)/shard_map/ppermute | solution.py:508
  4.5 0.0 collective-permute-done.2.mate_ref
  4.5 1.3 %collective-permute-start.7 = (bf16[16,32,128]{2,1,0:T(8,128)(2,1)S(1)}, bf16[16,32,128]{2,1,0:T(8,128)(2,1)S(1)}, u32[]{:S(2)}, u32[]{:S(2)}) collective-permute-start(bf16[16,32,128]{2,1,0:T(8,128)(2,1)S(1)} %collective-permute-done.2.mate_ref), channel_id=1, source_target_pairs={{4,0},{6,2},{8,4},{10,6},{12,8},{14,10},{15,14},{13,12},{1,5},{3,7... | collective-permute-start | bytes 393224 | tf_op jit(solution)/shard_map/ppermute | solution.py:508
  5.8 0.0 collective-permute-done.tile_ref
  5.8 1.3 %collective-permute-start.4 = (bf16[16,32,128]{2,1,0:T(8,128)(2,1)S(1)}, bf16[16,32,128]{2,1,0:T(8,128)(2,1)S(1)}, u32[]{:S(2)}, u32[]{:S(2)}) collective-permute-start(bf16[16,32,128]{2,1,0:T(8,128)(2,1)S(1)} %collective-permute-done.2.mate_ref), channel_id=1, source_target_pairs={{2,0},{4,2},{6,4},{8,6},{10,8},{12,10},{14,12},{15,14},{1,3},{3,5}... | collective-permute-start | bytes 393224 | tf_op jit(solution)/shard_map/ppermute | solution.py:508
  7.1 0.8 %first_spectra.2 = (f32[16,32,128]{2,1,0:T(8,128)S(1)}, f32[16,32,128]{2,1,0:T(8,128)S(1)}, f32[8,128]{1,0:T(8,128)S(1)}, bf16[256,256]{1,0:T(8,128)(2,1)S(1)}, ...) custom-call(bf16[16,32,128]{2,1,0:T(8,128)(2,1)S(1)} %collective-permute-done.tile_ref, s32[1,8]{1,0:T(1,128)} %shift_x_hbm.1, ...), custom_call_target="tpu_custom_call" | custom-call | flops 2000000000 | bytes 2000000 | tf_op jit(solution)/shard_map/first_spectra/pallas_call | solution.py:533
  7.9 0.0 collective-permute-done.3.near_own_ref
  7.9 1.3 %collective-permute-start.8 = (bf16[16,32,128]{2,1,0:T(8,128)(2,1)S(1)}, bf16[16,32,128]{2,1,0:T(8,128)(2,1)S(1)}, u32[]{:S(2)}, u32[]{:S(2)}) collective-permute-start(bf16[16,32,128]{2,1,0:T(8,128)(2,1)S(1)} %collective-permute-done.3.near_own_ref), channel_id=1, source_target_pairs={{0,1},{1,0},{2,3},{3,2},{4,5},{5,4},{6,7},{7,6},{8,9},{9,8},{10,11... | collective-permute-start | bytes 393224 | tf_op jit(solution)/shard_map/ppermute | solution.py:508
  9.2 0.5 %collective-permute-start.1 = (s32[2,8]{1,0:T(2,128)S(1)}, s32[2,8]{1,0:T(2,128)S(1)}, u32[]{:S(2)}, u32[]{:S(2)}) collective-permute-start(s32[2,8]{1,0:T(2,128)S(1)} %get-tuple-element.21), channel_id=1, source_target_pairs={{0,1},{1,0},{2,3},{3,2},{4,5},{5,4},{6,7},{7,6},{8,9},{9,8},{10,11... | collective-permute-start | bytes 200 | tf_op jit(solution)/shard_map/ppermute | solution.py:508
  9.7 1.2 %collective-permute-done.5.far_own_ref = bf16[16,32,128]{2,1,0:T(8,128)(2,1)S(1)} collective-permute-done((bf16[16,32,128]{2,1,0:T(8,128)(2,1)}, bf16[16,32,128]{2,1,0:T(8,128)(2,1)S(1)}, u32[]{:S(2)}, u32[]{:S(2)}) %collective-permute-start.5) | collective-permute-done | bytes 131104 | tf_op jit(solution)/shard_map/ppermute | solution.py:508
  11.0 0.0 collective-permute-start.10
  11.0 1.4 %collective-permute-done.7.far_mate_ref = bf16[16,32,128]{2,1,0:T(8,128)(2,1)S(1)} collective-permute-done((bf16[16,32,128]{2,1,0:T(8,128)(2,1)S(1)}, bf16[16,32,128]{2,1,0:T(8,128)(2,1)S(1)}, u32[]{:S(2)}, u32[]{:S(2)}) %collective-permute-start.7) | collective-permute-done | bytes 131104 | tf_op jit(solution)/shard_map/ppermute | solution.py:508
  12.4 0.0 collective-permute-done.4.near_mate_ref
  12.4 0.0 collective-permute-start.9
  12.4 0.0 copy-start
  12.4 0.0 copy-start.1
  12.4 0.0 copy-start.2
  12.4 0.0 copy-start.3
  12.4 0.0 copy-start.4
  12.4 1.5 %first_spectra.3 = (f32[32,32,128]{2,1,0:T(8,128)S(1)}, f32[32,32,128]{2,1,0:T(8,128)S(1)}, f32[32,128]{1,0:T(8,128)S(1)}, f32[8,128]{1,0:T(8,128)S(1)}) custom-call(bf16[16,32,128]{2,1,0:T(8,128)(2,1)S(1)} %collective-permute-done.6.next_ref, bf16[16,32,128]{2,1,0:T(8,128)(2,1)S(1)} %copy-done.5, bf16[256,256]{1,0:T(8,128)(2,1)S(1)} %get-tuple-element.28.y_ref, ...), custom_call_target="tpu_custom_call" | custom-call | flops 2000000000 | bytes 2000000 | tf_op jit(solution)/shard_map/first_spectra/pallas_call | solution.py:533
  14.0 0.0 collective-permute-done.1.shifts_ref
  14.0 0.0 collective-permute-done.8.mate_near_own_ref
  14.0 0.0 collective-permute-done.10.mate_far_own_ref
  14.0 3.1 %second_maps.1.made_ref = f32[256,128]{1,0:T(8,128)S(1)} custom-call(s32[2,8]{1,0:T(2,128)S(1)} %collective-permute-done.1.shifts_ref, bf16[16,32,128]{2,1,0:T(8,128)(2,1)S(1)} %copy-done.2, bf16[16,32,128]{2,1,0:T(8,128)(2,1)S(1)} %collective-permute-done.2.mate_ref, bf16[16,32,128]{2,1,0:T(8,128)(2,1)S(1)} %collective-permute-done.3.near_own_ref, ...), custom_call_target="tpu_custom_call" | custom-call | tf_op jit(solution)/shard_map/second_maps/pallas_call | solution.py:572
  17.2 2.9 %collective-permute-start.11 = (f32[256,128]{1,0:T(8,128)S(1)}, f32[256,128]{1,0:T(8,128)S(1)}, u32[]{:S(2)}, u32[]{:S(2)}) collective-permute-start(f32[256,128]{1,0:T(8,128)S(1)} %second_maps.1.made_ref), channel_id=1, source_target_pairs={{0,2},{2,4},{4,6},{6,8},{8,10},{10,12},{12,14},{14,15},{3,1},{5,3}... | collective-permute-start | bytes 393224 | tf_op jit(solution)/shard_map/ppermute | solution.py:508
  20.1 0.0 collective-permute-start.12
  20.1 3.9 %collective-permute-done.11.other_ref = f32[256,128]{1,0:T(8,128)S(1)} collective-permute-done((f32[256,128]{1,0:T(8,128)S(1)}, f32[256,128]{1,0:T(8,128)S(1)}, u32[]{:S(2)}, u32[]{:S(2)}) %collective-permute-start.11) | collective-permute-done | bytes 131104 | tf_op jit(solution)/shard_map/ppermute | solution.py:508
  24.0 0.8 %product.1 = f32[256,128]{1,0:T(8,128)} custom-call(f32[256,128]{1,0:T(8,128)S(1)} %second_maps.1.made_ref, f32[256,128]{1,0:T(8,128)S(1)} %collective-permute-done.11.other_ref, f32[256,128]{1,0:T(8,128)S(1)} %collective-permute-done.12.own_ref), custom_call_target="tpu_custom_call" | custom-call | tf_op jit(solution)/shard_map/product/pallas_call | solution.py:603
  (10 shorter events, 0.0 us)
Async XLA Ops:
  0.0 12.4 %copy-start.5 = (bf16[16,32,128]{2,1,0:T(8,128)(2,1)S(1)}, bf16[16,32,128]{2,1,0:T(8,128)(2,1)}, u32[]{:S(2)}) copy-start(bf16[16,32,128]{2,1,0:T(8,128)(2,1)} %own_ref.2) | copy-start | bytes 393220
  0.0 4.5 %collective-permute-start.2 = (bf16[16,32,128]{2,1,0:T(8,128)(2,1)}, bf16[16,32,128]{2,1,0:T(8,128)(2,1)S(1)}, u32[]{:S(2)}, u32[]{:S(2)}) collective-permute-start(bf16[16,32,128]{2,1,0:T(8,128)(2,1)} %own_ref.3), channel_id=1, source_target_pairs={{0,1},{1,0},{2,3},{3,2},{4,5},{5,4},{6,7},{7,6},{8,9},{9,8},{10,11... | collective-permute-start | bytes 393224 | tf_op jit(solution)/shard_map/ppermute | solution.py:508
  0.5 5.4 %collective-permute-start = (bf16[16,32,128]{2,1,0:T(8,128)(2,1)}, bf16[16,32,128]{2,1,0:T(8,128)(2,1)S(1)}, u32[]{:S(2)}, u32[]{:S(2)}) collective-permute-start(bf16[16,32,128]{2,1,0:T(8,128)(2,1)} %own_ref.2), channel_id=1, source_target_pairs={{0,1},{1,0},{2,3},{3,2},{4,5},{5,4},{6,7},{7,6},{8,9},{9,8},{10,11... | collective-permute-start | bytes 393224 | tf_op jit(solution)/shard_map/ppermute | solution.py:508
  0.5 7.4 %collective-permute-start.3 = (bf16[16,32,128]{2,1,0:T(8,128)(2,1)}, bf16[16,32,128]{2,1,0:T(8,128)(2,1)S(1)}, u32[]{:S(2)}, u32[]{:S(2)}) collective-permute-start(bf16[16,32,128]{2,1,0:T(8,128)(2,1)} %own_ref.3), channel_id=1, source_target_pairs={{2,0},{4,2},{6,4},{8,6},{10,8},{12,10},{14,12},{15,14},{1,3},{3,5}... | collective-permute-start | bytes 393224 | tf_op jit(solution)/shard_map/ppermute | solution.py:508
  1.0 8.3 %collective-permute-start.6 = (bf16[16,32,128]{2,1,0:T(8,128)(2,1)}, bf16[16,32,128]{2,1,0:T(8,128)(2,1)S(1)}, u32[]{:S(2)}, u32[]{:S(2)}) collective-permute-start(bf16[16,32,128]{2,1,0:T(8,128)(2,1)} %own_ref.2), channel_id=1, source_target_pairs={{2,0},{4,2},{6,4},{8,6},{10,8},{12,10},{14,12},{15,14},{1,3},{3,5}... | collective-permute-start | bytes 393224 | tf_op jit(solution)/shard_map/ppermute | solution.py:508
  3.3 7.7 %collective-permute-start.5 = (bf16[16,32,128]{2,1,0:T(8,128)(2,1)}, bf16[16,32,128]{2,1,0:T(8,128)(2,1)S(1)}, u32[]{:S(2)}, u32[]{:S(2)}) collective-permute-start(bf16[16,32,128]{2,1,0:T(8,128)(2,1)} %own_ref.3), channel_id=1, source_target_pairs={{4,0},{6,2},{8,4},{10,6},{12,8},{14,10},{15,14},{13,12},{1,5},{3,7... | collective-permute-start | bytes 393224 | tf_op jit(solution)/shard_map/ppermute | solution.py:508
  4.5 7.8 %collective-permute-start.7 = (bf16[16,32,128]{2,1,0:T(8,128)(2,1)S(1)}, bf16[16,32,128]{2,1,0:T(8,128)(2,1)S(1)}, u32[]{:S(2)}, u32[]{:S(2)}) collective-permute-start(bf16[16,32,128]{2,1,0:T(8,128)(2,1)S(1)} %collective-permute-done.2.mate_ref), channel_id=1, source_target_pairs={{4,0},{6,2},{8,4},{10,6},{12,8},{14,10},{15,14},{13,12},{1,5},{3,7... | collective-permute-start | bytes 393224 | tf_op jit(solution)/shard_map/ppermute | solution.py:508
  5.8 6.6 %collective-permute-start.4 = (bf16[16,32,128]{2,1,0:T(8,128)(2,1)S(1)}, bf16[16,32,128]{2,1,0:T(8,128)(2,1)S(1)}, u32[]{:S(2)}, u32[]{:S(2)}) collective-permute-start(bf16[16,32,128]{2,1,0:T(8,128)(2,1)S(1)} %collective-permute-done.2.mate_ref), channel_id=1, source_target_pairs={{2,0},{4,2},{6,4},{8,6},{10,8},{12,10},{14,12},{15,14},{1,3},{3,5}... | collective-permute-start | bytes 393224 | tf_op jit(solution)/shard_map/ppermute | solution.py:508
  7.9 6.0 %collective-permute-start.8 = (bf16[16,32,128]{2,1,0:T(8,128)(2,1)S(1)}, bf16[16,32,128]{2,1,0:T(8,128)(2,1)S(1)}, u32[]{:S(2)}, u32[]{:S(2)}) collective-permute-start(bf16[16,32,128]{2,1,0:T(8,128)(2,1)S(1)} %collective-permute-done.3.near_own_ref), channel_id=1, source_target_pairs={{0,1},{1,0},{2,3},{3,2},{4,5},{5,4},{6,7},{7,6},{8,9},{9,8},{10,11... | collective-permute-start | bytes 393224 | tf_op jit(solution)/shard_map/ppermute | solution.py:508
  9.2 4.7 %collective-permute-start.1 = (s32[2,8]{1,0:T(2,128)S(1)}, s32[2,8]{1,0:T(2,128)S(1)}, u32[]{:S(2)}, u32[]{:S(2)}) collective-permute-start(s32[2,8]{1,0:T(2,128)S(1)} %get-tuple-element.21), channel_id=1, source_target_pairs={{0,1},{1,0},{2,3},{3,2},{4,5},{5,4},{6,7},{7,6},{8,9},{9,8},{10,11... | collective-permute-start | bytes 200 | tf_op jit(solution)/shard_map/ppermute | solution.py:508
  11.0 3.0 %collective-permute-start.10 = (bf16[16,32,128]{2,1,0:T(8,128)(2,1)S(1)}, bf16[16,32,128]{2,1,0:T(8,128)(2,1)S(1)}, u32[]{:S(2)}, u32[]{:S(2)}) collective-permute-start(bf16[16,32,128]{2,1,0:T(8,128)(2,1)S(1)} %collective-permute-done.5.far_own_ref), channel_id=1, source_target_pairs={{0,1},{1,0},{2,3},{3,2},{4,5},{5,4},{6,7},{7,6},{8,9},{9,8},{10,11... | collective-permute-start | bytes 393224 | tf_op jit(solution)/shard_map/ppermute | solution.py:508
  12.4 1.6 %collective-permute-start.9 = (bf16[16,32,128]{2,1,0:T(8,128)(2,1)S(1)}, bf16[16,32,128]{2,1,0:T(8,128)(2,1)S(1)}, u32[]{:S(2)}, u32[]{:S(2)}) collective-permute-start(bf16[16,32,128]{2,1,0:T(8,128)(2,1)S(1)} %collective-permute-done.4.near_mate_ref), channel_id=1, source_target_pairs={{0,1},{1,0},{2,3},{3,2},{4,5},{5,4},{6,7},{7,6},{8,9},{9,8},{10,11... | collective-permute-start | bytes 393224 | tf_op jit(solution)/shard_map/ppermute | solution.py:508
  12.4 1.6 %copy-start = (bf16[128,768]{1,0:T(8,128)(2,1)S(1)}, bf16[128,768]{1,0:T(8,128)(2,1)}, u32[]{:S(2)}) copy-start(bf16[128,768]{1,0:T(8,128)(2,1)} %constant.10.clone.z_inverse_ref) | copy-start | bytes 589828
  12.4 1.6 %copy-start.1 = (bf16[768,128]{1,0:T(8,128)(2,1)S(1)}, bf16[768,128]{1,0:T(8,128)(2,1)}, u32[]{:S(2)}) copy-start(bf16[768,128]{1,0:T(8,128)(2,1)} %constant.11.clone.y_inverse_ref) | copy-start | bytes 589828
  12.4 1.6 %copy-start.2 = (bf16[16,32,128]{2,1,0:T(8,128)(2,1)S(1)}, bf16[16,32,128]{2,1,0:T(8,128)(2,1)}, u32[]{:S(2)}) copy-start(bf16[16,32,128]{2,1,0:T(8,128)(2,1)} %own_ref.3) | copy-start | bytes 393220
  12.4 1.6 %copy-start.3 = (bf16[256,256]{1,0:T(8,128)(2,1)S(1)}, bf16[256,256]{1,0:T(8,128)(2,1)}, u32[]{:S(2)}) copy-start(bf16[256,256]{1,0:T(8,128)(2,1)} %constant.8.clone.y_high_ref) | copy-start | bytes 393220
  12.4 1.6 %copy-start.4 = (bf16[256,256]{1,0:T(8,128)(2,1)S(1)}, bf16[256,256]{1,0:T(8,128)(2,1)}, u32[]{:S(2)}) copy-start(bf16[256,256]{1,0:T(8,128)(2,1)} %constant.9.clone.y_low_ref) | copy-start | bytes 393220
  17.2 6.8 %collective-permute-start.11 = (f32[256,128]{1,0:T(8,128)S(1)}, f32[256,128]{1,0:T(8,128)S(1)}, u32[]{:S(2)}, u32[]{:S(2)}) collective-permute-start(f32[256,128]{1,0:T(8,128)S(1)} %second_maps.1.made_ref), channel_id=1, source_target_pairs={{0,2},{2,4},{4,6},{6,8},{8,10},{10,12},{12,14},{14,15},{3,1},{5,3}... | collective-permute-start | bytes 393224 | tf_op jit(solution)/shard_map/ppermute | solution.py:508
  20.1 3.9 %collective-permute-start.12 = (f32[256,128]{1,0:T(8,128)S(1)}, f32[256,128]{1,0:T(8,128)S(1)}, u32[]{:S(2)}, u32[]{:S(2)}) collective-permute-start(f32[256,128]{1,0:T(8,128)S(1)} %second_maps.1.made_ref), channel_id=1, source_target_pairs={{0,1},{1,0},{2,3},{3,2},{4,5},{5,4},{6,7},{7,6},{8,9},{9,8},{10,11... | collective-permute-start | bytes 393224 | tf_op jit(solution)/shard_map/ppermute | solution.py:508

commit v6 on v5

--- a/solution.py
+++ b/solution.py
@@ -184,11 +184,12 @@
 def variance(energy, mean_energy):
     total = jnp.sum(energy, 0, keepdims=True) + mean_energy
     total = jnp.broadcast_to(total, (8, LANES))
-    group_row = lax.broadcasted_iota(jnp.int32, (LANES, LANES), 0) // HALF
-    group_col = lax.broadcasted_iota(jnp.int32, (LANES, LANES), 1) // HALF
-    same = (group_row == group_col).astype(F32)
-    summed = jnp.dot(total, same, precision=lax.Precision.HIGHEST, preferred_element_type=F32)
-    return summed * (1.0 / (ZS * WIN * WIN * ZS * WIN))
+    place = lax.broadcasted_iota(jnp.int32, (8, LANES), 1) % HALF
+    for step in (1, 2, 4, 8):
+        ahead = pltpu.roll(total, step, 1)
+        around = pltpu.roll(total, LANES - HALF + step, 1)
+        total = total + jnp.where(place >= step, ahead, around)
+    return total * (1.0 / (ZS * WIN * WIN * ZS * WIN))
 
 
 def first_tables(y_ref, z_ref):
@@ -373,7 +374,7 @@
 
     lane = lax.broadcasted_iota(jnp.int32, (1, LANES), 1)
 
-    def eight_x(start, energy):
+    def eight_x(start):
         packs = []
         for half in range(2):
             total = None
@@ -389,15 +390,17 @@
                 else:
                     total = jnp.where(inside, turned, total)
             packs.append(total.astype(BF16))
-        windows = jnp.concatenate(packs, 1)
+        return jnp.concatenate(packs, 1)
+
+    energy = jnp.zeros((8, LANES), F32)
+    for base in range(0, WIN, 16):
+        windows = jnp.concatenate([eight_x(base + x) for x in range(0, 16, 8)], 0)
         values = dot(windows, y_high_ref[...]) + dot(windows, y_low_ref[...])
-        return energy + z_stage(
-            values[: 4 * ZS], values[4 * ZS :], z_ref, real_ref, imag_ref, start
-        )
-
-    energy = jnp.zeros((8, LANES), F32)
-    for start in range(0, WIN, 8):
-        energy = eight_x(start, energy)
+        for x in range(0, 16, 8):
+            part = values[x * ZS : (x + 8) * ZS]
+            energy = energy + z_stage(
+                part[: 4 * ZS], part[4 * ZS :], z_ref, real_ref, imag_ref, base + x
+            )
     def eight_slots(where_z):
         def value(x):
             return real_ref[x, where_z], imag_ref[x, where_z]

time: 24.9 us -> 24.6 us (0.988)
  Pallas kernels: 6.26 us -> 5.95 us
where the time goes in v6:
time: 24.6 us; the launch traced here: 24.4 us
  starting transfers between devices  11.8 us (48%)
  waiting for transfers between devices  6.57 us (27%)
  Pallas kernels  5.95 us (24%)
    ppermute x13, starting transfers between devices, send(): return lax.ppermute(value, 'gx', pairs)  11.8 us
    ppermute x13, waiting for transfers between devices, send(): return lax.ppermute(value, 'gx', pairs)  6.57 us
    pallas_call x1, Pallas kernels, local(): pl.pallas_call(second_kernel, out_shape=jax.ShapeDtypeStruct((SR * SR, LA...  3 us
    pallas_call x2, Pallas kernels, first_spectra(): pl.pallas_call(kernel, out_shape=outs, in_specs=specs, out_specs=(VMEM,)...  2.16 us
    pallas_call x1, Pallas kernels, local(): pl.pallas_call(product_kernel, out_shape=jax.ShapeDtypeStruct((SR * SR, L...  0.79 us
  transfers between devices with their start and end apart: 13, of which 3 were waited for; matrix products, arithmetic and copies ran while one was open for 0% of the time, Pallas kernels for 9%

profile of v6, /device:TPU:0, one launch (start us, length us, event | category | flops | bytes accessed | tf_op | source)
XLA Modules:
  0.0 24.4 jit_solution(634097633448239979)
XLA Ops:
  0.0 0.5 %collective-permute-start.2 = (bf16[16,32,128]{2,1,0:T(8,128)(2,1)}, bf16[16,32,128]{2,1,0:T(8,128)(2,1)S(1)}, u32[]{:S(2)}, u32[]{:S(2)}) collective-permute-start(bf16[16,32,128]{2,1,0:T(8,128)(2,1)} %own_ref.3), channel_id=1, source_target_pairs={{0,1},{1,0},{2,3},{3,2},{4,5},{5,4},{6,7},{7,6},{8,9},{9,8},{10,11... | collective-permute-start | bytes 393224 | tf_op jit(solution)/shard_map/ppermute | solution.py:511
  0.5 0.1 collective-permute-start
  0.5 0.4 %collective-permute-start.3 = (bf16[16,32,128]{2,1,0:T(8,128)(2,1)}, bf16[16,32,128]{2,1,0:T(8,128)(2,1)S(1)}, u32[]{:S(2)}, u32[]{:S(2)}) collective-permute-start(bf16[16,32,128]{2,1,0:T(8,128)(2,1)} %own_ref.3), channel_id=1, source_target_pairs={{2,0},{4,2},{6,4},{8,6},{10,8},{12,10},{14,12},{15,14},{1,3},{3,5}... | collective-permute-start | bytes 393224 | tf_op jit(solution)/shard_map/ppermute | solution.py:511
  1.0 2.3 %collective-permute-start.6 = (bf16[16,32,128]{2,1,0:T(8,128)(2,1)}, bf16[16,32,128]{2,1,0:T(8,128)(2,1)S(1)}, u32[]{:S(2)}, u32[]{:S(2)}) collective-permute-start(bf16[16,32,128]{2,1,0:T(8,128)(2,1)} %own_ref.2), channel_id=1, source_target_pairs={{2,0},{4,2},{6,4},{8,6},{10,8},{12,10},{14,12},{15,14},{1,3},{3,5}... | collective-permute-start | bytes 393224 | tf_op jit(solution)/shard_map/ppermute | solution.py:511
  3.3 1.2 %collective-permute-start.5 = (bf16[16,32,128]{2,1,0:T(8,128)(2,1)}, bf16[16,32,128]{2,1,0:T(8,128)(2,1)S(1)}, u32[]{:S(2)}, u32[]{:S(2)}) collective-permute-start(bf16[16,32,128]{2,1,0:T(8,128)(2,1)} %own_ref.3), channel_id=1, source_target_pairs={{4,0},{6,2},{8,4},{10,6},{12,8},{14,10},{15,14},{13,12},{1,5},{3,7... | collective-permute-start | bytes 393224 | tf_op jit(solution)/shard_map/ppermute | solution.py:511
  4.5 0.0 collective-permute-done.2.mate_ref
  4.5 1.3 %collective-permute-start.7 = (bf16[16,32,128]{2,1,0:T(8,128)(2,1)S(1)}, bf16[16,32,128]{2,1,0:T(8,128)(2,1)S(1)}, u32[]{:S(2)}, u32[]{:S(2)}) collective-permute-start(bf16[16,32,128]{2,1,0:T(8,128)(2,1)S(1)} %collective-permute-done.2.mate_ref), channel_id=1, source_target_pairs={{4,0},{6,2},{8,4},{10,6},{12,8},{14,10},{15,14},{13,12},{1,5},{3,7... | collective-permute-start | bytes 393224 | tf_op jit(solution)/shard_map/ppermute | solution.py:511
  5.8 0.0 collective-permute-done.tile_ref
  5.8 1.3 %collective-permute-start.4 = (bf16[16,32,128]{2,1,0:T(8,128)(2,1)S(1)}, bf16[16,32,128]{2,1,0:T(8,128)(2,1)S(1)}, u32[]{:S(2)}, u32[]{:S(2)}) collective-permute-start(bf16[16,32,128]{2,1,0:T(8,128)(2,1)S(1)} %collective-permute-done.2.mate_ref), channel_id=1, source_target_pairs={{2,0},{4,2},{6,4},{8,6},{10,8},{12,10},{14,12},{15,14},{1,3},{3,5}... | collective-permute-start | bytes 393224 | tf_op jit(solution)/shard_map/ppermute | solution.py:511
  7.1 0.8 %first_spectra.2 = (f32[16,32,128]{2,1,0:T(8,128)S(1)}, f32[16,32,128]{2,1,0:T(8,128)S(1)}, f32[8,128]{1,0:T(8,128)S(1)}, bf16[256,256]{1,0:T(8,128)(2,1)S(1)}, ...) custom-call(bf16[16,32,128]{2,1,0:T(8,128)(2,1)S(1)} %collective-permute-done.tile_ref, s32[1,8]{1,0:T(1,128)} %shift_x_hbm.1, ...), custom_call_target="tpu_custom_call" | custom-call | flops 2000000000 | bytes 2000000 | tf_op jit(solution)/shard_map/first_spectra/pallas_call | solution.py:536
  7.9 0.0 collective-permute-done.3.near_own_ref
  7.9 1.3 %collective-permute-start.8 = (bf16[16,32,128]{2,1,0:T(8,128)(2,1)S(1)}, bf16[16,32,128]{2,1,0:T(8,128)(2,1)S(1)}, u32[]{:S(2)}, u32[]{:S(2)}) collective-permute-start(bf16[16,32,128]{2,1,0:T(8,128)(2,1)S(1)} %collective-permute-done.3.near_own_ref), channel_id=1, source_target_pairs={{0,1},{1,0},{2,3},{3,2},{4,5},{5,4},{6,7},{7,6},{8,9},{9,8},{10,11... | collective-permute-start | bytes 393224 | tf_op jit(solution)/shard_map/ppermute | solution.py:511
  9.2 0.5 %collective-permute-start.1 = (s32[2,8]{1,0:T(2,128)S(1)}, s32[2,8]{1,0:T(2,128)S(1)}, u32[]{:S(2)}, u32[]{:S(2)}) collective-permute-start(s32[2,8]{1,0:T(2,128)S(1)} %get-tuple-element.21), channel_id=1, source_target_pairs={{0,1},{1,0},{2,3},{3,2},{4,5},{5,4},{6,7},{7,6},{8,9},{9,8},{10,11... | collective-permute-start | bytes 200 | tf_op jit(solution)/shard_map/ppermute | solution.py:511
  9.7 1.2 %collective-permute-done.5.far_own_ref = bf16[16,32,128]{2,1,0:T(8,128)(2,1)S(1)} collective-permute-done((bf16[16,32,128]{2,1,0:T(8,128)(2,1)}, bf16[16,32,128]{2,1,0:T(8,128)(2,1)S(1)}, u32[]{:S(2)}, u32[]{:S(2)}) %collective-permute-start.5) | collective-permute-done | bytes 131104 | tf_op jit(solution)/shard_map/ppermute | solution.py:511
  11.0 0.0 collective-permute-start.10
  11.0 1.4 %collective-permute-done.7.far_mate_ref = bf16[16,32,128]{2,1,0:T(8,128)(2,1)S(1)} collective-permute-done((bf16[16,32,128]{2,1,0:T(8,128)(2,1)S(1)}, bf16[16,32,128]{2,1,0:T(8,128)(2,1)S(1)}, u32[]{:S(2)}, u32[]{:S(2)}) %collective-permute-start.7) | collective-permute-done | bytes 131104 | tf_op jit(solution)/shard_map/ppermute | solution.py:511
  12.4 0.0 collective-permute-done.4.near_mate_ref
  12.4 0.0 collective-permute-start.9
  12.4 0.0 copy-start
  12.4 0.0 copy-start.1
  12.4 0.0 copy-start.2
  12.4 0.0 copy-start.3
  12.4 0.0 copy-start.4
  12.4 1.4 %first_spectra.3 = (f32[32,32,128]{2,1,0:T(8,128)S(1)}, f32[32,32,128]{2,1,0:T(8,128)S(1)}, f32[32,128]{1,0:T(8,128)S(1)}, f32[8,128]{1,0:T(8,128)S(1)}) custom-call(bf16[16,32,128]{2,1,0:T(8,128)(2,1)S(1)} %collective-permute-done.6.next_ref, bf16[16,32,128]{2,1,0:T(8,128)(2,1)S(1)} %copy-done.5, bf16[256,256]{1,0:T(8,128)(2,1)S(1)} %get-tuple-element.28.y_ref, ...), custom_call_target="tpu_custom_call" | custom-call | flops 2000000000 | bytes 2000000 | tf_op jit(solution)/shard_map/first_spectra/pallas_call | solution.py:536
  13.8 0.0 collective-permute-done.1.shifts_ref
  13.8 0.0 collective-permute-done.8.mate_near_own_ref
  13.8 0.0 collective-permute-done.10.mate_far_own_ref
  13.9 3.0 %second_maps.1.made_ref = f32[256,128]{1,0:T(8,128)S(1)} custom-call(s32[2,8]{1,0:T(2,128)S(1)} %collective-permute-done.1.shifts_ref, bf16[16,32,128]{2,1,0:T(8,128)(2,1)S(1)} %copy-done.2, bf16[16,32,128]{2,1,0:T(8,128)(2,1)S(1)} %collective-permute-done.2.mate_ref, bf16[16,32,128]{2,1,0:T(8,128)(2,1)S(1)} %collective-permute-done.3.near_own_ref, ...), custom_call_target="tpu_custom_call" | custom-call | tf_op jit(solution)/shard_map/second_maps/pallas_call | solution.py:575
  16.9 2.9 %collective-permute-start.11 = (f32[256,128]{1,0:T(8,128)S(1)}, f32[256,128]{1,0:T(8,128)S(1)}, u32[]{:S(2)}, u32[]{:S(2)}) collective-permute-start(f32[256,128]{1,0:T(8,128)S(1)} %second_maps.1.made_ref), channel_id=1, source_target_pairs={{0,2},{2,4},{4,6},{6,8},{8,10},{10,12},{12,14},{14,15},{3,1},{5,3}... | collective-permute-start | bytes 393224 | tf_op jit(solution)/shard_map/ppermute | solution.py:511
  19.8 3.9 %collective-permute-done.11.other_ref = f32[256,128]{1,0:T(8,128)S(1)} collective-permute-done((f32[256,128]{1,0:T(8,128)S(1)}, f32[256,128]{1,0:T(8,128)S(1)}, u32[]{:S(2)}, u32[]{:S(2)}) %collective-permute-start.11) | collective-permute-done | bytes 131104 | tf_op jit(solution)/shard_map/ppermute | solution.py:511
  23.6 0.0 collective-permute-done.12.own_ref
  23.7 0.8 %product.1 = f32[256,128]{1,0:T(8,128)} custom-call(f32[256,128]{1,0:T(8,128)S(1)} %second_maps.1.made_ref, f32[256,128]{1,0:T(8,128)S(1)} %collective-permute-done.11.other_ref, f32[256,128]{1,0:T(8,128)S(1)} %collective-permute-done.12.own_ref), custom_call_target="tpu_custom_call" | custom-call | tf_op jit(solution)/shard_map/product/pallas_call | solution.py:606
  (10 shorter events, 0.0 us)
Async XLA Ops:
  0.0 12.4 %copy-start.5 = (bf16[16,32,128]{2,1,0:T(8,128)(2,1)S(1)}, bf16[16,32,128]{2,1,0:T(8,128)(2,1)}, u32[]{:S(2)}) copy-start(bf16[16,32,128]{2,1,0:T(8,128)(2,1)} %own_ref.2) | copy-start | bytes 393220
  0.0 4.5 %collective-permute-start.2 = (bf16[16,32,128]{2,1,0:T(8,128)(2,1)}, bf16[16,32,128]{2,1,0:T(8,128)(2,1)S(1)}, u32[]{:S(2)}, u32[]{:S(2)}) collective-permute-start(bf16[16,32,128]{2,1,0:T(8,128)(2,1)} %own_ref.3), channel_id=1, source_target_pairs={{0,1},{1,0},{2,3},{3,2},{4,5},{5,4},{6,7},{7,6},{8,9},{9,8},{10,11... | collective-permute-start | bytes 393224 | tf_op jit(solution)/shard_map/ppermute | solution.py:511
  0.5 5.4 %collective-permute-start = (bf16[16,32,128]{2,1,0:T(8,128)(2,1)}, bf16[16,32,128]{2,1,0:T(8,128)(2,1)S(1)}, u32[]{:S(2)}, u32[]{:S(2)}) collective-permute-start(bf16[16,32,128]{2,1,0:T(8,128)(2,1)} %own_ref.2), channel_id=1, source_target_pairs={{0,1},{1,0},{2,3},{3,2},{4,5},{5,4},{6,7},{7,6},{8,9},{9,8},{10,11... | collective-permute-start | bytes 393224 | tf_op jit(solution)/shard_map/ppermute | solution.py:511
  0.5 7.4 %collective-permute-start.3 = (bf16[16,32,128]{2,1,0:T(8,128)(2,1)}, bf16[16,32,128]{2,1,0:T(8,128)(2,1)S(1)}, u32[]{:S(2)}, u32[]{:S(2)}) collective-permute-start(bf16[16,32,128]{2,1,0:T(8,128)(2,1)} %own_ref.3), channel_id=1, source_target_pairs={{2,0},{4,2},{6,4},{8,6},{10,8},{12,10},{14,12},{15,14},{1,3},{3,5}... | collective-permute-start | bytes 393224 | tf_op jit(solution)/shard_map/ppermute | solution.py:511
  1.0 8.3 %collective-permute-start.6 = (bf16[16,32,128]{2,1,0:T(8,128)(2,1)}, bf16[16,32,128]{2,1,0:T(8,128)(2,1)S(1)}, u32[]{:S(2)}, u32[]{:S(2)}) collective-permute-start(bf16[16,32,128]{2,1,0:T(8,128)(2,1)} %own_ref.2), channel_id=1, source_target_pairs={{2,0},{4,2},{6,4},{8,6},{10,8},{12,10},{14,12},{15,14},{1,3},{3,5}... | collective-permute-start | bytes 393224 | tf_op jit(solution)/shard_map/ppermute | solution.py:511
  3.3 7.7 %collective-permute-start.5 = (bf16[16,32,128]{2,1,0:T(8,128)(2,1)}, bf16[16,32,128]{2,1,0:T(8,128)(2,1)S(1)}, u32[]{:S(2)}, u32[]{:S(2)}) collective-permute-start(bf16[16,32,128]{2,1,0:T(8,128)(2,1)} %own_ref.3), channel_id=1, source_target_pairs={{4,0},{6,2},{8,4},{10,6},{12,8},{14,10},{15,14},{13,12},{1,5},{3,7... | collective-permute-start | bytes 393224 | tf_op jit(solution)/shard_map/ppermute | solution.py:511
  4.5 7.8 %collective-permute-start.7 = (bf16[16,32,128]{2,1,0:T(8,128)(2,1)S(1)}, bf16[16,32,128]{2,1,0:T(8,128)(2,1)S(1)}, u32[]{:S(2)}, u32[]{:S(2)}) collective-permute-start(bf16[16,32,128]{2,1,0:T(8,128)(2,1)S(1)} %collective-permute-done.2.mate_ref), channel_id=1, source_target_pairs={{4,0},{6,2},{8,4},{10,6},{12,8},{14,10},{15,14},{13,12},{1,5},{3,7... | collective-permute-start | bytes 393224 | tf_op jit(solution)/shard_map/ppermute | solution.py:511
  5.8 6.6 %collective-permute-start.4 = (bf16[16,32,128]{2,1,0:T(8,128)(2,1)S(1)}, bf16[16,32,128]{2,1,0:T(8,128)(2,1)S(1)}, u32[]{:S(2)}, u32[]{:S(2)}) collective-permute-start(bf16[16,32,128]{2,1,0:T(8,128)(2,1)S(1)} %collective-permute-done.2.mate_ref), channel_id=1, source_target_pairs={{2,0},{4,2},{6,4},{8,6},{10,8},{12,10},{14,12},{15,14},{1,3},{3,5}... | collective-permute-start | bytes 393224 | tf_op jit(solution)/shard_map/ppermute | solution.py:511
  7.9 5.9 %collective-permute-start.8 = (bf16[16,32,128]{2,1,0:T(8,128)(2,1)S(1)}, bf16[16,32,128]{2,1,0:T(8,128)(2,1)S(1)}, u32[]{:S(2)}, u32[]{:S(2)}) collective-permute-start(bf16[16,32,128]{2,1,0:T(8,128)(2,1)S(1)} %collective-permute-done.3.near_own_ref), channel_id=1, source_target_pairs={{0,1},{1,0},{2,3},{3,2},{4,5},{5,4},{6,7},{7,6},{8,9},{9,8},{10,11... | collective-permute-start | bytes 393224 | tf_op jit(solution)/shard_map/ppermute | solution.py:511
  9.2 4.6 %collective-permute-start.1 = (s32[2,8]{1,0:T(2,128)S(1)}, s32[2,8]{1,0:T(2,128)S(1)}, u32[]{:S(2)}, u32[]{:S(2)}) collective-permute-start(s32[2,8]{1,0:T(2,128)S(1)} %get-tuple-element.21), channel_id=1, source_target_pairs={{0,1},{1,0},{2,3},{3,2},{4,5},{5,4},{6,7},{7,6},{8,9},{9,8},{10,11... | collective-permute-start | bytes 200 | tf_op jit(solution)/shard_map/ppermute | solution.py:511
  11.0 2.9 %collective-permute-start.10 = (bf16[16,32,128]{2,1,0:T(8,128)(2,1)S(1)}, bf16[16,32,128]{2,1,0:T(8,128)(2,1)S(1)}, u32[]{:S(2)}, u32[]{:S(2)}) collective-permute-start(bf16[16,32,128]{2,1,0:T(8,128)(2,1)S(1)} %collective-permute-done.5.far_own_ref), channel_id=1, source_target_pairs={{0,1},{1,0},{2,3},{3,2},{4,5},{5,4},{6,7},{7,6},{8,9},{9,8},{10,11... | collective-permute-start | bytes 393224 | tf_op jit(solution)/shard_map/ppermute | solution.py:511
  12.4 1.5 %collective-permute-start.9 = (bf16[16,32,128]{2,1,0:T(8,128)(2,1)S(1)}, bf16[16,32,128]{2,1,0:T(8,128)(2,1)S(1)}, u32[]{:S(2)}, u32[]{:S(2)}) collective-permute-start(bf16[16,32,128]{2,1,0:T(8,128)(2,1)S(1)} %collective-permute-done.4.near_mate_ref), channel_id=1, source_target_pairs={{0,1},{1,0},{2,3},{3,2},{4,5},{5,4},{6,7},{7,6},{8,9},{9,8},{10,11... | collective-permute-start | bytes 393224 | tf_op jit(solution)/shard_map/ppermute | solution.py:511
  12.4 1.5 %copy-start = (bf16[128,768]{1,0:T(8,128)(2,1)S(1)}, bf16[128,768]{1,0:T(8,128)(2,1)}, u32[]{:S(2)}) copy-start(bf16[128,768]{1,0:T(8,128)(2,1)} %constant.10.clone.z_inverse_ref) | copy-start | bytes 589828
  12.4 1.5 %copy-start.1 = (bf16[768,128]{1,0:T(8,128)(2,1)S(1)}, bf16[768,128]{1,0:T(8,128)(2,1)}, u32[]{:S(2)}) copy-start(bf16[768,128]{1,0:T(8,128)(2,1)} %constant.11.clone.y_inverse_ref) | copy-start | bytes 589828
  12.4 1.5 %copy-start.2 = (bf16[16,32,128]{2,1,0:T(8,128)(2,1)S(1)}, bf16[16,32,128]{2,1,0:T(8,128)(2,1)}, u32[]{:S(2)}) copy-start(bf16[16,32,128]{2,1,0:T(8,128)(2,1)} %own_ref.3) | copy-start | bytes 393220
  12.4 1.4 %copy-start.3 = (bf16[256,256]{1,0:T(8,128)(2,1)S(1)}, bf16[256,256]{1,0:T(8,128)(2,1)}, u32[]{:S(2)}) copy-start(bf16[256,256]{1,0:T(8,128)(2,1)} %constant.8.clone.y_high_ref) | copy-start | bytes 393220
  12.4 1.4 %copy-start.4 = (bf16[256,256]{1,0:T(8,128)(2,1)S(1)}, bf16[256,256]{1,0:T(8,128)(2,1)}, u32[]{:S(2)}) copy-start(bf16[256,256]{1,0:T(8,128)(2,1)} %constant.9.clone.y_low_ref) | copy-start | bytes 393220
  16.9 6.8 %collective-permute-start.11 = (f32[256,128]{1,0:T(8,128)S(1)}, f32[256,128]{1,0:T(8,128)S(1)}, u32[]{:S(2)}, u32[]{:S(2)}) collective-permute-start(f32[256,128]{1,0:T(8,128)S(1)} %second_maps.1.made_ref), channel_id=1, source_target_pairs={{0,2},{2,4},{4,6},{6,8},{8,10},{10,12},{12,14},{14,15},{3,1},{5,3}... | collective-permute-start | bytes 393224 | tf_op jit(solution)/shard_map/ppermute | solution.py:511
  19.8 3.9 %collective-permute-start.12 = (f32[256,128]{1,0:T(8,128)S(1)}, f32[256,128]{1,0:T(8,128)S(1)}, u32[]{:S(2)}, u32[]{:S(2)}) collective-permute-start(f32[256,128]{1,0:T(8,128)S(1)} %second_maps.1.made_ref), channel_id=1, source_target_pairs={{0,1},{1,0},{2,3},{3,2},{4,5},{5,4},{6,7},{7,6},{8,9},{9,8},{10,11... | collective-permute-start | bytes 393224 | tf_op jit(solution)/shard_map/ppermute | solution.py:511
